TPU v7x, 128 devices: a whole 4x4x4 slice. The times are simulated.
128 devices in a mesh: ha: 8 (over z, core), wa: 16 (over y, x).
Axes of the slice: x: 4, y: 4, z: 4, core: 2. Of those that a mesh axis runs over, the one named last changes fastest.
Arguments:
- features: bfloat16 [256, 512, 256], P('ha', 'wa'), may hold values from -6 to 6
- counts: int32 [8, 16], P('ha', 'wa'), may hold values from 0 to 16, as said below
- owner_perm: int32 [8, 16], P('ha'), may hold values from 0 to 15, each once within a row
- corners: int32 [2048, 2], P(('ha', 'wa')), may hold values from 0 to 31, as said below
- offsets: int32 [2048, 28], P(('ha', 'wa')), may hold values from 0 to 124
- kernels: bfloat16 [2, 3, 3, 256, 256], replicated, may hold values from -0.125 to 0.125
- cotangent: bfloat16 [1024, 14, 14, 256], P(('ha', 'wa')), may hold values from -6 to 6
Outputs:
- grad_features: float32 [256, 512, 256], P('ha', 'wa')
- grad_kernels: float32 [2, 3, 3, 256, 256], replicated
Inputs may be any that keep to these rules, and one draw needn't show every extreme that they name: In each row of tiles the counts add up to 8 times the number of devices along wa, and one tile of every row has exactly 16. `corners`: the first column is below 32, the second below 32.
All inputs are finite; a program needn't handle non-finite values.
Results may differ from a plain program's by a relative error of at most 0.012.
Values may be sent and summed in bfloat16 or wider, within the bound.
No kernel may reach another device: no remote copies, remote signals or barrier semaphores. Data moves between devices by JAX's collectives and lax.ppermute only.
A program may use at most 192 MiB of HBM per device.

v0:
```python
import jax
import jax.numpy as jnp
from jax import lax
from jax.sharding import PartitionSpec as P

SIDE = 14
BOX = 32
LAYERS = 2


highest = lax.Precision.HIGHEST


def shifted(value, axis, steps):
    count = lax.axis_size(axis)
    first, last = (max(0, -steps), min(count, count - steps))
    return lax.ppermute(value, axis, [(source, source + steps) for source in range(first, last)])


def in_order(pieces, dim):
    lengths = list(pieces.shape[1:])
    lengths[dim] *= pieces.shape[0]
    return jnp.moveaxis(pieces, 0, dim).reshape(lengths)


def from_everyone(x, axis):
    peers = lax.axis_size(axis)
    return lax.all_to_all(jnp.broadcast_to(x[None], (peers, *x.shape)), axis, 0, 0, tiled=True)


def collect(x, axis, dim):
    return in_order(from_everyone(x, axis), dim)


def placed_weights(sample_offsets, corner_at, span):
    places = 4 * (jnp.arange(span, dtype=jnp.int32)[None, :] - corner_at[:, None])
    spread = jnp.abs(places[:, None, :] - sample_offsets[:, :, None]).astype(jnp.float32)
    return jnp.maximum(0.0, 1.0 - spread / 4.0)


def gelu_exact(values):
    return jax.nn.gelu(values, approximate=False)


def patches_of(inputs):
    amount, channels = (inputs.shape[0], inputs.shape[3])
    padded = jnp.pad(inputs, ((0, 0), (1, 1), (1, 1), (0, 0)))
    pieces = []
    for row_step in range(3):
        for col_step in range(3):
            pieces.append(padded[:, row_step : row_step + SIDE, col_step : col_step + SIDE, :])
    return jnp.concatenate(pieces, axis=3).reshape(amount * SIDE * SIDE, 9 * channels)


def fold_back(columns, amount):
    channels = columns.shape[1] // 9
    pieces = columns.reshape(amount, SIDE, SIDE, 9, channels)
    totals = jnp.zeros((amount, SIDE + 2, SIDE + 2, channels), jnp.float32)
    for row_step in range(3):
        for col_step in range(3):
            totals = totals.at[:, row_step : row_step + SIDE, col_step : col_step + SIDE, :].add(
                pieces[:, :, :, 3 * row_step + col_step, :]
            )
    return totals[:, 1 : SIDE + 1, 1 : SIDE + 1, :]


def mask_head(samples, upstream, kernels):
    amount, channels = (samples.shape[0], samples.shape[3])
    inputs = samples
    saved = []
    for layer_step in range(LAYERS):
        matrix = kernels[layer_step].reshape(9 * channels, channels)
        columns = patches_of(inputs)
        before = jnp.dot(columns, matrix, preferred_element_type=jnp.float32)
        saved.append((columns, before, matrix))
        if layer_step + 1 < LAYERS:
            inputs = gelu_exact(before).astype(jnp.bfloat16).reshape(amount, SIDE, SIDE, channels)
    upward = upstream.reshape(amount * SIDE * SIDE, channels)
    kernel_grads = [None] * LAYERS
    for layer_step in reversed(range(LAYERS)):
        columns, before, matrix = saved[layer_step]
        ignored, gelu_slope = jax.vjp(gelu_exact, before)
        inner_grad = gelu_slope(upward.astype(jnp.float32))[0].astype(jnp.bfloat16)
        layer_grad = lax.dot_general(
            columns, inner_grad, (((0,), (0,)), ((), ())), preferred_element_type=jnp.float32
        )
        kernel_grads[layer_step] = layer_grad
        spread = lax.dot_general(
            inner_grad, matrix, (((1,), (1,)), ((), ())), preferred_element_type=jnp.float32
        )
        upward = (
            fold_back(spread, amount).astype(jnp.bfloat16).reshape(amount * SIDE * SIDE, channels)
        )
    return (upward.reshape(amount, SIDE * SIDE * channels), jnp.stack(kernel_grads))


def local(features, counts, owner_perm, corners, offsets, kernels, cotangent):
    tile_rows, tile_cols, channels = features.shape
    slot_total = corners.shape[0]
    owned = cotangent.shape[0]
    width_count = lax.axis_size("wa")
    pairs = slot_total // width_count
    col_index = lax.axis_index("wa")
    right_edge = shifted(features, "wa", -1)
    widened = jnp.concatenate([features, right_edge], axis=1)
    lower_edge = shifted(widened, "ha", -1)
    extended = jnp.concatenate([widened, lower_edge], axis=0)
    row_place = placed_weights(offsets[:, :SIDE], corners[:, 0], tile_rows + BOX)
    col_place = placed_weights(offsets[:, SIDE:], corners[:, 1], tile_cols + BOX)
    partial_rows = jnp.einsum(
        "siy,yxc->sixc",
        row_place.astype(jnp.bfloat16),
        extended,
        preferred_element_type=jnp.float32,
    )
    samples = jnp.einsum("sjx,sixc->sijc", col_place, partial_rows, precision=highest).astype(
        jnp.bfloat16
    )
    row_counts = collect(counts, "wa", 1)[0]
    starts = jnp.cumsum(row_counts) - row_counts
    device_ids = jnp.arange(width_count, dtype=jnp.int32)
    here_start = jnp.sum(jnp.where(device_ids == col_index, starts, 0))
    perm_row = owner_perm[0]
    slot_ids = jnp.arange(slot_total, dtype=jnp.int32)
    stream = here_start + slot_ids
    owner_of = jnp.sum(
        jnp.where((stream % width_count)[:, None] == device_ids[None, :], perm_row[None, :], 0),
        axis=1,
    )
    buffer_ids = jnp.arange(width_count * pairs, dtype=jnp.int32)
    live_slot = slot_ids < counts[0, 0]
    home_route = (
        ((owner_of * pairs + slot_ids // width_count)[:, None] == buffer_ids[None, :])
        & live_slot[:, None]
    ).astype(jnp.bfloat16)
    position = jnp.sum(jnp.where(perm_row == col_index, device_ids, 0))
    sender_match = (buffer_ids // pairs)[:, None] == device_ids[None, :]
    sender_start = jnp.sum(jnp.where(sender_match, starts[None, :], 0), axis=1)
    sender_count = jnp.sum(jnp.where(sender_match, row_counts[None, :], 0), axis=1)
    arrival = (
        sender_start + (position - sender_start) % width_count + buffer_ids % pairs * width_count
    )
    arrived = arrival < sender_start + sender_count
    own_route = (
        ((arrival // width_count)[None, :] == jnp.arange(owned, dtype=jnp.int32)[:, None])
        & arrived[None, :]
    ).astype(jnp.bfloat16)
    outgoing = jnp.dot(
        own_route.T,
        cotangent.reshape(owned, SIDE * SIDE * channels),
        preferred_element_type=jnp.float32,
    ).astype(jnp.bfloat16)
    incoming = lax.all_to_all(outgoing, "wa", split_axis=0, concat_axis=0, tiled=True)
    upstream = jnp.dot(home_route, incoming, preferred_element_type=jnp.float32).astype(
        jnp.bfloat16
    )
    home_grads, kernel_grads = mask_head(samples, upstream, kernels)
    kernel_grads = lax.psum(kernel_grads, ("ha", "wa"))
    sample_grads = home_grads.reshape(slot_total, SIDE, SIDE, channels)
    spread_cols = jnp.einsum(
        "sjx,sijc->sixc", col_place, sample_grads.astype(jnp.float32), precision=highest
    )
    grads_ext = jnp.einsum("siy,sixc->yxc", row_place, spread_cols, precision=highest)
    from_above = shifted(grads_ext[tile_rows:], "ha", 1)
    grads_ext = grads_ext.at[:BOX].add(from_above)
    from_left = shifted(grads_ext[:tile_rows, tile_cols:], "wa", 1)
    grad_tile = grads_ext[:tile_rows, :tile_cols].at[:, :BOX].add(from_left)
    return (grad_tile, kernel_grads.reshape(LAYERS, 3, 3, channels, channels))


def solution(mesh):
    in_specs = (
        P("ha", "wa", None),
        P("ha", "wa"),
        P("ha", None),
        P(("ha", "wa"), None),
        P(("ha", "wa"), None),
        P(),
        P(("ha", "wa"), None, None, None),
    )
    out_specs = (P("ha", "wa", None), P())
    return jax.shard_map(local, mesh=mesh, in_specs=in_specs, out_specs=out_specs, check_vma=False)
```

profile of v0, /device:TPU:1, one launch (start us, length us, event | category | flops | bytes accessed | tf_op | source)
XLA Modules:
  0.0 518.8 jit_solution(18232458355770207478)
XLA Ops:
  8.5 7.6 %all-to-all-start = ((s32[16,1,1]{2,1,0:T(1,128)}), s32[16,1,1]{2,1,0:T(1,128)S(1)}, u32[]{:S(2)}, u32[]{:S(2)}) async-start(s32[16,1,1]{2,1,0:T(1,128)} %broadcast_in_dim.57), calls=%async_computation | async-start | bytes 16384 | tf_op jit(solution)/shard_map/all_to_all | solution.py:28
  33.3 8.1 %all-to-all-start.1 = ((bf16[16,2,25088]{2,1,0:T(2,128)(2,1)}), bf16[16,2,25088]{2,1,0:T(2,128)(2,1)S(1)}, u32[]{:S(2)}, u32[]{:S(2)}) async-start(bf16[16,2,25088]{2,1,0:T(2,128)(2,1)} %reshape.1006), calls=%async_computation.1 | async-start | bytes 3211264 | tf_op jit(solution)/shard_map/all_to_all | solution.py:153
  51.3 11.3 %all-to-all-done.1 = bf16[16,2,25088]{2,1,0:T(2,128)(2,1)S(1)} async-done(((bf16[16,2,25088]{2,1,0:T(2,128)(2,1)}), bf16[16,2,25088]{2,1,0:T(2,128)(2,1)S(1)}, u32[]{:S(2)}, u32[]{:S(2)}) %all-to-all-start.1) | async-done | bytes 1605664 | tf_op jit(solution)/shard_map/all_to_all | solution.py:153
  62.6 6.1 %reshape.1007 = bf16[16,1,50176]{2,1,0:T(2,128)(2,1)} reshape(bf16[16,2,25088]{2,1,0:T(2,128)(2,1)S(1)} %all-to-all-done.1) | data formatting | bytes 3211264
  80.1 19.9 %convert_bitcast_fusion = bf16[16,14,14,256]{3,2,1,0:T(8,128)(2,1)S(1)} fusion(f32[16,14,64,256]{3,0,2,1:T(8,128)S(1)} %fusion.57, f32[16,14,64,1]{2,0,1,3:T(8,128)S(1)} %maximum_bitcast_fusion.2), kind=kOutput, calls=%fused_computation.117 | convolution fusion | flops 617365504 | bytes 16343040 | tf_op jit(solution)/shard_map/sjx,sixc->sijc/dot_general | solution.py:116
  117.3 21.6 %reshape.966 = bf16[3136,2304]{1,0:T(8,128)(2,1)} reshape(bf16[16,14,14,2304]{3,2,1,0:T(8,128)(2,1)} %slice_dynamic-update-slice_fusion) | data formatting | bytes 28901376 | tf_op jit(solution)/shard_map/reshape | solution.py:52
  139.0 15.4 %multiply_convert_fusion = (bf16[3136,256]{1,0:T(8,128)(2,1)S(1)}, f32[3136,256]{1,0:T(8,128)}, f32[3136,256]{1,0:T(8,128)}) fusion(bf16[3136,2304]{1,0:T(8,128)(2,1)} %reshape.966, bf16[2304,256]{1,0:T(8,128)(2,1)} %bitcast.188), kind=kOutput, calls=%fused_computation.85 | convolution fusion | flops 3751559168 | bytes 23658496 | tf_op jit(solution)/shard_map/dot_general | solution.py:74
  157.0 12.1 %pad_slice_fusion = (bf16[16,14,14,256]{3,2,1,0:T(8,128)(2,1)}, bf16[16,14,14,256]{3,2,1,0:T(8,128)(2,1)}, bf16[16,14,14,256]{3,2,1,0:T(8,128)(2,1)}, bf16[16,14...) fusion(bf16[16,14,14,256]{3,2,1,0:T(8,128)(2,1)} %reshape.967), kind=kLoop, calls=%fused_computation.126 | loop fusion | bytes 14450688 | tf_op jit(solution)/shard_map/slice | solution.py:51
  205.1 11.2 %fusion.11 = bf16[3136,256]{1,0:T(8,128)(2,1)S(1)} fusion(f32[3136,256]{1,0:T(8,128)S(1)} %copy-done.16, bf16[3136,2304]{1,0:T(8,128)(2,1)S(1)} %constant_dynamic-update-slice_fusion.3, bf16[2304,256]{1,0:T(8,128)(2,1)S(1)} %bitcast.191), kind=kOutput, calls=%fused_computation.21 | convolution fusion | flops 3757178880 | bytes 20447232 | tf_op jit(solution)/shard_map/dot_general | solution.py:74
  217.5 6.0 %convolution_bitcast_fusion.1 = f32[1,2304,256]{2,1,0:T(8,128)} fusion(bf16[3136,2304]{1,0:T(8,128)(2,1)S(1)} %constant_dynamic-update-slice_fusion.3, bf16[3136,256]{1,0:T(8,128)(2,1)S(1)} %fusion.11), kind=kOutput, calls=%fused_computation.14 | convolution fusion | flops 3699376128 | bytes 18415616 | tf_op jit(solution)/shard_map/dot_general | solution.py:84
  225.9 13.4 %fusion.68 = f32[16,14,14,9,256]{4,0,3,2,1:T(8,128)} fusion(bf16[9,256,256,1,1]{2,1,0,4,3:T(8,128)(2,1)} %bitcast.190, bf16[16,14,14,256,1]{3,2,1,0,4:T(8,128)(2,1)S(1)} %bitcast.187), kind=kOutput, calls=%fused_computation.123 | convolution fusion | flops 3699376128 | bytes 31686656 | tf_op jit(solution)/shard_map/dot_general | solution.py:88
  242.2 5.3 %fusion.41 = f32[16,16,16,256]{3,0,2,1:T(8,128)S(1)} fusion(f32[16,16,16,256]{3,0,2,1:T(8,128)S(1)} %scatter-add.60, s32[]{:T(128)} %bitcast.20, s32[]{:T(128)} %bitcast.21, f32[16,14,14,9,256]{4,0,3,2,1:T(8,128)} %fusion.68), kind=kLoop, calls=%fused_computation.70 | loop fusion | flops 802816 | bytes 9633800 | tf_op jit(solution)/shard_map/scatter-add | solution.py:61
  247.6 5.6 %fusion.12 = f32[16,16,16,256]{3,0,2,1:T(8,128)S(1)} fusion(f32[16,16,16,256]{3,0,2,1:T(8,128)S(1)} %fusion.41, s32[]{:T(128)} %bitcast.23, s32[]{:T(128)} %bitcast.24, f32[16,14,14,9,256]{4,0,3,2,1:T(8,128)} %fusion.68, pred[]{:T(512)} %and_reduce_fusion), kind=kLoop, calls=%fused_computation.22 | loop fusion | flops 1605632 | bytes 9633801 | tf_op jit(solution)/shard_map/scatter-add | solution.py:61
  267.0 6.3 %add_convert_fusion = bf16[3136,256]{1,0:T(8,128)(2,1)} fusion(f32[3136,256]{1,0:T(8,128)} %reshape.993, f32[3136,256]{1,0:T(8,128)} %get-tuple-element.261, f32[3136,256]{1,0:T(8,128)} %get-tuple-element.286), kind=kLoop, calls=%fused_computation.72 | loop fusion | flops 11239424 | bytes 11239424 | tf_op jit(solution)/shard_map/convert_element_type | solution.py:83
  275.7 13.2 %fusion.66 = f32[16,14,14,9,256]{4,0,2,1,3:T(8,128)} fusion(bf16[9,256,256,1,1]{2,1,4,3,0:T(8,128)(2,1)} %bitcast.189, bf16[16,14,14,256]{3,2,1,0:T(8,128)(2,1)S(1)} %dot_general.53), kind=kOutput, calls=%fused_computation.121 | convolution fusion | flops 3699376128 | bytes 31686656 | tf_op jit(solution)/shard_map/dot_general | solution.py:88
  291.8 5.3 %fusion.27 = f32[16,16,16,256]{3,0,2,1:T(8,128)S(1)} fusion(f32[16,16,16,256]{3,0,2,1:T(8,128)S(1)} %scatter-add.75, s32[]{:T(128)} %bitcast.20, s32[]{:T(128)} %bitcast.21, f32[16,14,14,9,256]{4,0,2,1,3:T(8,128)} %fusion.66), kind=kLoop, calls=%fused_computation.46 | loop fusion | flops 802816 | bytes 9633800 | tf_op jit(solution)/shard_map/scatter-add | solution.py:61
  297.1 5.6 %fusion.13 = f32[16,16,16,256]{3,0,2,1:T(8,128)S(1)} fusion(f32[16,16,16,256]{3,0,2,1:T(8,128)S(1)} %fusion.27, s32[]{:T(128)} %bitcast.23, s32[]{:T(128)} %bitcast.24, f32[16,14,14,9,256]{4,0,2,1,3:T(8,128)} %fusion.66, pred[]{:T(512)} %and_reduce_fusion), kind=kLoop, calls=%fused_computation.23 | loop fusion | flops 1605632 | bytes 9633801 | tf_op jit(solution)/shard_map/scatter-add | solution.py:61
  308.6 6.2 %convolution_bitcast_fusion = f32[16,14,64,256]{3,2,1,0:T(8,128)S(1)} fusion(bf16[16,14,14,256]{3,0,2,1:T(8,128)(2,1)S(1)} %slice.993, f32[16,14,64,1]{2,0,1,3:T(8,128)S(1)} %copy-done.18), kind=kOutput, calls=%fused_computation.8 | convolution fusion | flops 616562688 | bytes 16343040 | tf_op jit(solution)/shard_map/sjx,sijc->sixc/dot_general | solution.py:160
  314.9 17.7 %fusion.54 = f32[64,64,256]{2,0,1:T(8,128)S(1)} fusion(f32[16,14,64,256]{3,2,1,0:T(8,128)S(1)} %convolution_bitcast_fusion, s32[16,14]{0,1:T(8,128)S(1)} %copy-done.24, s32[16,64]{1,0:T(8,128)S(1)} %copy-done.22), kind=kOutput, calls=%fused_computation.102 | convolution fusion | flops 2818658304 | bytes 18879360 | tf_op jit(solution)/shard_map/siy,sixc->yxc/dot_general | solution.py:163
  334.1 7.7 %collective-permute-start.2 = (f32[32,64,256]{2,0,1:T(8,128)}, f32[32,64,256]{2,0,1:T(8,128)S(1)}, u32[]{:S(2)}, u32[]{:S(2)}) collective-permute-start(f32[32,64,256]{2,0,1:T(8,128)} %slice.876), channel_id=1, source_target_pairs={{0,16},{16,32},{32,48},{48,64},{64,80},{80,96},{96,112},{1,17},{17... | collective-permute-start | bytes 6291464 | tf_op jit(solution)/shard_map/ppermute | solution.py:17
  341.7 7.6 %convolution_bitcast_fusion.2 = f32[1,2304,256]{2,1,0:T(8,128)S(1)} fusion(bf16[3136,2304]{1,0:T(8,128)(2,1)} %reshape.966, bf16[3136,256]{1,0:T(8,128)(2,1)S(1)} %copy-done.14), kind=kOutput, calls=%fused_computation.15 | convolution fusion | flops 3699376128 | bytes 18415616 | tf_op jit(solution)/shard_map/dot_general | solution.py:84
  351.9 16.2 %collective-permute-done.2 = f32[32,64,256]{2,0,1:T(8,128)S(1)} collective-permute-done((f32[32,64,256]{2,0,1:T(8,128)}, f32[32,64,256]{2,0,1:T(8,128)S(1)}, u32[]{:S(2)}, u32[]{:S(2)}) %collective-permute-start.2) | collective-permute-done | bytes 2097184 | tf_op jit(solution)/shard_map/ppermute | solution.py:17
  371.6 14.8 %collective-permute-done.3 = f32[32,32,256]{2,0,1:T(8,128)S(1)} collective-permute-done((f32[32,32,256]{2,0,1:T(8,128)S(1)}, f32[32,32,256]{2,0,1:T(8,128)S(1)}, u32[]{:S(2)}, u32[]{:S(2)}) %collective-permute-start.3) | collective-permute-done | bytes 1048608 | tf_op jit(solution)/shard_map/ppermute | solution.py:17
  388.2 118.4 %all-reduce.6.cloned.1.call-done = f32[2,3,3,256,256]{4,3,2,1,0:T(8,128)} async-done(((f32[2,3,3,256,256]{4,3,2,1,0:T(8,128)}), f32[2,3,3,256,256]{4,3,2,1,0:T(8,128)}) %all-reduce.6.cloned.1.call-update) | async-done | bytes 4718608 | tf_op jit(solution)/shard_map/psum | solution.py:158
  (150 shorter events, 140.5 us)
Async XLA Ops:
  7.2 19.2 %copy-start = (bf16[8,14,14,256]{3,0,2,1:T(8,128)(2,1)S(1)}, bf16[8,14,14,256]{3,0,2,1:T(8,128)(2,1)}, u32[]{:S(2)}) copy-start(bf16[8,14,14,256]{3,0,2,1:T(8,128)(2,1)} %param.55) | copy-start | bytes 2408452
  8.5 15.9 %all-to-all-start = ((s32[16,1,1]{2,1,0:T(1,128)}), s32[16,1,1]{2,1,0:T(1,128)S(1)}, u32[]{:S(2)}, u32[]{:S(2)}) async-start(s32[16,1,1]{2,1,0:T(1,128)} %broadcast_in_dim.57), calls=%async_computation | async-start | bytes 16384 | tf_op jit(solution)/shard_map/all_to_all | solution.py:28
  18.2 27.2 %collective-permute-start = (bf16[32,32,256]{2,0,1:T(8,128)(2,1)}, bf16[32,32,256]{2,0,1:T(8,128)(2,1)}, u32[]{:S(2)}, u32[]{:S(2)}) collective-permute-start(bf16[32,32,256]{2,0,1:T(8,128)(2,1)} %get-tuple-element.276), channel_id=1, source_target_pairs={{1,0},{2,1},{3,2},{4,3},{5,4},{6,5},{7,6},{8,7},{9,8},{10,9},{11,1... | collective-permute-start | bytes 1572872 | tf_op jit(solution)/shard_map/ppermute | solution.py:17
  33.3 29.2 %all-to-all-start.1 = ((bf16[16,2,25088]{2,1,0:T(2,128)(2,1)}), bf16[16,2,25088]{2,1,0:T(2,128)(2,1)S(1)}, u32[]{:S(2)}, u32[]{:S(2)}) async-start(bf16[16,2,25088]{2,1,0:T(2,128)(2,1)} %reshape.1006), calls=%async_computation.1 | async-start | bytes 3211264 | tf_op jit(solution)/shard_map/all_to_all | solution.py:153
  41.4 9.7 %copy-start.25 = (s32[1,16]{1,0:T(1,128)S(1)}, s32[1,16]{1,0:T(1,128)}, u32[]{:S(2)}) copy-start(s32[1,16]{1,0:T(1,128)} %param.51) | copy-start | bytes 196
  41.4 465.2 %all-reduce.6.cloned.1.call-start = ((), (), s32[]{:S(2)}) async-start(), calls=%async_computation.2 | async-start | bytes 9437184 | tf_op jit(solution)/shard_map/psum | solution.py:158
  42.2 34.5 %copy-start.21 = (s32[16,64]{1,0:T(8,128)}, s32[16,64]{1,0:T(8,128)S(1)}, u32[]{:S(2)}) copy-start(s32[16,64]{1,0:T(8,128)S(1)} %get-tuple-element.290) | copy-start | bytes 12292
  46.6 30.2 %collective-permute-start.1 = (bf16[32,64,256]{2,0,1:T(8,128)(2,1)S(1)}, bf16[32,64,256]{2,0,1:T(8,128)(2,1)}, u32[]{:S(2)}, u32[]{:S(2)}) collective-permute-start(bf16[32,64,256]{2,0,1:T(8,128)(2,1)S(1)} %constant_dynamic-update-slice_fusion), channel_id=1, source_target_pairs={{16,0},{32,16},{48,32},{64,48},{80,64},{96,80},{112,96},{17,1},{33... | collective-permute-start | bytes 3145736 | tf_op jit(solution)/shard_map/ppermute | solution.py:17
  50.4 26.3 %copy-start.23 = (s32[16,14]{0,1:T(8,128)}, s32[16,14]{0,1:T(8,128)S(1)}, u32[]{:S(2)}) copy-start(s32[16,14]{0,1:T(8,128)S(1)} %copy.123) | copy-start | bytes 2692
  50.6 29.6 %copy-start.17 = (f32[16,14,64,1]{2,0,1,3:T(8,128)}, f32[16,14,64,1]{2,0,1,3:T(8,128)S(1)}, u32[]{:S(2)}) copy-start(f32[16,14,64,1]{2,0,1,3:T(8,128)S(1)} %maximum_bitcast_fusion.2) | copy-start | bytes 172036
  196.3 1.9 copy-start.13
  196.3 2.4 copy-start.12
  198.2 1.5 copy-start.11
  202.8 2.4 copy-start.16
  239.3 13.9 %copy-start.2 = (f32[16,14,14,9,256]{4,0,3,2,1:T(8,128)S(1)}, f32[16,14,14,9,256]{4,0,3,2,1:T(8,128)}, u32[]{:S(2)}) copy-start(f32[16,14,14,9,256]{4,0,3,2,1:T(8,128)} %fusion.68) | copy-start | bytes 86704128
  288.9 13.8 %copy-start.3 = (f32[16,14,14,9,256]{4,0,2,1,3:T(8,128)S(1)}, f32[16,14,14,9,256]{4,0,2,1,3:T(8,128)}, u32[]{:S(2)}) copy-start(f32[16,14,14,9,256]{4,0,2,1,3:T(8,128)} %fusion.66) | copy-start | bytes 86704128
  308.6 6.2 %copy-start.22 = (s32[16,64]{1,0:T(8,128)S(1)}, s32[16,64]{1,0:T(8,128)}, u32[]{:S(2)}) copy-start(s32[16,64]{1,0:T(8,128)} %copy-done.21) | copy-start | bytes 12292
  308.6 6.2 %copy-start.24 = (s32[16,14]{0,1:T(8,128)S(1)}, s32[16,14]{0,1:T(8,128)}, u32[]{:S(2)}) copy-start(s32[16,14]{0,1:T(8,128)} %copy-done.23) | copy-start | bytes 2692
  332.6 16.7 %copy-start.4 = (f32[64,64,256]{2,0,1:T(8,128)}, f32[64,64,256]{2,0,1:T(8,128)S(1)}, u32[]{:S(2)}) copy-start(f32[64,64,256]{2,0,1:T(8,128)S(1)} %fusion.54) | copy-start | bytes 12582916
  332.6 9.1 %copy-start.14 = (bf16[3136,256]{1,0:T(8,128)(2,1)S(1)}, bf16[3136,256]{1,0:T(8,128)(2,1)}, u32[]{:S(2)}) copy-start(bf16[3136,256]{1,0:T(8,128)(2,1)} %add_convert_fusion) | copy-start | bytes 4816900
  334.1 15.3 %copy-start.19 = (f32[1,2304,256]{2,1,0:T(8,128)S(1)}, f32[1,2304,256]{2,1,0:T(8,128)}, u32[]{:S(2)}) copy-start(f32[1,2304,256]{2,1,0:T(8,128)} %convolution_bitcast_fusion.1) | copy-start | bytes 7077892
  334.1 34.0 %collective-permute-start.2 = (f32[32,64,256]{2,0,1:T(8,128)}, f32[32,64,256]{2,0,1:T(8,128)S(1)}, u32[]{:S(2)}, u32[]{:S(2)}) collective-permute-start(f32[32,64,256]{2,0,1:T(8,128)} %slice.876), channel_id=1, source_target_pairs={{0,16},{16,32},{32,48},{48,64},{64,80},{80,96},{96,112},{1,17},{17... | collective-permute-start | bytes 6291464 | tf_op jit(solution)/shard_map/ppermute | solution.py:17
  370.2 16.2 %collective-permute-start.3 = (f32[32,32,256]{2,0,1:T(8,128)S(1)}, f32[32,32,256]{2,0,1:T(8,128)S(1)}, u32[]{:S(2)}, u32[]{:S(2)}) collective-permute-start(f32[32,32,256]{2,0,1:T(8,128)S(1)} %slice.878), channel_id=1, source_target_pairs={{0,1},{1,2},{2,3},{3,4},{4,5},{5,6},{6,7},{7,8},{8,9},{9,10},{10,1... | collective-permute-start | bytes 3145736 | tf_op jit(solution)/shard_map/ppermute | solution.py:17
  386.6 125.0 %copy-start.1 = (bf16[8,14,14,256]{3,0,2,1:T(8,128)(2,1)S(1)}, bf16[8,14,14,256]{3,0,2,1:T(8,128)(2,1)}, u32[]{:S(2)}) copy-start(bf16[8,14,14,256]{3,0,2,1:T(8,128)(2,1)} %param.55) | copy-start | bytes 2408452
  (9 other events, 12.3 us)
Sparse Core Ops, SparseCore 0:
  352.0 154.6 all-reduce.5
where the time goes:
time: 525 us; the launch traced here: 519 us
  waiting for transfers between devices  161 us (31%)
  local copies, waits for them, and re-layouts  143 us (27%)
  matrix products  119 us (23%)
  other arithmetic  51.1 us (10%)
  starting transfers between devices  29.7 us (6%)
  between operations  15.8 us (3%)
    psum x1, waiting for transfers between devices, local(): kernel_grads = lax.psum(kernel_grads, ('ha', 'wa'))  118 us
    unnamed x73, local copies, waits for them, and re-layouts  45.3 us
    scatter-add x16, other arithmetic, fold_back(): totals.at[:, row_step:row_step + SIDE, col_step:col_step + SIDE, :]  31.8 us
    ppermute x4, waiting for transfers between devices, shifted(): lax.ppermute(value, axis, [(source, source + steps) for source in range(f...  31.1 us
    concatenate x10, local copies, waits for them, and re-layouts, patches_of(): jnp.concatenate(pieces, axis=3).reshape(amount * SIDE * SIDE, 9 * channels)  29.2 us
    dot_general x2, matrix products, mask_head(): lax.dot_general(inner_grad, matrix, (((1,), (1,)), ((), ())), preferred_e...  26.6 us
    dot_general x2, matrix products, mask_head(): before = jnp.dot(columns, matrix, preferred_element_type=jnp.float32)  26.6 us
    reshape x1, local copies, waits for them, and re-layouts, patches_of(): jnp.concatenate(pieces, axis=3).reshape(amount * SIDE * SIDE, 9 * channels)  21.6 us
  transfers between devices with their start and end apart: 7, of which 4 were waited for; matrix products, arithmetic and copies ran while one was open for 10% of the time, Pallas kernels for 0%

commit v1 on v0

v1 whole, which is shorter than its diff:
```python
import functools

import jax
import jax.numpy as jnp
from jax import lax
from jax.experimental import pallas as pl
from jax.experimental.pallas import tpu as pltpu
from jax.sharding import PartitionSpec as P

SIDE = 14
PITCH = 16
PIX = SIDE * PITCH
BOX = 32
SPAN = 48
WIN = BOX * SPAN
ROWS = 288
C = 256
BF = jnp.bfloat16
F32 = jnp.float32


def shifted(value, axis, steps):
    count = lax.axis_size(axis)
    first, last = (max(0, -steps), min(count, count - steps))
    return lax.ppermute(value, axis, [(source, source + steps) for source in range(first, last)])


def dot(a, b, dims=(((1,), (0,)), ((), ()))):
    return lax.dot_general(a, b, dims, preferred_element_type=F32)


def inside(rows):
    pixel = lax.broadcasted_iota(jnp.int32, (rows, C), 0)
    return (pixel & (PITCH - 1)) < SIDE


def clear_edges(held, copies):
    for shift in range(3):
        for g in range(copies):
            held[shift, g, 0:16, :] = jnp.zeros((16, C), BF)
            held[shift, g, 16 + PIX : ROWS, :] = jnp.zeros((ROWS - 16 - PIX, C), BF)


def hold(held, g, value):
    held[0, g, 16 : 16 + PIX, :] = pltpu.roll(value, 1, 0).astype(BF)
    held[1, g, 16 : 16 + PIX, :] = value.astype(BF)
    held[2, g, 16 : 16 + PIX, :] = pltpu.roll(value, PIX - 1, 0).astype(BF)


def tent(places, offsets):
    return jnp.maximum(0.0, 1.0 - jnp.abs(places - offsets) * 0.25)


def gelu_parts(v):
    cdf = 0.5 * (1.0 + lax.erf(v * 0.7071067811865476))
    slope = cdf + v * (jnp.exp(v * v * -0.5) * 0.3989422804014327)
    return v * cdf, slope


def route_kernel(index_ref, x_ref, o_ref):
    o_ref[0, :, 0:SIDE, :] = x_ref[0]
    o_ref[0, :, SIDE:PITCH, :] = jnp.zeros((SIDE, PITCH - SIDE, C), BF)


def route(index, cotangent):
    peers = index.shape[0]
    return pl.pallas_call(
        route_kernel,
        name="route",
        out_shape=jax.ShapeDtypeStruct((peers, SIDE, PITCH, C), BF),
        grid_spec=pltpu.PrefetchScalarGridSpec(
            num_scalar_prefetch=1,
            grid=(peers,),
            in_specs=[pl.BlockSpec((1, SIDE, SIDE, C), lambda i, index: (index[i], 0, 0, 0))],
            out_specs=pl.BlockSpec((1, SIDE, PITCH, C), lambda i, index: (i, 0, 0, 0)),
        ),
        cost_estimate=pl.CostEstimate(flops=0, bytes_accessed=4 << 20, transcendentals=0),
    )(index, cotangent)


FG = 2


def forward_kernel(
    corner_ref, tl_ref, tr_ref, bl_ref, br_ref, off_ref, place_ref, k_ref,
    a0_ref, a1_ref, g0_ref, g1_ref, ext, row_w, weight, held,
):
    step = pl.program_id(0)

    @pl.when(step == 0)
    def _():
        clear_edges(held, FG)
        ext[0:BOX, 0:BOX, :] = tl_ref[...]
        ext[0:BOX, BOX : 2 * BOX, :] = tr_ref[...]
        ext[BOX : 2 * BOX, 0:BOX, :] = bl_ref[...]
        ext[BOX : 2 * BOX, BOX : 2 * BOX, :] = br_ref[...]

    keep = inside(PIX)
    for g in range(FG):
        slot = step * FG + g
        top = corner_ref[slot, 0]
        left = pl.multiple_of(corner_ref[slot, 1] // 16 * 16, 16)
        rows = off_ref[g, 0:16, 0:1]
        cols = off_ref[g, 16:32, 0:1]
        row_w[g] = tent(place_ref[0:1, :], rows)
        col_w = tent(place_ref[1:2, :], cols)
        for i in range(SIDE):
            weight[g, i * PITCH : (i + 1) * PITCH, :] = (row_w[g, i : i + 1, :] * col_w).astype(BF)
        window = ext[pl.ds(top, BOX), pl.ds(left, SPAN), :].reshape(WIN, C)
        hold(held, g, dot(weight[g], window))
        a0_ref[:, g * C : (g + 1) * C] = held[1, g, 16 : 16 + C, :].T
    for layer in range(2):
        for g in range(FG):
            pre = jnp.zeros((PIX, C), F32)
            for dy in range(3):
                for dx in range(3):
                    pre += dot(held[dx, g, 16 * dy : 16 * dy + PIX, :], k_ref[layer, dy * 3 + dx])
            value, slope = gelu_parts(pre)
            slope = jnp.where(keep, slope, 0.0).astype(BF)
            if layer == 0:
                g0_ref[g] = slope
                hold(held, g, jnp.where(keep, value, 0.0))
                a1_ref[:, g * C : (g + 1) * C] = held[1, g, 16 : 16 + C, :].T
            else:
                g1_ref[g] = slope


def forward(corners, pieces, off_cols, places, kernels):
    slots = corners.shape[0]
    whole = lambda *shape: pl.BlockSpec(shape, lambda i, *_: (0,) * len(shape))
    return pl.pallas_call(
        forward_kernel,
        name="forward",
        out_shape=[
            jax.ShapeDtypeStruct((C, slots * C), BF),
            jax.ShapeDtypeStruct((C, slots * C), BF),
            jax.ShapeDtypeStruct((slots, PIX, C), BF),
            jax.ShapeDtypeStruct((slots, PIX, C), BF),
        ],
        grid_spec=pltpu.PrefetchScalarGridSpec(
            num_scalar_prefetch=1,
            grid=(slots // FG,),
            in_specs=[whole(BOX, BOX, C)] * 4
            + [
                pl.BlockSpec((FG, 32, 128), lambda i, *_: (i, 0, 0)),
                whole(8, WIN),
                whole(2, 9, C, C),
            ],
            out_specs=[
                pl.BlockSpec((C, FG * C), lambda i, *_: (0, i)),
                pl.BlockSpec((C, FG * C), lambda i, *_: (0, i)),
                pl.BlockSpec((FG, PIX, C), lambda i, *_: (i, 0, 0)),
                pl.BlockSpec((FG, PIX, C), lambda i, *_: (i, 0, 0)),
            ],
            scratch_shapes=[
                pltpu.VMEM((2 * BOX, 2 * BOX, C), BF),
                pltpu.VMEM((FG, 16, WIN), F32),
                pltpu.VMEM((FG, PIX, WIN), BF),
                pltpu.VMEM((3, FG, ROWS, C), BF),
            ],
        ),
        cost_estimate=pl.CostEstimate(
            flops=11_300_000_000, bytes_accessed=12 << 20, transcendentals=4_000_000
        ),
    )(corners, *pieces, off_cols, places, kernels)


BG = 4


def top_grad(meta_ref, slot, in_ref, g1_ref, g):
    source = meta_ref[slot]
    live = slot < meta_ref[16]
    grad = in_ref[source].astype(F32) * g1_ref[g].astype(F32)
    return jnp.where(live, grad, 0.0)


def kernel_grad(step, steps, held, a_ref, acc, o_ref):
    @pl.when(step == 0)
    def _():
        acc[...] = jnp.zeros_like(acc)

    for dy in range(3):
        for dx in range(3):
            grads = held[2 - dx, :, 32 - 16 * dy : 32 - 16 * dy + C, :].reshape(BG * C, C)
            acc[dy * 3 + dx] += dot(a_ref[...], grads)

    @pl.when(step == steps - 1)
    def _():
        o_ref[...] = acc[...].astype(BF)


def last_kernel(meta_ref, in_ref, g1_ref, a_ref, o_ref, held, acc):
    step = pl.program_id(0)

    @pl.when(step == 0)
    def _():
        clear_edges(held, BG)

    for g in range(BG):
        hold(held, g, top_grad(meta_ref, step * BG + g, in_ref, g1_ref, g))
    kernel_grad(step, pl.num_programs(0), held, a_ref, acc, o_ref)


def last_grad(meta, incoming, slope1, acts1):
    slots = slope1.shape[0]
    return pl.pallas_call(
        last_kernel,
        name="last_grad",
        out_shape=jax.ShapeDtypeStruct((9, C, C), BF),
        grid_spec=pltpu.PrefetchScalarGridSpec(
            num_scalar_prefetch=1,
            grid=(slots // BG,),
            in_specs=[
                pl.BlockSpec((16, PIX, C), lambda i, *_: (0, 0, 0)),
                pl.BlockSpec((BG, PIX, C), lambda i, *_: (i, 0, 0)),
                pl.BlockSpec((C, BG * C), lambda i, *_: (0, i)),
            ],
            out_specs=pl.BlockSpec((9, C, C), lambda i, *_: (0, 0, 0)),
            scratch_shapes=[pltpu.VMEM((3, BG, ROWS, C), BF), pltpu.VMEM((9, C, C), F32)],
        ),
        cost_estimate=pl.CostEstimate(
            flops=4_800_000_000, bytes_accessed=8 << 20, transcendentals=0
        ),
    )(meta, incoming, slope1, acts1)


def input_grad(held, g, k_ref):
    total = jnp.zeros((PIX, C), F32)
    for dy in range(3):
        for dx in range(3):
            total += dot(
                held[2 - dx, g, 32 - 16 * dy : 32 - 16 * dy + PIX, :],
                k_ref[dy * 3 + dx],
                (((1,), (1,)), ((), ())),
            )
    return total.astype(BF)


def middle_kernel(
    meta_ref, in_ref, g1_ref, g0_ref, k_ref, a_ref, p_ref, o_ref, upper, held, acc
):
    step = pl.program_id(0)

    @pl.when(step == 0)
    def _():
        clear_edges(upper, BG)
        clear_edges(held, BG)

    for g in range(BG):
        hold(upper, g, top_grad(meta_ref, step * BG + g, in_ref, g1_ref, g))
    for g in range(BG):
        grad = input_grad(upper, g, k_ref).astype(F32) * g0_ref[g].astype(F32)
        p_ref[g] = grad.astype(BF)
        hold(held, g, grad)
    kernel_grad(step, pl.num_programs(0), held, a_ref, acc, o_ref)


def middle_grad(meta, incoming, slope1, slope0, kernel1, acts0):
    slots = slope1.shape[0]
    return pl.pallas_call(
        middle_kernel,
        name="middle_grad",
        out_shape=[
            jax.ShapeDtypeStruct((slots, PIX, C), BF),
            jax.ShapeDtypeStruct((9, C, C), BF),
        ],
        grid_spec=pltpu.PrefetchScalarGridSpec(
            num_scalar_prefetch=1,
            grid=(slots // BG,),
            in_specs=[
                pl.BlockSpec((16, PIX, C), lambda i, *_: (0, 0, 0)),
                pl.BlockSpec((BG, PIX, C), lambda i, *_: (i, 0, 0)),
                pl.BlockSpec((BG, PIX, C), lambda i, *_: (i, 0, 0)),
                pl.BlockSpec((9, C, C), lambda i, *_: (0, 0, 0)),
                pl.BlockSpec((C, BG * C), lambda i, *_: (0, i)),
            ],
            out_specs=[
                pl.BlockSpec((BG, PIX, C), lambda i, *_: (i, 0, 0)),
                pl.BlockSpec((9, C, C), lambda i, *_: (0, 0, 0)),
            ],
            scratch_shapes=[
                pltpu.VMEM((3, BG, ROWS, C), BF),
                pltpu.VMEM((3, BG, ROWS, C), BF),
                pltpu.VMEM((9, C, C), F32),
            ],
        ),
        cost_estimate=pl.CostEstimate(
            flops=9_000_000_000, bytes_accessed=12 << 20, transcendentals=0
        ),
    )(meta, incoming, slope1, slope0, kernel1, acts0)


SG = 2


def spread_kernel(
    corner_ref, p_ref, off_ref, k_ref, tl_ref, tr_ref, bl_ref, br_ref, held, row_w, weight, total
):
    step = pl.program_id(0)

    @pl.when(step == 0)
    def _():
        clear_edges(held, SG)
        total[...] = jnp.zeros_like(total)

    for g in range(SG):
        hold(held, g, p_ref[g].astype(F32))
    row_at = 4.0 * lax.broadcasted_iota(jnp.int32, (BOX, C), 0).astype(F32)
    col_at = 4.0 * lax.broadcasted_iota(jnp.int32, (SPAN, C), 0).astype(F32)
    for g in range(SG):
        row_w[g] = tent(row_at, off_ref[g, 0:1, :])
        col_w = tent(col_at, off_ref[g, 1:2, :])
        for p in range(BOX):
            weight[g, p * SPAN : (p + 1) * SPAN, :] = (row_w[g, p : p + 1, :] * col_w).astype(BF)
    for g in range(SG):
        slot = step * SG + g
        top = corner_ref[slot, 0]
        left = pl.multiple_of(corner_ref[slot, 1] // 16 * 16, 16)
        grad = jnp.concatenate([input_grad(held, g, k_ref), jnp.zeros((C - PIX, C), BF)], axis=0)
        for part in range(4):
            at = part * (BOX // 4)
            spread = dot(weight[g, at * SPAN : (at + BOX // 4) * SPAN, :], grad)
            total[pl.ds(top + at, BOX // 4), pl.ds(left, SPAN), :] += spread.reshape(
                BOX // 4, SPAN, C
            )

    @pl.when(step == pl.num_programs(0) - 1)
    def _():
        tl_ref[...] = total[0:BOX, 0:BOX, :]
        tr_ref[...] = total[0:BOX, BOX : 2 * BOX, :].astype(BF)
        bl_ref[...] = total[BOX : 2 * BOX, 0:BOX, :].astype(BF)
        br_ref[...] = total[BOX : 2 * BOX, BOX : 2 * BOX, :].astype(BF)


def spread(corners, inner, off_rows, kernel0):
    slots = corners.shape[0]
    whole = lambda *shape: pl.BlockSpec(shape, lambda i, *_: (0,) * len(shape))
    piece = lambda kind: jax.ShapeDtypeStruct((BOX, BOX, C), kind)
    return pl.pallas_call(
        spread_kernel,
        name="spread",
        out_shape=[piece(F32), piece(BF), piece(BF), piece(BF)],
        grid_spec=pltpu.PrefetchScalarGridSpec(
            num_scalar_prefetch=1,
            grid=(slots // SG,),
            in_specs=[
                pl.BlockSpec((SG, PIX, C), lambda i, *_: (i, 0, 0)),
                pl.BlockSpec((SG, 8, C), lambda i, *_: (i, 0, 0)),
                whole(9, C, C),
            ],
            out_specs=[whole(BOX, BOX, C)] * 4,
            scratch_shapes=[
                pltpu.VMEM((3, SG, ROWS, C), BF),
                pltpu.VMEM((SG, BOX, C), F32),
                pltpu.VMEM((SG, WIN, C), BF),
                pltpu.VMEM((2 * BOX, 2 * BOX, C), F32),
            ],
        ),
        cost_estimate=pl.CostEstimate(
            flops=7_000_000_000, bytes_accessed=6 << 20, transcendentals=0
        ),
    )(corners, inner, off_rows, kernel0)


def swap_cores(x):
    return lax.ppermute(x, "ha", [(i, i ^ 1) for i in range(lax.axis_size("ha"))])


def sum_everywhere(grads):
    core = lax.axis_index("ha") % 2
    rows = grads.shape[0] // 2
    mine = lax.dynamic_slice_in_dim(grads, core * rows, rows)
    other = lax.dynamic_slice_in_dim(grads, (1 - core) * rows, rows)
    half = (mine.astype(F32) + swap_cores(other).astype(F32)).astype(BF)
    peers = lax.axis_size("wa")
    parts = lax.all_to_all(half.reshape(peers, rows // peers, C), "wa", 0, 0, tiled=True)
    part = jnp.sum(parts.astype(F32), axis=0).astype(BF)
    total = part.astype(F32)
    count = lax.axis_size("ha")
    for hop in range(2, count, 2):
        moved = lax.ppermute(part, "ha", [(i, (i + hop) % count) for i in range(count)])
        total = total + moved.astype(F32)
    whole = jnp.broadcast_to(total.astype(BF)[None], (peers, *total.shape))
    half = lax.all_to_all(whole, "wa", 0, 0, tiled=True).reshape(rows, C)
    other = swap_cores(half)
    return jnp.where(
        core == 0, jnp.concatenate([half, other]), jnp.concatenate([other, half])
    ).astype(F32)


def local(features, counts, owner_perm, corners, offsets, kernels, cotangent):
    slots = corners.shape[0]
    peers = lax.axis_size("wa")
    col_index = lax.axis_index("wa")
    chunks = 4
    rows = BOX // chunks
    cut = lambda x: [x[rows * k : rows * (k + 1)] for k in range(chunks)]
    from_right = [shifted(piece, "wa", -1) for piece in cut(features)]
    below = shifted(features, "ha", -1)
    corner = [shifted(piece, "ha", -1) for piece in from_right]
    pieces = (features, jnp.concatenate(from_right), below, jnp.concatenate(corner))
    row_counts = lax.all_to_all(
        jnp.broadcast_to(counts[None], (peers, 1, 1)), "wa", 0, 0, tiled=True
    ).reshape(peers)
    ids = jnp.arange(peers, dtype=jnp.int32)
    starts = jnp.sum(jnp.where(ids[None, :] < ids[:, None], row_counts[None, :], 0), axis=1)
    here_start = jnp.sum(jnp.where(ids == col_index, starts, 0))
    perm_row = owner_perm[0]
    position = jnp.sum(jnp.where(perm_row == col_index, ids, 0))
    arrival = starts + (position - starts) % peers
    index = jnp.clip(arrival // peers, 0, cotangent.shape[0] - 1).astype(jnp.int32)
    stream = (here_start + ids) % peers
    owner_of = jnp.sum(jnp.where(stream[:, None] == ids[None, :], perm_row[None, :], 0), axis=1)
    meta = jnp.concatenate([owner_of, counts[0]]).astype(jnp.int32)
    outgoing = route(index, cotangent).reshape(peers, PIX, C)
    incoming = lax.all_to_all(outgoing, "wa", split_axis=0, concat_axis=0, tiled=True)
    shift = (corners[:, 1:2] % 16) * 4
    row_off = offsets[:, :SIDE].astype(F32)
    col_off = (offsets[:, SIDE:] + shift).astype(F32)
    pad = lambda x, n: jnp.pad(x, ((0, 0), (0, n)), constant_values=-1000.0)
    both = jnp.concatenate([pad(row_off, 2), pad(col_off, 2)], axis=1)
    off_cols = jnp.broadcast_to(both[:, :, None], (slots, 32, 128))
    row_lanes = pad(jnp.repeat(row_off, PITCH, axis=1), C - PIX)
    col_lanes = pad(jnp.tile(pad(col_off, 2), (1, SIDE)), C - PIX)
    off_rows = jnp.broadcast_to(
        jnp.stack([row_lanes, col_lanes], axis=1)[:, None], (slots, 4, 2, C)
    ).reshape(slots, 8, C)
    at = jnp.arange(WIN, dtype=jnp.int32)
    places = jnp.broadcast_to(
        jnp.stack([4 * (at // SPAN), 4 * (at % SPAN)])[None], (4, 2, WIN)
    ).reshape(8, WIN).astype(F32)
    taps = kernels.reshape(2, 9, C, C)
    acts0, acts1, slope0, slope1 = forward(corners, pieces, off_cols, places, taps)
    grad1 = last_grad(meta, incoming, slope1, acts1)
    inner, grad0 = middle_grad(meta, incoming, slope1, slope0, taps[1], acts0)
    grads = sum_everywhere(jnp.concatenate([grad0, grad1]).reshape(-1, C))
    tile, right, lower, corner = spread(corners, inner, off_rows, taps[0])
    parts = []
    for own, piece in zip(cut(right), cut(corner)):
        moved = shifted(piece, "ha", 1)
        parts.append(shifted((own.astype(F32) + moved.astype(F32)).astype(BF), "wa", 1))
    from_above = shifted(lower, "ha", 1)
    tile = tile + from_above.astype(F32) + jnp.concatenate(parts).astype(F32)
    return (tile, grads.reshape(2, 3, 3, C, C))


def solution(mesh):
    in_specs = (
        P("ha", "wa", None),
        P("ha", "wa"),
        P("ha", None),
        P(("ha", "wa"), None),
        P(("ha", "wa"), None),
        P(),
        P(("ha", "wa"), None, None, None),
    )
    out_specs = (P("ha", "wa", None), P())
    return jax.shard_map(local, mesh=mesh, in_specs=in_specs, out_specs=out_specs, check_vma=False)
```

time: 525 us -> 234 us (0.45)
  waiting for transfers between devices: 161 us -> 10.8 us
  local copies, waits for them, and re-layouts: 143 us -> 13.1 us
  matrix products: 119 us -> 0 us
  Pallas kernels: 0 us -> 84.3 us
  starting transfers between devices: 29.7 us -> 77.4 us
  other arithmetic: 51.1 us -> 17.8 us
  blocking collectives: 0 us -> 25 us
  between operations: 15.8 us -> 1.66 us
    dot_general x12 -> x0, matrix products: 119 us -> none  [the longest x2 26.6 us: mask_head(): lax.dot_general(inner_grad, matrix, (((1,), (1,)), ((), ())), preferred_e...]
    psum x1 -> x0, waiting for transfers between devices: 118 us -> none  [local(): kernel_grads = lax.psum(kernel_grads, ('ha', 'wa'))]
    pallas_call x0 -> x5, Pallas kernels: none -> 84.3 us  [the longest x1 24 us: spread(): pl.pallas_call(spread_kernel, name='spread', out_shape=[piece(F32), piece...]
    unnamed x73 -> x14, local copies, waits for them, and re-layouts: 45.3 us -> 4.83 us
    scatter-add x16 -> x0, other arithmetic: 31.8 us -> none  [fold_back(): totals.at[:, row_step:row_step + SIDE, col_step:col_step + SIDE, :]]
    ppermute x4 -> x18, starting transfers between devices: 14 us -> 45.2 us  [shifted(): lax.ppermute(value, axis, [(source, source + steps) for source in range(f...]
    concatenate x11 -> x0, local copies, waits for them, and re-layouts: 30.3 us -> none  [the longest x10 29.2 us: patches_of(): jnp.concatenate(pieces, axis=3).reshape(amount * SIDE * SIDE, 9 * channels)]
    ppermute x4 -> x18, waiting for transfers between devices: 31.1 us -> 5.72 us  [shifted(): lax.ppermute(value, axis, [(source, source + steps) for source in range(f...]
  transfers between devices with their start and end apart: 7 -> 26, of which waited for: 4 -> 6; matrix products, arithmetic and copies ran while one was open for 10% -> 10% of each run, Pallas kernels for 0% -> 24%
where the time goes in v1:
time: 234 us; the launch traced here: 230 us
  Pallas kernels  84.3 us (36%)
  starting transfers between devices  77.4 us (33%)
  blocking collectives  25 us (11%)
  other arithmetic  17.8 us (8%)
  local copies, waits for them, and re-layouts  13.1 us (6%)
  waiting for transfers between devices  10.8 us (5%)
    ppermute x18, starting transfers between devices, shifted(): lax.ppermute(value, axis, [(source, source + steps) for source in range(f...  45.2 us
    all_to_all x1, blocking collectives, sum_everywhere(): lax.all_to_all(half.reshape(peers, rows // peers, C), 'wa', 0, 0, tiled=T...  25 us
    pallas_call x1, Pallas kernels, spread(): pl.pallas_call(spread_kernel, name='spread', out_shape=[piece(F32), piece...  24 us
    pallas_call x1, Pallas kernels, forward(): pl.pallas_call(forward_kernel, name='forward', out_shape=[jax.ShapeDtypeS...  22.6 us
    pallas_call x1, Pallas kernels, middle_grad(): pl.pallas_call(middle_kernel, name='middle_grad', out_shape=[jax.ShapeDty...  18.2 us
    all_to_all x1, starting transfers between devices, local(): lax.all_to_all(jnp.broadcast_to(counts[None], (peers, 1, 1)), 'wa', 0, 0,...  12.9 us
    pallas_call x1, Pallas kernels, last_grad(): pl.pallas_call(last_kernel, name='last_grad', out_shape=jax.ShapeDtypeStr...  10.7 us
    pallas_call x1, Pallas kernels, route(): pl.pallas_call(route_kernel, name='route', out_shape=jax.ShapeDtypeStruct...  8.81 us
  transfers between devices with their start and end apart: 26, of which 6 were waited for; matrix products, arithmetic and copies ran while one was open for 10% of the time, Pallas kernels for 24%

profile of v1, /device:TPU:1, one launch (start us, length us, event | category | flops | bytes accessed | tf_op | source)
XLA Modules:
  0.0 230.2 jit_solution(3871939875037897654)
XLA Ops:
  0.6 3.4 %collective-permute-start.4 = (bf16[32,32,256]{2,1,0:T(8,128)(2,1)}, bf16[32,32,256]{2,1,0:T(8,128)(2,1)}, u32[]{:S(2)}, u32[]{:S(2)}) collective-permute-start(bf16[32,32,256]{2,1,0:T(8,128)(2,1)} %tl_ref.1), channel_id=1, source_target_pairs={{16,0},{32,16},{48,32},{64,48},{80,64},{96,80},{112,96},{17,1},{33... | collective-permute-start | bytes 1572872 | tf_op jit(solution)/shard_map/ppermute | solution.py:25
  11.7 12.9 %all-to-all-start = ((s32[16,1,1]{2,1,0:T(1,128)}), s32[16,1,1]{2,1,0:T(1,128)S(1)}, u32[]{:S(2)}, u32[]{:S(2)}) async-start(s32[16,1,1]{2,1,0:T(1,128)} %broadcast_in_dim.67), calls=%async_computation | async-start | bytes 16384 | tf_op jit(solution)/shard_map/all_to_all | solution.py:403
  34.2 8.8 %route.1 = bf16[16,14,16,256]{3,2,1,0:T(8,128)(2,1)} custom-call(s32[16]{0:T(128)} %get-tuple-element.38.index_ref, bf16[8,14,14,256]{3,2,1,0:T(8,128)(2,1)} %copy.24.x_ref), custom_call_target="tpu_custom_call" | custom-call | bytes 4194304 | tf_op jit(solution)/shard_map/route/pallas_call | solution.py:67
  43.0 7.2 %all-to-all-start.1 = ((bf16[16,224,256]{2,1,0:T(8,128)(2,1)}), bf16[16,224,256]{2,1,0:T(8,128)(2,1)S(1)}, u32[]{:S(2)}, u32[]{:S(2)}) async-start(bf16[16,224,256]{2,1,0:T(8,128)(2,1)} %bitcast.24), calls=%async_computation.1 | async-start | bytes 3670016 | tf_op jit(solution)/shard_map/all_to_all | solution.py:417
  51.1 3.3 %collective-permute-start.5 = (bf16[8,32,256]{2,1,0:T(8,128)(2,1)S(1)}, bf16[8,32,256]{2,1,0:T(8,128)(2,1)S(1)}, u32[]{:S(2)}, u32[]{:S(2)}) collective-permute-start(bf16[8,32,256]{2,1,0:T(8,128)(2,1)S(1)} %collective-permute-done), channel_id=1, source_target_pairs={{16,0},{32,16},{48,32},{64,48},{80,64},{96,80},{112,96},{17,1},{33... | collective-permute-start | bytes 393224 | tf_op jit(solution)/shard_map/ppermute | solution.py:25
  66.6 22.6 %forward.1 = (bf16[256,4096]{1,0:T(8,128)(2,1)}, bf16[256,4096]{1,0:T(8,128)(2,1)}, bf16[16,224,256]{2,1,0:T(8,128)(2,1)}, bf16[16,224,256]{2,1,0:T(8,128)(2,1)}) custom-call(s32[16,2]{1,0:T(8,128)} %copy.27.corner_ref, bf16[32,32,256]{2,1,0:T(8,128)(2,1)} %tl_ref.1, bf16[32,32,256]{2,1,0:T(8,128)(2,1)} %pad_maximum_fusion.1.tr_ref, ...), custom_call_target="tpu_custom_call" | custom-call | flops 11299999744 | bytes 12582912 | tf_op jit(solution)/shard_map/forward/pallas_call | solution.py:131
  90.4 10.7 %last_grad.1 = bf16[9,256,256]{2,1,0:T(8,128)(2,1)} custom-call(s32[17]{0:T(128)} %pad_add_fusion.meta_ref, bf16[16,224,256]{2,1,0:T(8,128)(2,1)} %copy-done.1, bf16[16,224,256]{2,1,0:T(8,128)(2,1)} %get-tuple-element.12.g1_ref, bf16[256,4096]{1,0:T(8,128)(2,1)} %get-tuple-element.21.a_ref), custom_call_target="tpu_custom_call" | custom-call | flops 4800000000 | bytes 8388608 | tf_op jit(solution)/shard_map/last_grad/pallas_call | solution.py:207
  101.2 18.2 %middle_grad.1 = (bf16[16,224,256]{2,1,0:T(8,128)(2,1)}, bf16[9,256,256]{2,1,0:T(8,128)(2,1)}) custom-call(s32[17]{0:T(128)} %pad_add_fusion.meta_ref, bf16[16,224,256]{2,1,0:T(8,128)(2,1)} %copy-done.1, bf16[16,224,256]{2,1,0:T(8,128)(2,1)} %get-tuple-element.12.g1_ref, bf16[16,224,256]{2,1,0:T(8,128)(2,1)} %get-tuple-element.13.g0_ref, ...), custom_call_target="tpu_custom_call" | custom-call | flops 8999999488 | bytes 12582912 | tf_op jit(solution)/shard_map/middle_grad/pallas_call | solution.py:261
  121.0 3.0 %collective-permute-done.18 = bf16[2304,256]{1,0:T(8,128)(2,1)} collective-permute-done((bf16[2304,256]{1,0:T(8,128)(2,1)S(1)}, bf16[2304,256]{1,0:T(8,128)(2,1)}, u32[]{:S(2)}, u32[]{:S(2)}) %collective-permute-start.18) | collective-permute-done | bytes 1179680 | tf_op jit(solution)/shard_map/ppermute | solution.py:367
  125.5 25.0 %all_to_all.20 = bf16[16,144,256]{2,1,0:T(8,128)(2,1)S(1)} all-to-all(bf16[16,144,256]{2,1,0:T(8,128)(2,1)S(1)} %bitcast.27), channel_id=1, replica_groups=mesh['ha'=8,'wa'=16] {'wa'}, dimensions={0} | all-to-all | bytes 2359296 | tf_op jit(solution)/shard_map/all_to_all | solution.py:377
  160.1 3.9 %all-to-all-start.3 = ((bf16[16,144,256]{2,1,0:T(8,128)(2,1)}), bf16[16,144,256]{2,1,0:T(8,128)(2,1)S(1)}, u32[]{:S(2)}, u32[]{:S(2)}) async-start(bf16[16,144,256]{2,1,0:T(8,128)(2,1)} %broadcast_in_dim.78), calls=%async_computation.3 | async-start | bytes 2359296 | tf_op jit(solution)/shard_map/all_to_all | solution.py:385
  165.2 24.0 %spread.1 = (f32[32,32,256]{2,1,0:T(8,128)}, bf16[32,32,256]{2,1,0:T(8,128)(2,1)}, bf16[32,32,256]{2,1,0:T(8,128)(2,1)}, bf16[32,32,256]{2,1,0:T(8,128)(2,1)}) custom-call(s32[16,2]{1,0:T(8,128)} %copy.27.corner_ref, bf16[16,224,256]{2,1,0:T(8,128)(2,1)} %get-tuple-element.15.p_ref, f32[16,8,256]{2,1,0:T(8,128)} %reshape.121.off_ref, ...), custom_call_target="tpu_custom_call" | custom-call | flops 7000000000 | bytes 6291456 | tf_op jit(solution)/shard_map/spread/pallas_call | solution.py:340
  192.3 2.8 %collective-permute-start.10 = (bf16[8,32,256]{2,1,0:T(8,128)(2,1)S(1)}, bf16[8,32,256]{2,1,0:T(8,128)(2,1)S(1)}, u32[]{:S(2)}, u32[]{:S(2)}) collective-permute-start(bf16[8,32,256]{2,1,0:T(8,128)(2,1)S(1)} %get-tuple-element.28), channel_id=1, source_target_pairs={{0,16},{16,32},{32,48},{48,64},{64,80},{80,96},{96,112},{1,17},{17... | collective-permute-start | bytes 393224 | tf_op jit(solution)/shard_map/ppermute | solution.py:25
  195.2 2.3 %collective-permute-start.12 = (bf16[8,32,256]{2,1,0:T(8,128)(2,1)S(1)}, bf16[8,32,256]{2,1,0:T(8,128)(2,1)S(1)}, u32[]{:S(2)}, u32[]{:S(2)}) collective-permute-start(bf16[8,32,256]{2,1,0:T(8,128)(2,1)S(1)} %get-tuple-element.31), channel_id=1, source_target_pairs={{0,16},{16,32},{32,48},{48,64},{64,80},{80,96},{96,112},{1,17},{17... | collective-permute-start | bytes 393224 | tf_op jit(solution)/shard_map/ppermute | solution.py:25
  197.5 3.0 %collective-permute-start.14 = (bf16[8,32,256]{2,1,0:T(8,128)(2,1)S(1)}, bf16[8,32,256]{2,1,0:T(8,128)(2,1)S(1)}, u32[]{:S(2)}, u32[]{:S(2)}) collective-permute-start(bf16[8,32,256]{2,1,0:T(8,128)(2,1)S(1)} %get-tuple-element.30), channel_id=1, source_target_pairs={{0,16},{16,32},{32,48},{48,64},{64,80},{80,96},{96,112},{1,17},{17... | collective-permute-start | bytes 393224 | tf_op jit(solution)/shard_map/ppermute | solution.py:25
  200.5 2.3 %collective-permute-start.16 = (bf16[8,32,256]{2,1,0:T(8,128)(2,1)S(1)}, bf16[8,32,256]{2,1,0:T(8,128)(2,1)S(1)}, u32[]{:S(2)}, u32[]{:S(2)}) collective-permute-start(bf16[8,32,256]{2,1,0:T(8,128)(2,1)S(1)} %get-tuple-element.29), channel_id=1, source_target_pairs={{0,16},{16,32},{32,48},{48,64},{64,80},{80,96},{96,112},{1,17},{17... | collective-permute-start | bytes 393224 | tf_op jit(solution)/shard_map/ppermute | solution.py:25
  202.8 4.0 %collective-permute-start.9 = (bf16[32,32,256]{2,1,0:T(8,128)(2,1)}, bf16[32,32,256]{2,1,0:T(8,128)(2,1)}, u32[]{:S(2)}, u32[]{:S(2)}) collective-permute-start(bf16[32,32,256]{2,1,0:T(8,128)(2,1)} %get-tuple-element.17), channel_id=1, source_target_pairs={{0,16},{16,32},{32,48},{48,64},{64,80},{80,96},{96,112},{1,17},{17... | collective-permute-start | bytes 1572872 | tf_op jit(solution)/shard_map/ppermute | solution.py:25
  208.8 3.4 %collective-permute-start.11 = (bf16[8,32,256]{2,1,0:T(8,128)(2,1)S(1)}, bf16[8,32,256]{2,1,0:T(8,128)(2,1)S(1)}, u32[]{:S(2)}, u32[]{:S(2)}) collective-permute-start(bf16[8,32,256]{2,1,0:T(8,128)(2,1)S(1)} %get-tuple-element.24), channel_id=1, source_target_pairs={{0,1},{1,2},{2,3},{3,4},{4,5},{5,6},{6,7},{7,8},{8,9},{9,10},{10,1... | collective-permute-start | bytes 393224 | tf_op jit(solution)/shard_map/ppermute | solution.py:25
  212.3 3.7 %collective-permute-start.13 = (bf16[8,32,256]{2,1,0:T(8,128)(2,1)}, bf16[8,32,256]{2,1,0:T(8,128)(2,1)}, u32[]{:S(2)}, u32[]{:S(2)}) collective-permute-start(bf16[8,32,256]{2,1,0:T(8,128)(2,1)} %get-tuple-element.27), channel_id=1, source_target_pairs={{0,1},{1,2},{2,3},{3,4},{4,5},{5,6},{6,7},{7,8},{8,9},{9,10},{10,1... | collective-permute-start | bytes 393224 | tf_op jit(solution)/shard_map/ppermute | solution.py:25
  216.0 2.8 %collective-permute-start.15 = (bf16[8,32,256]{2,1,0:T(8,128)(2,1)}, bf16[8,32,256]{2,1,0:T(8,128)(2,1)}, u32[]{:S(2)}, u32[]{:S(2)}) collective-permute-start(bf16[8,32,256]{2,1,0:T(8,128)(2,1)} %get-tuple-element.26), channel_id=1, source_target_pairs={{0,1},{1,2},{2,3},{3,4},{4,5},{5,6},{6,7},{7,8},{8,9},{9,10},{10,1... | collective-permute-start | bytes 393224 | tf_op jit(solution)/shard_map/ppermute | solution.py:25
  218.8 3.1 %collective-permute-start.17 = (bf16[8,32,256]{2,1,0:T(8,128)(2,1)}, bf16[8,32,256]{2,1,0:T(8,128)(2,1)}, u32[]{:S(2)}, u32[]{:S(2)}) collective-permute-start(bf16[8,32,256]{2,1,0:T(8,128)(2,1)} %get-tuple-element.25), channel_id=1, source_target_pairs={{0,1},{1,2},{2,3},{3,4},{4,5},{5,6},{6,7},{7,8},{8,9},{9,10},{10,1... | collective-permute-start | bytes 393224 | tf_op jit(solution)/shard_map/ppermute | solution.py:25
  222.0 2.5 %collective-permute-done.17 = bf16[8,32,256]{2,1,0:T(8,128)(2,1)} collective-permute-done((bf16[8,32,256]{2,1,0:T(8,128)(2,1)}, bf16[8,32,256]{2,1,0:T(8,128)(2,1)}, u32[]{:S(2)}, u32[]{:S(2)}) %collective-permute-start.17) | collective-permute-done | bytes 131104 | tf_op jit(solution)/shard_map/ppermute | solution.py:25
  224.5 2.3 %convert_add_fusion = f32[32,32,256]{2,1,0:T(8,128)} fusion(f32[32,32,256]{2,1,0:T(8,128)S(1)} %copy-done.3, bf16[32,32,256]{2,1,0:T(8,128)(2,1)} %collective-permute-done.9, bf16[8,32,256]{2,1,0:T(8,128)(2,1)} %collective-permute-done.17, bf16[8,32,256]{2,1,0:T(8,128)(2,1)} %collective-permute-done.15, bf16[8,32,256]{2,1,0:T(8,128)(2,1)} %collective-permute-done.13, ...), kind=kLoop, calls=%fused_computation.3 | loop fusion | flops 1835008 | bytes 3145728 | tf_op jit(solution)/shard_map/add | solution.py:444
  227.5 2.7 %convert.2 = f32[2,3,3,256,256]{4,3,2,1,0:T(8,128)} convert(bf16[2,3,3,256,256]{4,3,2,1,0:T(8,128)(2,1)S(1)} %bitcast.21) | non-fusion elementwise | flops 1179648 | bytes 7077888 | tf_op jit(solution)/shard_map/convert_element_type | solution.py:389
  (89 shorter events, 50.4 us)
Async XLA Ops:
  0.6 65.1 %collective-permute-start.4 = (bf16[32,32,256]{2,1,0:T(8,128)(2,1)}, bf16[32,32,256]{2,1,0:T(8,128)(2,1)}, u32[]{:S(2)}, u32[]{:S(2)}) collective-permute-start(bf16[32,32,256]{2,1,0:T(8,128)(2,1)} %tl_ref.1), channel_id=1, source_target_pairs={{16,0},{32,16},{48,32},{64,48},{80,64},{96,80},{112,96},{17,1},{33... | collective-permute-start | bytes 1572872 | tf_op jit(solution)/shard_map/ppermute | solution.py:25
  5.2 45.9 %collective-permute-start = (bf16[8,32,256]{2,1,0:T(8,128)(2,1)S(1)}, bf16[8,32,256]{2,1,0:T(8,128)(2,1)S(1)}, u32[]{:S(2)}, u32[]{:S(2)}) collective-permute-start(bf16[8,32,256]{2,1,0:T(8,128)(2,1)S(1)} %get-tuple-element.32), channel_id=1, source_target_pairs={{1,0},{2,1},{3,2},{4,3},{5,4},{6,5},{7,6},{8,7},{9,8},{10,9},{11,1... | collective-permute-start | bytes 393224 | tf_op jit(solution)/shard_map/ppermute | solution.py:25
  6.5 47.9 %collective-permute-start.1 = (bf16[8,32,256]{2,1,0:T(8,128)(2,1)S(1)}, bf16[8,32,256]{2,1,0:T(8,128)(2,1)S(1)}, u32[]{:S(2)}, u32[]{:S(2)}) collective-permute-start(bf16[8,32,256]{2,1,0:T(8,128)(2,1)S(1)} %get-tuple-element.35), channel_id=1, source_target_pairs={{1,0},{2,1},{3,2},{4,3},{5,4},{6,5},{7,6},{8,7},{9,8},{10,9},{11,1... | collective-permute-start | bytes 393224 | tf_op jit(solution)/shard_map/ppermute | solution.py:25
  7.8 48.5 %collective-permute-start.2 = (bf16[8,32,256]{2,1,0:T(8,128)(2,1)S(1)}, bf16[8,32,256]{2,1,0:T(8,128)(2,1)S(1)}, u32[]{:S(2)}, u32[]{:S(2)}) collective-permute-start(bf16[8,32,256]{2,1,0:T(8,128)(2,1)S(1)} %get-tuple-element.34), channel_id=1, source_target_pairs={{1,0},{2,1},{3,2},{4,3},{5,4},{6,5},{7,6},{8,7},{9,8},{10,9},{11,1... | collective-permute-start | bytes 393224 | tf_op jit(solution)/shard_map/ppermute | solution.py:25
  9.1 49.2 %collective-permute-start.3 = (bf16[8,32,256]{2,1,0:T(8,128)(2,1)S(1)}, bf16[8,32,256]{2,1,0:T(8,128)(2,1)S(1)}, u32[]{:S(2)}, u32[]{:S(2)}) collective-permute-start(bf16[8,32,256]{2,1,0:T(8,128)(2,1)S(1)} %get-tuple-element.33), channel_id=1, source_target_pairs={{1,0},{2,1},{3,2},{4,3},{5,4},{6,5},{7,6},{8,7},{9,8},{10,9},{11,1... | collective-permute-start | bytes 393224 | tf_op jit(solution)/shard_map/ppermute | solution.py:25
  11.7 20.2 %all-to-all-start = ((s32[16,1,1]{2,1,0:T(1,128)}), s32[16,1,1]{2,1,0:T(1,128)S(1)}, u32[]{:S(2)}, u32[]{:S(2)}) async-start(s32[16,1,1]{2,1,0:T(1,128)} %broadcast_in_dim.67), calls=%async_computation | async-start | bytes 16384 | tf_op jit(solution)/shard_map/all_to_all | solution.py:403
  43.0 46.2 %all-to-all-start.1 = ((bf16[16,224,256]{2,1,0:T(8,128)(2,1)}), bf16[16,224,256]{2,1,0:T(8,128)(2,1)S(1)}, u32[]{:S(2)}, u32[]{:S(2)}) async-start(bf16[16,224,256]{2,1,0:T(8,128)(2,1)} %bitcast.24), calls=%async_computation.1 | async-start | bytes 3670016 | tf_op jit(solution)/shard_map/all_to_all | solution.py:417
  51.1 10.6 %collective-permute-start.5 = (bf16[8,32,256]{2,1,0:T(8,128)(2,1)S(1)}, bf16[8,32,256]{2,1,0:T(8,128)(2,1)S(1)}, u32[]{:S(2)}, u32[]{:S(2)}) collective-permute-start(bf16[8,32,256]{2,1,0:T(8,128)(2,1)S(1)} %collective-permute-done), channel_id=1, source_target_pairs={{16,0},{32,16},{48,32},{64,48},{80,64},{96,80},{112,96},{17,1},{33... | collective-permute-start | bytes 393224 | tf_op jit(solution)/shard_map/ppermute | solution.py:25
  54.4 7.3 %collective-permute-start.6 = (bf16[8,32,256]{2,1,0:T(8,128)(2,1)S(1)}, bf16[8,32,256]{2,1,0:T(8,128)(2,1)S(1)}, u32[]{:S(2)}, u32[]{:S(2)}) collective-permute-start(bf16[8,32,256]{2,1,0:T(8,128)(2,1)S(1)} %collective-permute-done.1), channel_id=1, source_target_pairs={{16,0},{32,16},{48,32},{64,48},{80,64},{96,80},{112,96},{17,1},{33... | collective-permute-start | bytes 393224 | tf_op jit(solution)/shard_map/ppermute | solution.py:25
  56.4 6.6 %collective-permute-start.7 = (bf16[8,32,256]{2,1,0:T(8,128)(2,1)S(1)}, bf16[8,32,256]{2,1,0:T(8,128)(2,1)S(1)}, u32[]{:S(2)}, u32[]{:S(2)}) collective-permute-start(bf16[8,32,256]{2,1,0:T(8,128)(2,1)S(1)} %collective-permute-done.2), channel_id=1, source_target_pairs={{16,0},{32,16},{48,32},{64,48},{80,64},{96,80},{112,96},{17,1},{33... | collective-permute-start | bytes 393224 | tf_op jit(solution)/shard_map/ppermute | solution.py:25
  58.3 6.6 %collective-permute-start.8 = (bf16[8,32,256]{2,1,0:T(8,128)(2,1)S(1)}, bf16[8,32,256]{2,1,0:T(8,128)(2,1)S(1)}, u32[]{:S(2)}, u32[]{:S(2)}) collective-permute-start(bf16[8,32,256]{2,1,0:T(8,128)(2,1)S(1)} %collective-permute-done.3), channel_id=1, source_target_pairs={{16,0},{32,16},{48,32},{64,48},{80,64},{96,80},{112,96},{17,1},{33... | collective-permute-start | bytes 393224 | tf_op jit(solution)/shard_map/ppermute | solution.py:25
  150.7 6.1 %collective-permute-start.19 = (bf16[144,256]{1,0:T(8,128)(2,1)S(1)}, bf16[144,256]{1,0:T(8,128)(2,1)S(1)}, u32[]{:S(2)}, u32[]{:S(2)}) collective-permute-start(bf16[144,256]{1,0:T(8,128)(2,1)S(1)} %reduce_sum.52), channel_id=1, source_target_pairs={{0,32},{16,48},{32,64},{48,80},{64,96},{80,112},{96,0},{112,16},{1... | collective-permute-start | bytes 221192 | tf_op jit(solution)/shard_map/ppermute | solution.py:382
  152.7 4.9 %collective-permute-start.20 = (bf16[144,256]{1,0:T(8,128)(2,1)S(1)}, bf16[144,256]{1,0:T(8,128)(2,1)S(1)}, u32[]{:S(2)}, u32[]{:S(2)}) collective-permute-start(bf16[144,256]{1,0:T(8,128)(2,1)S(1)} %reduce_sum.52), channel_id=1, source_target_pairs={{0,64},{16,80},{32,96},{48,112},{64,0},{80,16},{96,32},{112,48},{1... | collective-permute-start | bytes 221192 | tf_op jit(solution)/shard_map/ppermute | solution.py:382
  160.1 29.1 %all-to-all-start.3 = ((bf16[16,144,256]{2,1,0:T(8,128)(2,1)}), bf16[16,144,256]{2,1,0:T(8,128)(2,1)S(1)}, u32[]{:S(2)}, u32[]{:S(2)}) async-start(bf16[16,144,256]{2,1,0:T(8,128)(2,1)} %broadcast_in_dim.78), calls=%async_computation.3 | async-start | bytes 2359296 | tf_op jit(solution)/shard_map/all_to_all | solution.py:385
  189.2 37.6 %collective-permute-start.22 = (bf16[2304,256]{1,0:T(8,128)(2,1)S(1)}, bf16[2304,256]{1,0:T(8,128)(2,1)S(1)}, u32[]{:S(2)}, u32[]{:S(2)}) collective-permute-start(bf16[2304,256]{1,0:T(8,128)(2,1)S(1)} %bitcast.25), channel_id=1, source_target_pairs={{0,16},{16,0},{32,48},{48,32},{64,80},{80,64},{96,112},{112,96},{1... | collective-permute-start | bytes 3538952 | tf_op jit(solution)/shard_map/ppermute | solution.py:367
  192.3 10.5 %collective-permute-start.10 = (bf16[8,32,256]{2,1,0:T(8,128)(2,1)S(1)}, bf16[8,32,256]{2,1,0:T(8,128)(2,1)S(1)}, u32[]{:S(2)}, u32[]{:S(2)}) collective-permute-start(bf16[8,32,256]{2,1,0:T(8,128)(2,1)S(1)} %get-tuple-element.28), channel_id=1, source_target_pairs={{0,16},{16,32},{32,48},{48,64},{64,80},{80,96},{96,112},{1,17},{17... | collective-permute-start | bytes 393224 | tf_op jit(solution)/shard_map/ppermute | solution.py:25
  195.2 11.7 %collective-permute-start.12 = (bf16[8,32,256]{2,1,0:T(8,128)(2,1)S(1)}, bf16[8,32,256]{2,1,0:T(8,128)(2,1)S(1)}, u32[]{:S(2)}, u32[]{:S(2)}) collective-permute-start(bf16[8,32,256]{2,1,0:T(8,128)(2,1)S(1)} %get-tuple-element.31), channel_id=1, source_target_pairs={{0,16},{16,32},{32,48},{48,64},{64,80},{80,96},{96,112},{1,17},{17... | collective-permute-start | bytes 393224 | tf_op jit(solution)/shard_map/ppermute | solution.py:25
  197.5 9.4 %collective-permute-start.14 = (bf16[8,32,256]{2,1,0:T(8,128)(2,1)S(1)}, bf16[8,32,256]{2,1,0:T(8,128)(2,1)S(1)}, u32[]{:S(2)}, u32[]{:S(2)}) collective-permute-start(bf16[8,32,256]{2,1,0:T(8,128)(2,1)S(1)} %get-tuple-element.30), channel_id=1, source_target_pairs={{0,16},{16,32},{32,48},{48,64},{64,80},{80,96},{96,112},{1,17},{17... | collective-permute-start | bytes 393224 | tf_op jit(solution)/shard_map/ppermute | solution.py:25
  200.5 6.4 %collective-permute-start.16 = (bf16[8,32,256]{2,1,0:T(8,128)(2,1)S(1)}, bf16[8,32,256]{2,1,0:T(8,128)(2,1)S(1)}, u32[]{:S(2)}, u32[]{:S(2)}) collective-permute-start(bf16[8,32,256]{2,1,0:T(8,128)(2,1)S(1)} %get-tuple-element.29), channel_id=1, source_target_pairs={{0,16},{16,32},{32,48},{48,64},{64,80},{80,96},{96,112},{1,17},{17... | collective-permute-start | bytes 393224 | tf_op jit(solution)/shard_map/ppermute | solution.py:25
  202.8 21.7 %collective-permute-start.9 = (bf16[32,32,256]{2,1,0:T(8,128)(2,1)}, bf16[32,32,256]{2,1,0:T(8,128)(2,1)}, u32[]{:S(2)}, u32[]{:S(2)}) collective-permute-start(bf16[32,32,256]{2,1,0:T(8,128)(2,1)} %get-tuple-element.17), channel_id=1, source_target_pairs={{0,16},{16,32},{32,48},{48,64},{64,80},{80,96},{96,112},{1,17},{17... | collective-permute-start | bytes 1572872 | tf_op jit(solution)/shard_map/ppermute | solution.py:25
  208.8 10.0 %collective-permute-start.11 = (bf16[8,32,256]{2,1,0:T(8,128)(2,1)S(1)}, bf16[8,32,256]{2,1,0:T(8,128)(2,1)S(1)}, u32[]{:S(2)}, u32[]{:S(2)}) collective-permute-start(bf16[8,32,256]{2,1,0:T(8,128)(2,1)S(1)} %get-tuple-element.24), channel_id=1, source_target_pairs={{0,1},{1,2},{2,3},{3,4},{4,5},{5,6},{6,7},{7,8},{8,9},{9,10},{10,1... | collective-permute-start | bytes 393224 | tf_op jit(solution)/shard_map/ppermute | solution.py:25
  212.3 9.7 %collective-permute-start.13 = (bf16[8,32,256]{2,1,0:T(8,128)(2,1)}, bf16[8,32,256]{2,1,0:T(8,128)(2,1)}, u32[]{:S(2)}, u32[]{:S(2)}) collective-permute-start(bf16[8,32,256]{2,1,0:T(8,128)(2,1)} %get-tuple-element.27), channel_id=1, source_target_pairs={{0,1},{1,2},{2,3},{3,4},{4,5},{5,6},{6,7},{7,8},{8,9},{9,10},{10,1... | collective-permute-start | bytes 393224 | tf_op jit(solution)/shard_map/ppermute | solution.py:25
  216.0 6.0 %collective-permute-start.15 = (bf16[8,32,256]{2,1,0:T(8,128)(2,1)}, bf16[8,32,256]{2,1,0:T(8,128)(2,1)}, u32[]{:S(2)}, u32[]{:S(2)}) collective-permute-start(bf16[8,32,256]{2,1,0:T(8,128)(2,1)} %get-tuple-element.26), channel_id=1, source_target_pairs={{0,1},{1,2},{2,3},{3,4},{4,5},{5,6},{6,7},{7,8},{8,9},{9,10},{10,1... | collective-permute-start | bytes 393224 | tf_op jit(solution)/shard_map/ppermute | solution.py:25
  218.8 5.6 %collective-permute-start.17 = (bf16[8,32,256]{2,1,0:T(8,128)(2,1)}, bf16[8,32,256]{2,1,0:T(8,128)(2,1)}, u32[]{:S(2)}, u32[]{:S(2)}) collective-permute-start(bf16[8,32,256]{2,1,0:T(8,128)(2,1)} %get-tuple-element.25), channel_id=1, source_target_pairs={{0,1},{1,2},{2,3},{3,4},{4,5},{5,6},{6,7},{7,8},{8,9},{9,10},{10,1... | collective-permute-start | bytes 393224 | tf_op jit(solution)/shard_map/ppermute | solution.py:25
  (8 other events, 94.2 us)

commit v2 on v1

v2 whole, which is shorter than its diff:
```python
import functools

import jax
import jax.numpy as jnp
from jax import lax
from jax.experimental import pallas as pl
from jax.experimental.pallas import tpu as pltpu
from jax.sharding import PartitionSpec as P

SIDE = 14
PITCH = 16
PIX = SIDE * PITCH
BOX = 32
SPAN = 48
WIN = BOX * SPAN
ROWS = 288
C = 256
BF = jnp.bfloat16
F32 = jnp.float32


def shifted(value, axis, steps):
    count = lax.axis_size(axis)
    first, last = (max(0, -steps), min(count, count - steps))
    return lax.ppermute(value, axis, [(source, source + steps) for source in range(first, last)])


def dot(a, b, dims=(((1,), (0,)), ((), ()))):
    return lax.dot_general(a, b, dims, preferred_element_type=F32)


def inside(rows):
    pixel = lax.broadcasted_iota(jnp.int32, (rows, C), 0)
    return (pixel & (PITCH - 1)) < SIDE


def clear_edges(held, copies):
    for shift in range(3):
        for g in range(copies):
            held[shift, g, 0:16, :] = jnp.zeros((16, C), BF)
            held[shift, g, 16 + PIX : ROWS, :] = jnp.zeros((ROWS - 16 - PIX, C), BF)


def hold(held, g, value):
    held[0, g, 16 : 16 + PIX, :] = pltpu.roll(value, 1, 0).astype(BF)
    held[1, g, 16 : 16 + PIX, :] = value.astype(BF)
    held[2, g, 16 : 16 + PIX, :] = pltpu.roll(value, PIX - 1, 0).astype(BF)


def tent(places, offsets):
    return jnp.maximum(0.0, 1.0 - jnp.abs(places - offsets) * 0.25)


def gelu_parts(v):
    cdf = 0.5 * (1.0 + lax.erf(v * 0.7071067811865476))
    slope = cdf + v * (jnp.exp(v * v * -0.5) * 0.3989422804014327)
    return v * cdf, slope


def route_kernel(count_ref, perm_ref, x_ref, o_ref, meta_ref):
    peers = o_ref.shape[0]
    here = lax.axis_index("wa")
    position = jnp.int32(0)
    for i in range(peers):
        position = jnp.where(perm_ref[0, i] == here, i, position)
    start = jnp.int32(0)
    here_start = jnp.int32(0)
    gap = jnp.zeros((SIDE, PITCH - SIDE, C), BF)
    for i in range(peers):
        here_start = jnp.where(here == i, start, here_start)
        arrival = start + ((position - start) & (peers - 1))
        region = jnp.clip(arrival // peers, 0, x_ref.shape[0] - 1)
        o_ref[i, :, 0:SIDE, :] = x_ref[region]
        o_ref[i, :, SIDE:PITCH, :] = gap
        start = start + count_ref[i]
    for i in range(peers):
        meta_ref[i] = perm_ref[0, (here_start + i) & (peers - 1)]
    meta_ref[peers] = count_ref[here]


def route(counts, perm, cotangent):
    peers = counts.shape[0]
    smem = pl.BlockSpec(memory_space=pltpu.SMEM)
    vmem = pl.BlockSpec(memory_space=pltpu.VMEM)
    return pl.pallas_call(
        route_kernel,
        name="route",
        out_shape=[
            jax.ShapeDtypeStruct((peers, SIDE, PITCH, C), BF),
            jax.ShapeDtypeStruct((peers + 1,), jnp.int32),
        ],
        in_specs=[smem, smem, vmem],
        out_specs=[vmem, smem],
        cost_estimate=pl.CostEstimate(flops=0, bytes_accessed=4 << 20, transcendentals=0),
    )(counts, perm, cotangent)


FG = 4


def forward_kernel(
    corner_ref, tl_ref, tr0_ref, tr1_ref, bl_ref, br0_ref, br1_ref, off_ref, k_ref,
    a0_ref, a1_ref, g0_ref, g1_ref, t_ref, ext, places, row_w, weight, held,
):
    step = pl.program_id(0)
    half = BOX // 2

    @pl.when(step == 0)
    def _():
        clear_edges(held, FG)
        ext[0:BOX, 0:BOX, :] = tl_ref[...]
        ext[0:half, BOX : 2 * BOX, :] = tr0_ref[...]
        ext[half:BOX, BOX : 2 * BOX, :] = tr1_ref[...]
        ext[BOX : 2 * BOX, 0:BOX, :] = bl_ref[...]
        ext[BOX : BOX + half, BOX : 2 * BOX, :] = br0_ref[...]
        ext[BOX + half : 2 * BOX, BOX : 2 * BOX, :] = br1_ref[...]
        at = lax.broadcasted_iota(jnp.int32, (16, WIN), 1).astype(F32)
        row = jnp.floor((at + 0.5) * (1.0 / SPAN))
        places[0] = 4.0 * row
        places[1] = 4.0 * (at - SPAN * row)

    keep = inside(PIX)
    lane = lax.broadcasted_iota(jnp.int32, (32, 128), 1)
    for g in range(FG):
        slot = step * FG + g
        top = corner_ref[slot]
        left = pl.multiple_of(corner_ref[16 + slot] // 16 * 16, 16)
        offsets = jnp.sum(jnp.where(lane == slot, off_ref[...], 0.0), axis=1, keepdims=True)
        row_w[g] = tent(places[0], offsets[0:16])
        col_w = tent(places[1], offsets[16:32])
        for i in range(SIDE):
            weight[g, i * PITCH : (i + 1) * PITCH, :] = (row_w[g, i : i + 1, :] * col_w).astype(BF)
        window = ext[pl.ds(top, BOX), pl.ds(left, SPAN), :].reshape(WIN, C)
        hold(held, g, dot(weight[g], window))
        a0_ref[:, g * C : (g + 1) * C] = held[1, g, 16 : 16 + C, :].T
    for i in range(5):
        tap = jnp.minimum(step * 5 + i, 17)
        t_ref[tap] = k_ref[tap].T
    for layer in range(2):
        for g in range(FG):
            pre = jnp.zeros((PIX, C), F32)
            for dy in range(3):
                for dx in range(3):
                    pre += dot(held[dx, g, 16 * dy : 16 * dy + PIX, :], k_ref[layer * 9 + dy * 3 + dx])
            value, slope = gelu_parts(pre)
            slope = jnp.where(keep, slope, 0.0).astype(BF)
            if layer == 0:
                g0_ref[g] = slope
                hold(held, g, jnp.where(keep, value, 0.0))
                a1_ref[:, g * C : (g + 1) * C] = held[1, g, 16 : 16 + C, :].T
            else:
                g1_ref[g] = slope


def forward(corners, pieces, offsets, kernels):
    slots = 16
    half = BOX // 2
    whole = lambda *shape: pl.BlockSpec(shape, lambda i, *_: (0,) * len(shape))
    columns = pl.BlockSpec((C, FG * C), lambda i, *_: (0, i))
    regions = pl.BlockSpec((FG, PIX, C), lambda i, *_: (i, 0, 0))
    return pl.pallas_call(
        forward_kernel,
        name="forward",
        out_shape=[
            jax.ShapeDtypeStruct((C, slots * C), BF),
            jax.ShapeDtypeStruct((C, slots * C), BF),
            jax.ShapeDtypeStruct((slots, PIX, C), BF),
            jax.ShapeDtypeStruct((slots, PIX, C), BF),
            jax.ShapeDtypeStruct((18, C, C), BF),
        ],
        grid_spec=pltpu.PrefetchScalarGridSpec(
            num_scalar_prefetch=1,
            grid=(slots // FG,),
            in_specs=[
                whole(BOX, BOX, C),
                whole(half, BOX, C),
                whole(half, BOX, C),
                whole(BOX, BOX, C),
                whole(half, BOX, C),
                whole(half, BOX, C),
                whole(32, 128),
                whole(18, C, C),
            ],
            out_specs=[columns, columns, regions, regions, whole(18, C, C)],
            scratch_shapes=[
                pltpu.VMEM((2 * BOX, 2 * BOX, C), BF),
                pltpu.VMEM((2, 16, WIN), F32),
                pltpu.VMEM((FG, 16, WIN), F32),
                pltpu.VMEM((FG, PIX, WIN), BF),
                pltpu.VMEM((3, FG, ROWS, C), BF),
            ],
        ),
        cost_estimate=pl.CostEstimate(
            flops=11_300_000_000, bytes_accessed=14 << 20, transcendentals=4_000_000
        ),
    )(corners, *pieces, offsets, kernels)


BG = 4


def top_grad(meta_ref, slot, in_ref, g1_ref, g):
    source = meta_ref[slot]
    live = slot < meta_ref[16]
    grad = in_ref[source].astype(F32) * g1_ref[g].astype(F32)
    return jnp.where(live, grad, 0.0)


def kernel_grad(step, steps, held, a_ref, acc, o_ref):
    @pl.when(step == 0)
    def _():
        acc[...] = jnp.zeros_like(acc)

    for dy in range(3):
        for dx in range(3):
            grads = held[2 - dx, :, 32 - 16 * dy : 32 - 16 * dy + C, :].reshape(BG * C, C)
            acc[dy * 3 + dx] += dot(a_ref[...], grads)

    @pl.when(step == steps - 1)
    def _():
        o_ref[...] = acc[...].astype(BF)


def last_kernel(meta_ref, in_ref, g1_ref, a_ref, o_ref, held, acc):
    step = pl.program_id(0)

    @pl.when(step == 0)
    def _():
        clear_edges(held, BG)

    for g in range(BG):
        hold(held, g, top_grad(meta_ref, step * BG + g, in_ref, g1_ref, g))
    kernel_grad(step, pl.num_programs(0), held, a_ref, acc, o_ref)


def last_grad(meta, incoming, slope1, acts1):
    slots = slope1.shape[0]
    return pl.pallas_call(
        last_kernel,
        name="last_grad",
        out_shape=jax.ShapeDtypeStruct((9, C, C), BF),
        grid_spec=pltpu.PrefetchScalarGridSpec(
            num_scalar_prefetch=1,
            grid=(slots // BG,),
            in_specs=[
                pl.BlockSpec((16, PIX, C), lambda i, *_: (0, 0, 0)),
                pl.BlockSpec((BG, PIX, C), lambda i, *_: (i, 0, 0)),
                pl.BlockSpec((C, BG * C), lambda i, *_: (0, i)),
            ],
            out_specs=pl.BlockSpec((9, C, C), lambda i, *_: (0, 0, 0)),
            scratch_shapes=[pltpu.VMEM((3, BG, ROWS, C), BF), pltpu.VMEM((9, C, C), F32)],
        ),
        cost_estimate=pl.CostEstimate(
            flops=4_800_000_000, bytes_accessed=8 << 20, transcendentals=0
        ),
    )(meta, incoming, slope1, acts1)


def input_grad(held, g, k_ref):
    total = jnp.zeros((PIX, C), F32)
    for dy in range(3):
        for dx in range(3):
            total += dot(
                held[2 - dx, g, 32 - 16 * dy : 32 - 16 * dy + PIX, :],
                k_ref[dy * 3 + dx],
            )
    return total.astype(BF)


def middle_kernel(
    meta_ref, in_ref, g1_ref, g0_ref, k_ref, a_ref, p_ref, o_ref, upper, held, acc
):
    step = pl.program_id(0)

    @pl.when(step == 0)
    def _():
        clear_edges(upper, BG)
        clear_edges(held, BG)

    for g in range(BG):
        hold(upper, g, top_grad(meta_ref, step * BG + g, in_ref, g1_ref, g))
    for g in range(BG):
        grad = input_grad(upper, g, k_ref).astype(F32) * g0_ref[g].astype(F32)
        p_ref[g] = grad.astype(BF)
        hold(held, g, grad)
    kernel_grad(step, pl.num_programs(0), held, a_ref, acc, o_ref)


def middle_grad(meta, incoming, slope1, slope0, kernels, acts0):
    slots = slope1.shape[0]
    return pl.pallas_call(
        middle_kernel,
        name="middle_grad",
        out_shape=[
            jax.ShapeDtypeStruct((slots, PIX, C), BF),
            jax.ShapeDtypeStruct((9, C, C), BF),
        ],
        grid_spec=pltpu.PrefetchScalarGridSpec(
            num_scalar_prefetch=1,
            grid=(slots // BG,),
            in_specs=[
                pl.BlockSpec((16, PIX, C), lambda i, *_: (0, 0, 0)),
                pl.BlockSpec((BG, PIX, C), lambda i, *_: (i, 0, 0)),
                pl.BlockSpec((BG, PIX, C), lambda i, *_: (i, 0, 0)),
                pl.BlockSpec((9, C, C), lambda i, *_: (1, 0, 0)),
                pl.BlockSpec((C, BG * C), lambda i, *_: (0, i)),
            ],
            out_specs=[
                pl.BlockSpec((BG, PIX, C), lambda i, *_: (i, 0, 0)),
                pl.BlockSpec((9, C, C), lambda i, *_: (0, 0, 0)),
            ],
            scratch_shapes=[
                pltpu.VMEM((3, BG, ROWS, C), BF),
                pltpu.VMEM((3, BG, ROWS, C), BF),
                pltpu.VMEM((9, C, C), F32),
            ],
        ),
        cost_estimate=pl.CostEstimate(
            flops=9_000_000_000, bytes_accessed=12 << 20, transcendentals=0
        ),
    )(meta, incoming, slope1, slope0, kernels, acts0)


SG = 4
PART = 4


def spread_kernel(
    corner_ref, p_ref, off_ref, k_ref, tl_ref, tr_ref, bl_ref, br_ref, held, row_w, lanes, total
):
    step = pl.program_id(0)

    @pl.when(step == 0)
    def _():
        clear_edges(held, SG)
        total[...] = jnp.zeros_like(total)
        entry = lax.broadcasted_iota(jnp.int32, (32, C), 0)
        pixel = lax.broadcasted_iota(jnp.int32, (32, C), 1)
        for axis in range(2):
            index = pixel // PITCH if axis == 0 else 16 + (pixel & (PITCH - 1))
            pick = jnp.where(entry == index, 1.0, 0.0).astype(BF)
            lanes[axis] = dot(off_ref[...].astype(BF), pick)

    for g in range(SG):
        hold(held, g, p_ref[g].astype(F32))
    row_at = 4.0 * lax.broadcasted_iota(jnp.int32, (BOX, C), 0).astype(F32)
    col_at = 4.0 * lax.broadcasted_iota(jnp.int32, (SPAN, C), 0).astype(F32)
    grads = [
        jnp.concatenate([input_grad(held, g, k_ref), jnp.zeros((C - PIX, C), BF)], axis=0)
        for g in range(SG)
    ]
    for g in range(SG):
        slot = step * SG + g
        top = corner_ref[slot]
        left = pl.multiple_of(corner_ref[16 + slot] // 16 * 16, 16)
        row_w[g] = tent(row_at, lanes[0, pl.ds(slot, 1), :])
        col_w = tent(col_at, lanes[1, pl.ds(slot, 1), :])
        for at in range(0, BOX, PART):
            weight = jnp.concatenate(
                [(row_w[g, p : p + 1, :] * col_w).astype(BF) for p in range(at, at + PART)], axis=0
            )
            total[pl.ds(top + at, PART), pl.ds(left, SPAN), :] += dot(weight, grads[g]).reshape(
                PART, SPAN, C
            )

    @pl.when(step == pl.num_programs(0) - 1)
    def _():
        tl_ref[...] = total[0:BOX, 0:BOX, :]
        tr_ref[...] = total[0:BOX, BOX : 2 * BOX, :].astype(BF)
        bl_ref[...] = total[BOX : 2 * BOX, 0:BOX, :].astype(BF)
        br_ref[...] = total[BOX : 2 * BOX, BOX : 2 * BOX, :].astype(BF)


def spread(corners, inner, offsets, kernels):
    slots = inner.shape[0]
    whole = lambda *shape: pl.BlockSpec(shape, lambda i, *_: (0,) * len(shape))
    piece = lambda kind: jax.ShapeDtypeStruct((BOX, BOX, C), kind)
    return pl.pallas_call(
        spread_kernel,
        name="spread",
        out_shape=[piece(F32), piece(BF), piece(BF), piece(BF)],
        grid_spec=pltpu.PrefetchScalarGridSpec(
            num_scalar_prefetch=1,
            grid=(slots // SG,),
            in_specs=[
                pl.BlockSpec((SG, PIX, C), lambda i, *_: (i, 0, 0)),
                whole(16, 32),
                whole(9, C, C),
            ],
            out_specs=[whole(BOX, BOX, C)] * 4,
            scratch_shapes=[
                pltpu.VMEM((3, SG, ROWS, C), BF),
                pltpu.VMEM((SG, BOX, C), F32),
                pltpu.VMEM((2, 16, C), F32),
                pltpu.VMEM((2 * BOX, 2 * BOX, C), F32),
            ],
        ),
        cost_estimate=pl.CostEstimate(
            flops=7_000_000_000, bytes_accessed=6 << 20, transcendentals=0
        ),
    )(corners, inner, offsets, kernels)


def swap_cores(x):
    return lax.ppermute(x, "ha", [(i, i ^ 1) for i in range(lax.axis_size("ha"))])


def pick_layer(index, first, second):
    return jnp.where(index == 0, first, second)


def local(features, counts, owner_perm, corners, offsets, kernels, cotangent):
    peers = lax.axis_size("wa")
    core = lax.axis_index("ha") % 2
    rows = BOX // 2
    cut = lambda x: (x[:rows], x[rows:])
    row_counts = lax.all_to_all(
        jnp.broadcast_to(counts[None], (peers, 1, 1)), "wa", 0, 0, tiled=True
    ).reshape(peers)
    features, row_counts = lax.optimization_barrier((features, row_counts))
    from_right = [shifted(piece, "wa", -1) for piece in cut(features)]
    below = shifted(features, "ha", -1)
    outgoing, meta = route(row_counts, owner_perm, cotangent)
    incoming = lax.all_to_all(
        outgoing.reshape(peers, PIX, C), "wa", split_axis=0, concat_axis=0, tiled=True
    )
    corner = [shifted(piece, "ha", -1) for piece in from_right]
    pieces = (features, *from_right, below, *corner)
    places = jnp.concatenate(
        [offsets[:, :SIDE], offsets[:, SIDE:] + (corners[:, 1:2] % 16) * 4], axis=1
    ).astype(F32)
    pad = lambda x: jnp.pad(x, ((0, 0), (0, 2)), constant_values=-1000.0)
    places = jnp.concatenate([pad(places[:, :SIDE]), pad(places[:, SIDE:])], axis=1)
    place_cols = jnp.pad(places.T, ((0, 0), (0, 112)))
    corners = corners.T.reshape(-1)
    acts0, acts1, slope0, slope1, turned = forward(
        corners, pieces, place_cols, kernels.reshape(18, C, C)
    )
    grad1 = last_grad(meta, incoming, slope1, acts1)
    inner, grad0 = middle_grad(meta, incoming, slope1, slope0, turned, acts0)
    mine = swap_cores(pick_layer(core, grad1, grad0)).astype(F32)
    mine = (mine + pick_layer(core, grad0, grad1).astype(F32)).astype(BF)
    parts = lax.all_to_all(mine.reshape(peers, -1, C), "wa", 0, 0, tiled=True)
    tile, right, lower, corner = spread(corners, inner, places, turned)
    parts, tile, right, lower, corner = lax.optimization_barrier(
        (parts, tile, right, lower, corner)
    )
    part = jnp.sum(parts.astype(F32), axis=0).astype(BF)
    count = lax.axis_size("ha")
    total = part.astype(F32)
    for hop in range(2, count, 2):
        moved = lax.ppermute(part, "ha", [(i, (i + hop) % count) for i in range(count)])
        total = total + moved.astype(F32)
    whole = jnp.broadcast_to(total.astype(BF)[None], (peers, *total.shape))
    mine = lax.all_to_all(whole, "wa", 0, 0, tiled=True).reshape(9, C, C)
    sides = []
    for own, piece in zip(cut(right), cut(corner)):
        moved = shifted(piece, "ha", 1)
        sides.append(shifted((own.astype(F32) + moved.astype(F32)).astype(BF), "wa", 1))
    from_above = shifted(lower, "ha", 1)
    mine, from_above, *sides = lax.optimization_barrier((mine, from_above, *sides))
    tile = tile + from_above.astype(F32) + jnp.concatenate(sides).astype(F32)
    other = swap_cores(mine)
    grads = jnp.stack([pick_layer(core, mine, other), pick_layer(core, other, mine)]).astype(F32)
    return (tile, grads.reshape(2, 3, 3, C, C))


def solution(mesh):
    in_specs = (
        P("ha", "wa", None),
        P("ha", "wa"),
        P("ha", None),
        P(("ha", "wa"), None),
        P(("ha", "wa"), None),
        P(),
        P(("ha", "wa"), None, None, None),
    )
    out_specs = (P("ha", "wa", None), P())
    return jax.shard_map(local, mesh=mesh, in_specs=in_specs, out_specs=out_specs, check_vma=False)
```

time: 234 us -> 180 us (0.77)
  blocking collectives: 25 us -> 0 us
  waiting for transfers between devices: 10.8 us -> 33.2 us
  Pallas kernels: 84.3 us -> 64.3 us
  starting transfers between devices: 77.4 us -> 60.6 us
  other arithmetic: 17.8 us -> 9.77 us
  local copies, waits for them, and re-layouts: 13.1 us -> 7.53 us
    all_to_all x1 -> x0, blocking collectives: 25 us -> none  [sum_everywhere(): lax.all_to_all(half.reshape(peers, rows // peers, C), 'wa', 0, 0, tiled=T...]
    ppermute x18 -> x10, starting transfers between devices: 45.2 us -> 26.5 us  [shifted(): lax.ppermute(value, axis, [(source, source + steps) for source in range(f...]
    pallas_call x1, Pallas kernels: 24 us -> 12.8 us  [spread(): pl.pallas_call(spread_kernel, name='spread', out_shape=[piece(F32), piece...]
    all_to_all x2 -> x3, starting transfers between devices: 11.1 us -> 22.3 us  [the longest x1 11.9 us: local(): parts = lax.all_to_all(mine.reshape(peers, -1, C), 'wa', 0, 0, tiled=True)]
    ppermute x18 -> x10, waiting for transfers between devices: 5.72 us -> 15.6 us  [shifted(): lax.ppermute(value, axis, [(source, source + steps) for source in range(f...]
    pallas_call x1, Pallas kernels: 8.81 us -> 2.69 us  [route(): pl.pallas_call(route_kernel, name='route', out_shape=[jax.ShapeDtypeStruc...]
    all_to_all x2 -> x3, waiting for transfers between devices: 0.01 us -> 5.47 us  [the longest x1 5.47 us: local(): parts = lax.all_to_all(mine.reshape(peers, -1, C), 'wa', 0, 0, tiled=True)]
    all_to_all x1, starting transfers between devices: 12.9 us -> 7.57 us  [local(): lax.all_to_all(jnp.broadcast_to(counts[None], (peers, 1, 1)), 'wa', 0, 0,...]
  transfers between devices with their start and end apart: 26 -> 19, of which waited for: 6 -> 12; matrix products, arithmetic and copies ran while one was open for 10% -> 4% of each run, Pallas kernels for 24% -> 21%
where the time goes in v2:
time: 180 us; the launch traced here: 177 us
  Pallas kernels  64.3 us (36%)
  starting transfers between devices  60.6 us (34%)
  waiting for transfers between devices  33.2 us (18%)
  other arithmetic  9.77 us (5%)
  local copies, waits for them, and re-layouts  7.53 us (4%)
    ppermute x10, starting transfers between devices, shifted(): lax.ppermute(value, axis, [(source, source + steps) for source in range(f...  26.5 us
    pallas_call x1, Pallas kernels, forward(): pl.pallas_call(forward_kernel, name='forward', out_shape=[jax.ShapeDtypeS...  21.2 us
    pallas_call x1, Pallas kernels, middle_grad(): pl.pallas_call(middle_kernel, name='middle_grad', out_shape=[jax.ShapeDty...  16.9 us
    ppermute x10, waiting for transfers between devices, shifted(): lax.ppermute(value, axis, [(source, source + steps) for source in range(f...  15.6 us
    pallas_call x1, Pallas kernels, spread(): pl.pallas_call(spread_kernel, name='spread', out_shape=[piece(F32), piece...  12.8 us
    all_to_all x1, starting transfers between devices, local(): parts = lax.all_to_all(mine.reshape(peers, -1, C), 'wa', 0, 0, tiled=True)  11.9 us
    pallas_call x1, Pallas kernels, last_grad(): pl.pallas_call(last_kernel, name='last_grad', out_shape=jax.ShapeDtypeStr...  10.7 us
    all_to_all x1, starting transfers between devices, local(): lax.all_to_all(jnp.broadcast_to(counts[None], (peers, 1, 1)), 'wa', 0, 0,...  7.57 us
  transfers between devices with their start and end apart: 19, of which 12 were waited for; matrix products, arithmetic and copies ran while one was open for 4% of the time, Pallas kernels for 21%

profile of v2, /device:TPU:1, one launch (start us, length us, event | category | flops | bytes accessed | tf_op | source)
XLA Modules:
  0.0 177.0 jit_solution(10694548956862429262)
XLA Ops:
  1.9 7.6 %all-to-all-start = ((s32[16,1,1]{2,1,0:T(1,128)}), s32[16,1,1]{2,1,0:T(1,128)S(1)}, u32[]{:S(2)}, u32[]{:S(2)}) async-start(s32[16,1,1]{2,1,0:T(1,128)} %broadcast_in_dim.7), calls=%async_computation | async-start | bytes 16384 | tf_op jit(solution)/shard_map/all_to_all | solution.py:417
  12.5 3.4 %all-to-all-done = s32[16,1,1]{2,1,0:T(1,128)S(1)} async-done(((s32[16,1,1]{2,1,0:T(1,128)}), s32[16,1,1]{2,1,0:T(1,128)S(1)}, u32[]{:S(2)}, u32[]{:S(2)}) %all-to-all-start) | async-done | bytes 96 | tf_op jit(solution)/shard_map/all_to_all | solution.py:417
  16.8 4.0 %collective-permute-start.2 = (bf16[32,32,256]{2,1,0:T(8,128)(2,1)S(1)}, bf16[32,32,256]{2,1,0:T(8,128)(2,1)S(1)}, u32[]{:S(2)}, u32[]{:S(2)}) collective-permute-start(bf16[32,32,256]{2,1,0:T(8,128)(2,1)S(1)} %copy-done.5), channel_id=1, source_target_pairs={{16,0},{32,16},{48,32},{64,48},{80,64},{96,80},{112,96},{17,1},{33... | collective-permute-start | bytes 1572872 | tf_op jit(solution)/shard_map/ppermute | solution.py:25
  23.4 2.7 %route.1 = (bf16[16,14,16,256]{3,2,1,0:T(8,128)(2,1)}, s32[17]{0:T(128)}) custom-call(s32[16]{0:T(128)} %reduce.1.count_ref, s32[1,16]{1,0:T(1,128)} %perm_ref.1, bf16[8,14,14,256]{3,2,1,0:T(8,128)(2,1)} %copy.13.x_ref), custom_call_target="tpu_custom_call" | custom-call | bytes 4194304 | tf_op jit(solution)/shard_map/route/pallas_call | solution.py:85
  26.2 6.6 %all-to-all-start.1 = ((bf16[16,224,256]{2,1,0:T(8,128)(2,1)}), bf16[16,224,256]{2,1,0:T(8,128)(2,1)S(1)}, u32[]{:S(2)}, u32[]{:S(2)}) async-start(bf16[16,224,256]{2,1,0:T(8,128)(2,1)} %bitcast.17), calls=%async_computation.1 | async-start | bytes 3670016 | tf_op jit(solution)/shard_map/all_to_all | solution.py:424
  39.6 3.0 %collective-permute-done.4.br1_ref = bf16[16,32,256]{2,1,0:T(8,128)(2,1)S(1)} collective-permute-done((bf16[16,32,256]{2,1,0:T(8,128)(2,1)}, bf16[16,32,256]{2,1,0:T(8,128)(2,1)S(1)}, u32[]{:S(2)}, u32[]{:S(2)}) %collective-permute-start.4) | collective-permute-done | bytes 262176 | tf_op jit(solution)/shard_map/ppermute | solution.py:25
  42.5 3.0 %collective-permute-done.3.br0_ref = bf16[16,32,256]{2,1,0:T(8,128)(2,1)} collective-permute-done((bf16[16,32,256]{2,1,0:T(8,128)(2,1)}, bf16[16,32,256]{2,1,0:T(8,128)(2,1)}, u32[]{:S(2)}, u32[]{:S(2)}) %collective-permute-start.3) | collective-permute-done | bytes 262176 | tf_op jit(solution)/shard_map/ppermute | solution.py:25
  46.3 21.2 %forward.1 = (bf16[256,4096]{1,0:T(8,128)(2,1)}, bf16[256,4096]{1,0:T(8,128)(2,1)}, bf16[16,224,256]{2,1,0:T(8,128)(2,1)}, bf16[16,224,256]{2,1,0:T(8,128)(2,1)}, bf16[18,256,256]{2,1,0:T(8,128)(2,1)}) custom-call(s32[32]{0:T(128)} %reshape.33.corner_ref, bf16[32,32,256]{2,1,0:T(8,128)(2,1)} %tl_ref, bf16[16,32,256]{2,1,0:T(8,128)(2,1)} %collective-permute-done.tr0_ref, ...), custom_call_target="tpu_custom_call" | custom-call | flops 11299999744 | bytes 14680064 | tf_op jit(solution)/shard_map/forward/pallas_call | solution.py:161
  68.8 10.7 %last_grad.1 = bf16[9,256,256]{2,1,0:T(8,128)(2,1)} custom-call(s32[17]{0:T(128)} %get-tuple-element.27.meta_ref, bf16[16,224,256]{2,1,0:T(8,128)(2,1)} %copy-done.2, bf16[16,224,256]{2,1,0:T(8,128)(2,1)} %get-tuple-element.30.g1_ref, bf16[256,4096]{1,0:T(8,128)(2,1)} %get-tuple-element.31.a_ref), custom_call_target="tpu_custom_call" | custom-call | flops 4800000000 | bytes 8388608 | tf_op jit(solution)/shard_map/last_grad/pallas_call | solution.py:238
  79.5 16.9 %middle_grad.1 = (bf16[16,224,256]{2,1,0:T(8,128)(2,1)}, bf16[9,256,256]{2,1,0:T(8,128)(2,1)}) custom-call(s32[17]{0:T(128)} %get-tuple-element.27.meta_ref, bf16[16,224,256]{2,1,0:T(8,128)(2,1)} %copy-done.2, bf16[16,224,256]{2,1,0:T(8,128)(2,1)} %get-tuple-element.30.g1_ref, bf16[16,224,256]{2,1,0:T(8,128)(2,1)} %get-tuple-element.32.g0_ref, ...), custom_call_target="tpu_custom_call" | custom-call | flops 8999999488 | bytes 12582912 | tf_op jit(solution)/shard_map/middle_grad/pallas_call | solution.py:291
  98.0 2.8 %collective-permute-done.5 = bf16[9,256,256]{2,1,0:T(8,128)(2,1)S(1)} collective-permute-done((bf16[9,256,256]{2,1,0:T(8,128)(2,1)S(1)}, bf16[9,256,256]{2,1,0:T(8,128)(2,1)S(1)}, u32[]{:S(2)}, u32[]{:S(2)}) %collective-permute-start.5) | collective-permute-done | bytes 1179680 | tf_op jit(solution)/shard_map/ppermute | solution.py:405
  102.4 11.9 %all-to-all-start.2 = ((bf16[16,144,256]{2,1,0:T(8,128)(2,1)}), bf16[16,144,256]{2,1,0:T(8,128)(2,1)S(1)}, u32[]{:S(2)}, u32[]{:S(2)}) async-start(bf16[16,144,256]{2,1,0:T(8,128)(2,1)} %bitcast.6), calls=%async_computation.2 | async-start | bytes 2359296 | tf_op jit(solution)/shard_map/all_to_all | solution.py:443
  114.9 12.8 %spread.1 = (f32[32,32,256]{2,1,0:T(8,128)}, bf16[32,32,256]{2,1,0:T(8,128)(2,1)}, bf16[32,32,256]{2,1,0:T(8,128)(2,1)}, bf16[32,32,256]{2,1,0:T(8,128)(2,1)}) custom-call(s32[32]{0:T(128)} %reshape.33.corner_ref, bf16[16,224,256]{2,1,0:T(8,128)(2,1)} %get-tuple-element.36.p_ref, f32[16,32]{1,0:T(8,128)} %select_maximum_fusion.off_ref, ...), custom_call_target="tpu_custom_call" | custom-call | flops 7000000000 | bytes 6291456 | tf_op jit(solution)/shard_map/spread/pallas_call | solution.py:378
  127.7 5.5 %all-to-all-done.2 = bf16[16,144,256]{2,1,0:T(8,128)(2,1)S(1)} async-done(((bf16[16,144,256]{2,1,0:T(8,128)(2,1)}), bf16[16,144,256]{2,1,0:T(8,128)(2,1)S(1)}, u32[]{:S(2)}, u32[]{:S(2)}) %all-to-all-start.2) | async-done | bytes 1179680 | tf_op jit(solution)/shard_map/all_to_all | solution.py:443
  133.4 3.4 %collective-permute-start.7 = (bf16[144,256]{1,0:T(8,128)(2,1)S(1)}, bf16[144,256]{1,0:T(8,128)(2,1)S(1)}, u32[]{:S(2)}, u32[]{:S(2)}) collective-permute-start(bf16[144,256]{1,0:T(8,128)(2,1)S(1)} %reduce_sum.12), channel_id=1, source_target_pairs={{0,64},{16,80},{32,96},{48,112},{64,0},{80,16},{96,32},{112,48},{1... | collective-permute-start | bytes 221192 | tf_op jit(solution)/shard_map/ppermute | solution.py:452
  138.5 3.2 %collective-permute-done.6 = bf16[144,256]{1,0:T(8,128)(2,1)S(1)} collective-permute-done((bf16[144,256]{1,0:T(8,128)(2,1)S(1)}, bf16[144,256]{1,0:T(8,128)(2,1)S(1)}, u32[]{:S(2)}, u32[]{:S(2)}) %collective-permute-start.6) | collective-permute-done | bytes 73760 | tf_op jit(solution)/shard_map/ppermute | solution.py:452
  142.9 3.8 %all-to-all-start.3 = ((bf16[16,144,256]{2,1,0:T(8,128)(2,1)}), bf16[16,144,256]{2,1,0:T(8,128)(2,1)S(1)}, u32[]{:S(2)}, u32[]{:S(2)}) async-start(bf16[16,144,256]{2,1,0:T(8,128)(2,1)} %broadcast_in_dim.16), calls=%async_computation.3 | async-start | bytes 2359296 | tf_op jit(solution)/shard_map/all_to_all | solution.py:455
  146.8 4.3 %collective-permute-start.12 = (bf16[16,32,256]{2,1,0:T(8,128)(2,1)S(1)}, bf16[16,32,256]{2,1,0:T(8,128)(2,1)S(1)}, u32[]{:S(2)}, u32[]{:S(2)}) collective-permute-start(bf16[16,32,256]{2,1,0:T(8,128)(2,1)S(1)} %get-tuple-element.54), channel_id=1, source_target_pairs={{0,16},{16,32},{32,48},{48,64},{64,80},{80,96},{96,112},{1,17},{17... | collective-permute-start | bytes 786440 | tf_op jit(solution)/shard_map/ppermute | solution.py:25
  153.0 2.8 %collective-permute-start.9 = (bf16[32,32,256]{2,1,0:T(8,128)(2,1)}, bf16[32,32,256]{2,1,0:T(8,128)(2,1)S(1)}, u32[]{:S(2)}, u32[]{:S(2)}) collective-permute-start(bf16[32,32,256]{2,1,0:T(8,128)(2,1)} %get-tuple-element.43), channel_id=1, source_target_pairs={{0,16},{16,32},{32,48},{48,64},{64,80},{80,96},{96,112},{1,17},{17... | collective-permute-start | bytes 1572872 | tf_op jit(solution)/shard_map/ppermute | solution.py:25
  157.3 3.4 %collective-permute-start.13 = (bf16[16,32,256]{2,1,0:T(8,128)(2,1)S(1)}, bf16[16,32,256]{2,1,0:T(8,128)(2,1)S(1)}, u32[]{:S(2)}, u32[]{:S(2)}) collective-permute-start(bf16[16,32,256]{2,1,0:T(8,128)(2,1)S(1)} %get-tuple-element.52), channel_id=1, source_target_pairs={{0,1},{1,2},{2,3},{3,4},{4,5},{5,6},{6,7},{7,8},{8,9},{9,10},{10,1... | collective-permute-start | bytes 786440 | tf_op jit(solution)/shard_map/ppermute | solution.py:25
  160.8 3.1 %collective-permute-start.11 = (bf16[16,32,256]{2,1,0:T(8,128)(2,1)S(1)}, bf16[16,32,256]{2,1,0:T(8,128)(2,1)S(1)}, u32[]{:S(2)}, u32[]{:S(2)}) collective-permute-start(bf16[16,32,256]{2,1,0:T(8,128)(2,1)S(1)} %get-tuple-element.53), channel_id=1, source_target_pairs={{0,1},{1,2},{2,3},{3,4},{4,5},{5,6},{6,7},{7,8},{8,9},{9,10},{10,1... | collective-permute-start | bytes 786440 | tf_op jit(solution)/shard_map/ppermute | solution.py:25
  163.9 3.0 %collective-permute-done.13 = bf16[16,32,256]{2,1,0:T(8,128)(2,1)S(1)} collective-permute-done((bf16[16,32,256]{2,1,0:T(8,128)(2,1)S(1)}, bf16[16,32,256]{2,1,0:T(8,128)(2,1)S(1)}, u32[]{:S(2)}, u32[]{:S(2)}) %collective-permute-start.13) | collective-permute-done | bytes 262176 | tf_op jit(solution)/shard_map/ppermute | solution.py:25
  166.9 4.6 %collective-permute-done.11 = bf16[16,32,256]{2,1,0:T(8,128)(2,1)S(1)} collective-permute-done((bf16[16,32,256]{2,1,0:T(8,128)(2,1)S(1)}, bf16[16,32,256]{2,1,0:T(8,128)(2,1)S(1)}, u32[]{:S(2)}, u32[]{:S(2)}) %collective-permute-start.11) | collective-permute-done | bytes 262176 | tf_op jit(solution)/shard_map/ppermute | solution.py:25
  174.5 2.5 %maximum_convert_fusion = f32[2,3,3,256,256]{4,3,2,1,0:T(8,128)} fusion(bf16[1,3,3,256,256]{4,3,2,1,0:T(8,128)(2,1)S(1)} %bitcast.14, bf16[1,3,3,256,256]{4,3,2,1,0:T(8,128)(2,1)S(1)} %bitcast.13), kind=kLoop, calls=%fused_computation | loop fusion | flops 2359296 | bytes 7077888 | tf_op jit(solution)/shard_map/convert_element_type | solution.py:464
  (67 shorter events, 29.3 us)
Async XLA Ops:
  0.6 16.2 %copy-start.5 = (bf16[32,32,256]{2,1,0:T(8,128)(2,1)S(1)}, bf16[32,32,256]{2,1,0:T(8,128)(2,1)}, u32[]{:S(2)}) copy-start(bf16[32,32,256]{2,1,0:T(8,128)(2,1)} %tl_ref) | copy-start | bytes 1572868
  1.9 13.9 %all-to-all-start = ((s32[16,1,1]{2,1,0:T(1,128)}), s32[16,1,1]{2,1,0:T(1,128)S(1)}, u32[]{:S(2)}, u32[]{:S(2)}) async-start(s32[16,1,1]{2,1,0:T(1,128)} %broadcast_in_dim.7), calls=%async_computation | async-start | bytes 16384 | tf_op jit(solution)/shard_map/all_to_all | solution.py:417
  16.8 28.7 %collective-permute-start.2 = (bf16[32,32,256]{2,1,0:T(8,128)(2,1)S(1)}, bf16[32,32,256]{2,1,0:T(8,128)(2,1)S(1)}, u32[]{:S(2)}, u32[]{:S(2)}) collective-permute-start(bf16[32,32,256]{2,1,0:T(8,128)(2,1)S(1)} %copy-done.5), channel_id=1, source_target_pairs={{16,0},{32,16},{48,32},{64,48},{80,64},{96,80},{112,96},{17,1},{33... | collective-permute-start | bytes 1572872 | tf_op jit(solution)/shard_map/ppermute | solution.py:25
  20.8 12.9 %collective-permute-start.1 = (bf16[16,32,256]{2,1,0:T(8,128)(2,1)S(1)}, bf16[16,32,256]{2,1,0:T(8,128)(2,1)}, u32[]{:S(2)}, u32[]{:S(2)}) collective-permute-start(bf16[16,32,256]{2,1,0:T(8,128)(2,1)S(1)} %get-tuple-element.56), channel_id=1, source_target_pairs={{1,0},{2,1},{3,2},{4,3},{5,4},{6,5},{7,6},{8,7},{9,8},{10,9},{11,1... | collective-permute-start | bytes 786440 | tf_op jit(solution)/shard_map/ppermute | solution.py:25
  22.1 14.3 %collective-permute-start = (bf16[16,32,256]{2,1,0:T(8,128)(2,1)S(1)}, bf16[16,32,256]{2,1,0:T(8,128)(2,1)}, u32[]{:S(2)}, u32[]{:S(2)}) collective-permute-start(bf16[16,32,256]{2,1,0:T(8,128)(2,1)S(1)} %get-tuple-element.57), channel_id=1, source_target_pairs={{1,0},{2,1},{3,2},{4,3},{5,4},{6,5},{7,6},{8,7},{9,8},{10,9},{11,1... | collective-permute-start | bytes 786440 | tf_op jit(solution)/shard_map/ppermute | solution.py:25
  26.2 12.6 %copy-start.8 = (pred[16]{0:T(512)(128)(4,1)S(1)}, pred[16]{0:T(512)(128)(4,1)}, u32[]{:S(2)}) copy-start(pred[16]{0:T(512)(128)(4,1)} %constant.38.clone.1) | copy-start | bytes 52
  26.2 41.3 %all-to-all-start.1 = ((bf16[16,224,256]{2,1,0:T(8,128)(2,1)}), bf16[16,224,256]{2,1,0:T(8,128)(2,1)S(1)}, u32[]{:S(2)}, u32[]{:S(2)}) async-start(bf16[16,224,256]{2,1,0:T(8,128)(2,1)} %bitcast.17), calls=%async_computation.1 | async-start | bytes 3670016 | tf_op jit(solution)/shard_map/all_to_all | solution.py:424
  33.7 8.8 %collective-permute-start.4 = (bf16[16,32,256]{2,1,0:T(8,128)(2,1)}, bf16[16,32,256]{2,1,0:T(8,128)(2,1)S(1)}, u32[]{:S(2)}, u32[]{:S(2)}) collective-permute-start(bf16[16,32,256]{2,1,0:T(8,128)(2,1)} %collective-permute-done.1.tr1_ref), channel_id=1, source_target_pairs={{16,0},{32,16},{48,32},{64,48},{80,64},{96,80},{112,96},{17,1},{33... | collective-permute-start | bytes 786440 | tf_op jit(solution)/shard_map/ppermute | solution.py:25
  36.5 9.0 %collective-permute-start.3 = (bf16[16,32,256]{2,1,0:T(8,128)(2,1)}, bf16[16,32,256]{2,1,0:T(8,128)(2,1)}, u32[]{:S(2)}, u32[]{:S(2)}) collective-permute-start(bf16[16,32,256]{2,1,0:T(8,128)(2,1)} %collective-permute-done.tr0_ref), channel_id=1, source_target_pairs={{16,0},{32,16},{48,32},{64,48},{80,64},{96,80},{112,96},{17,1},{33... | collective-permute-start | bytes 786440 | tf_op jit(solution)/shard_map/ppermute | solution.py:25
  79.5 16.9 %copy-start = (bf16[9,256,256]{2,1,0:T(8,128)(2,1)S(1)}, bf16[9,256,256]{2,1,0:T(8,128)(2,1)}, u32[]{:S(2)}) copy-start(bf16[9,256,256]{2,1,0:T(8,128)(2,1)} %last_grad.1) | copy-start | bytes 3538948
  97.9 2.9 %collective-permute-start.5 = (bf16[9,256,256]{2,1,0:T(8,128)(2,1)S(1)}, bf16[9,256,256]{2,1,0:T(8,128)(2,1)S(1)}, u32[]{:S(2)}, u32[]{:S(2)}) collective-permute-start(bf16[9,256,256]{2,1,0:T(8,128)(2,1)S(1)} %broadcast_select_fusion.2), channel_id=1, source_target_pairs={{0,16},{16,0},{32,48},{48,32},{64,80},{80,64},{96,112},{112,96},{1... | collective-permute-start | bytes 3538952 | tf_op jit(solution)/shard_map/ppermute | solution.py:405
  102.4 30.8 %all-to-all-start.2 = ((bf16[16,144,256]{2,1,0:T(8,128)(2,1)}), bf16[16,144,256]{2,1,0:T(8,128)(2,1)S(1)}, u32[]{:S(2)}, u32[]{:S(2)}) async-start(bf16[16,144,256]{2,1,0:T(8,128)(2,1)} %bitcast.6), calls=%async_computation.2 | async-start | bytes 2359296 | tf_op jit(solution)/shard_map/all_to_all | solution.py:443
  133.3 4.1 %collective-permute-start.8 = (bf16[144,256]{1,0:T(8,128)(2,1)S(1)}, bf16[144,256]{1,0:T(8,128)(2,1)S(1)}, u32[]{:S(2)}, u32[]{:S(2)}) collective-permute-start(bf16[144,256]{1,0:T(8,128)(2,1)S(1)} %reduce_sum.12), channel_id=1, source_target_pairs={{0,96},{16,112},{32,0},{48,16},{64,32},{80,48},{96,64},{112,80},{1... | collective-permute-start | bytes 221192 | tf_op jit(solution)/shard_map/ppermute | solution.py:452
  133.4 5.1 %collective-permute-start.7 = (bf16[144,256]{1,0:T(8,128)(2,1)S(1)}, bf16[144,256]{1,0:T(8,128)(2,1)S(1)}, u32[]{:S(2)}, u32[]{:S(2)}) collective-permute-start(bf16[144,256]{1,0:T(8,128)(2,1)S(1)} %reduce_sum.12), channel_id=1, source_target_pairs={{0,64},{16,80},{32,96},{48,112},{64,0},{80,16},{96,32},{112,48},{1... | collective-permute-start | bytes 221192 | tf_op jit(solution)/shard_map/ppermute | solution.py:452
  136.7 5.0 %collective-permute-start.6 = (bf16[144,256]{1,0:T(8,128)(2,1)S(1)}, bf16[144,256]{1,0:T(8,128)(2,1)S(1)}, u32[]{:S(2)}, u32[]{:S(2)}) collective-permute-start(bf16[144,256]{1,0:T(8,128)(2,1)S(1)} %reduce_sum.12), channel_id=1, source_target_pairs={{0,32},{16,48},{32,64},{48,80},{64,96},{80,112},{96,0},{112,16},{1... | collective-permute-start | bytes 221192 | tf_op jit(solution)/shard_map/ppermute | solution.py:452
  142.9 14.3 %copy-start.4 = (bf16[32,32,256]{2,1,0:T(8,128)(2,1)S(1)}, bf16[32,32,256]{2,1,0:T(8,128)(2,1)}, u32[]{:S(2)}) copy-start(bf16[32,32,256]{2,1,0:T(8,128)(2,1)} %get-tuple-element.44) | copy-start | bytes 1572868
  142.9 28.7 %all-to-all-start.3 = ((bf16[16,144,256]{2,1,0:T(8,128)(2,1)}), bf16[16,144,256]{2,1,0:T(8,128)(2,1)S(1)}, u32[]{:S(2)}, u32[]{:S(2)}) async-start(bf16[16,144,256]{2,1,0:T(8,128)(2,1)} %broadcast_in_dim.16), calls=%async_computation.3 | async-start | bytes 2359296 | tf_op jit(solution)/shard_map/all_to_all | solution.py:455
  146.7 24.8 %copy-start.3 = (f32[32,32,256]{2,1,0:T(8,128)S(1)}, f32[32,32,256]{2,1,0:T(8,128)}, u32[]{:S(2)}) copy-start(f32[32,32,256]{2,1,0:T(8,128)} %get-tuple-element.41) | copy-start | bytes 3145732
  146.8 9.0 %collective-permute-start.12 = (bf16[16,32,256]{2,1,0:T(8,128)(2,1)S(1)}, bf16[16,32,256]{2,1,0:T(8,128)(2,1)S(1)}, u32[]{:S(2)}, u32[]{:S(2)}) collective-permute-start(bf16[16,32,256]{2,1,0:T(8,128)(2,1)S(1)} %get-tuple-element.54), channel_id=1, source_target_pairs={{0,16},{16,32},{32,48},{48,64},{64,80},{80,96},{96,112},{1,17},{17... | collective-permute-start | bytes 786440 | tf_op jit(solution)/shard_map/ppermute | solution.py:25
  151.0 6.1 %collective-permute-start.10 = (bf16[16,32,256]{2,1,0:T(8,128)(2,1)S(1)}, bf16[16,32,256]{2,1,0:T(8,128)(2,1)S(1)}, u32[]{:S(2)}, u32[]{:S(2)}) collective-permute-start(bf16[16,32,256]{2,1,0:T(8,128)(2,1)S(1)} %get-tuple-element.55), channel_id=1, source_target_pairs={{0,16},{16,32},{32,48},{48,64},{64,80},{80,96},{96,112},{1,17},{17... | collective-permute-start | bytes 786440 | tf_op jit(solution)/shard_map/ppermute | solution.py:25
  153.0 10.9 %collective-permute-start.9 = (bf16[32,32,256]{2,1,0:T(8,128)(2,1)}, bf16[32,32,256]{2,1,0:T(8,128)(2,1)S(1)}, u32[]{:S(2)}, u32[]{:S(2)}) collective-permute-start(bf16[32,32,256]{2,1,0:T(8,128)(2,1)} %get-tuple-element.43), channel_id=1, source_target_pairs={{0,16},{16,32},{32,48},{48,64},{64,80},{80,96},{96,112},{1,17},{17... | collective-permute-start | bytes 1572872 | tf_op jit(solution)/shard_map/ppermute | solution.py:25
  157.3 9.5 %collective-permute-start.13 = (bf16[16,32,256]{2,1,0:T(8,128)(2,1)S(1)}, bf16[16,32,256]{2,1,0:T(8,128)(2,1)S(1)}, u32[]{:S(2)}, u32[]{:S(2)}) collective-permute-start(bf16[16,32,256]{2,1,0:T(8,128)(2,1)S(1)} %get-tuple-element.52), channel_id=1, source_target_pairs={{0,1},{1,2},{2,3},{3,4},{4,5},{5,6},{6,7},{7,8},{8,9},{9,10},{10,1... | collective-permute-start | bytes 786440 | tf_op jit(solution)/shard_map/ppermute | solution.py:25
  160.8 10.7 %collective-permute-start.11 = (bf16[16,32,256]{2,1,0:T(8,128)(2,1)S(1)}, bf16[16,32,256]{2,1,0:T(8,128)(2,1)S(1)}, u32[]{:S(2)}, u32[]{:S(2)}) collective-permute-start(bf16[16,32,256]{2,1,0:T(8,128)(2,1)S(1)} %get-tuple-element.53), channel_id=1, source_target_pairs={{0,1},{1,2},{2,3},{3,4},{4,5},{5,6},{6,7},{7,8},{8,9},{9,10},{10,1... | collective-permute-start | bytes 786440 | tf_op jit(solution)/shard_map/ppermute | solution.py:25
  171.5 2.8 %collective-permute-start.14 = (bf16[9,256,256]{2,1,0:T(8,128)(2,1)S(1)}, bf16[9,256,256]{2,1,0:T(8,128)(2,1)S(1)}, u32[]{:S(2)}, u32[]{:S(2)}) collective-permute-start(bf16[9,256,256]{2,1,0:T(8,128)(2,1)S(1)} %bitcast.15), channel_id=1, source_target_pairs={{0,16},{16,0},{32,48},{48,32},{64,80},{80,64},{96,112},{112,96},{1... | collective-permute-start | bytes 3538952 | tf_op jit(solution)/shard_map/ppermute | solution.py:405
  (7 other events, 26.7 us)

commit v3 on v2

--- a/solution.py
+++ b/solution.py
@@ -1,5 +1,3 @@
-import functools
-
 import jax
 import jax.numpy as jnp
 from jax import lax
@@ -417,14 +415,14 @@
     row_counts = lax.all_to_all(
         jnp.broadcast_to(counts[None], (peers, 1, 1)), "wa", 0, 0, tiled=True
     ).reshape(peers)
-    features, row_counts = lax.optimization_barrier((features, row_counts))
     from_right = [shifted(piece, "wa", -1) for piece in cut(features)]
     below = shifted(features, "ha", -1)
     outgoing, meta = route(row_counts, owner_perm, cotangent)
+    outgoing, from_right[0] = lax.optimization_barrier((outgoing, from_right[0]))
+    corner = [shifted(piece, "ha", -1) for piece in from_right]
     incoming = lax.all_to_all(
         outgoing.reshape(peers, PIX, C), "wa", split_axis=0, concat_axis=0, tiled=True
     )
-    corner = [shifted(piece, "ha", -1) for piece in from_right]
     pieces = (features, *from_right, below, *corner)
     places = jnp.concatenate(
         [offsets[:, :SIDE], offsets[:, SIDE:] + (corners[:, 1:2] % 16) * 4], axis=1
@@ -442,24 +440,21 @@
     mine = (mine + pick_layer(core, grad0, grad1).astype(F32)).astype(BF)
     parts = lax.all_to_all(mine.reshape(peers, -1, C), "wa", 0, 0, tiled=True)
     tile, right, lower, corner = spread(corners, inner, places, turned)
-    parts, tile, right, lower, corner = lax.optimization_barrier(
-        (parts, tile, right, lower, corner)
-    )
+    from_above = [shifted(piece, "ha", 1) for piece in (*cut(corner), lower)]
     part = jnp.sum(parts.astype(F32), axis=0).astype(BF)
     count = lax.axis_size("ha")
+    sides = []
+    for own, moved in zip(cut(right), from_above):
+        sides.append(shifted((own.astype(F32) + moved.astype(F32)).astype(BF), "wa", 1))
     total = part.astype(F32)
     for hop in range(2, count, 2):
         moved = lax.ppermute(part, "ha", [(i, (i + hop) % count) for i in range(count)])
         total = total + moved.astype(F32)
     whole = jnp.broadcast_to(total.astype(BF)[None], (peers, *total.shape))
     mine = lax.all_to_all(whole, "wa", 0, 0, tiled=True).reshape(9, C, C)
-    sides = []
-    for own, piece in zip(cut(right), cut(corner)):
-        moved = shifted(piece, "ha", 1)
-        sides.append(shifted((own.astype(F32) + moved.astype(F32)).astype(BF), "wa", 1))
-    from_above = shifted(lower, "ha", 1)
-    mine, from_above, *sides = lax.optimization_barrier((mine, from_above, *sides))
-    tile = tile + from_above.astype(F32) + jnp.concatenate(sides).astype(F32)
+    tile = tile + from_above[2].astype(F32)
+    mine, tile, *sides = lax.optimization_barrier((mine, tile, *sides))
+    tile = tile + jnp.concatenate(sides).astype(F32)
     other = swap_cores(mine)
     grads = jnp.stack([pick_layer(core, mine, other), pick_layer(core, other, mine)]).astype(F32)
     return (tile, grads.reshape(2, 3, 3, C, C))
@@ -476,4 +471,5 @@
         P(("ha", "wa"), None, None, None),
     )
     out_specs = (P("ha", "wa", None), P())
+
     return jax.shard_map(local, mesh=mesh, in_specs=in_specs, out_specs=out_specs, check_vma=False)

time: 180 us -> 189 us (1.050)
  the two profiles are of different devices: /device:TPU:1 before, /device:TPU:41 now
where the time goes in v3:
time: 189 us; the launch traced here: 188 us
  Pallas kernels  64.1 us (34%)
  starting transfers between devices  54.4 us (29%)
  waiting for transfers between devices  27.5 us (15%)
  blocking collectives  22.6 us (12%)
  other arithmetic  8.85 us (5%)
  local copies, waits for them, and re-layouts  8.6 us (5%)
    ppermute x10, starting transfers between devices, shifted(): lax.ppermute(value, axis, [(source, source + steps) for source in range(f...  33.5 us
    all_to_all x1, blocking collectives, local(): parts = lax.all_to_all(mine.reshape(peers, -1, C), 'wa', 0, 0, tiled=True)  22.6 us
    pallas_call x1, Pallas kernels, forward(): pl.pallas_call(forward_kernel, name='forward', out_shape=[jax.ShapeDtypeS...  21.1 us
    ppermute x10, waiting for transfers between devices, shifted(): lax.ppermute(value, axis, [(source, source + steps) for source in range(f...  20.5 us
    pallas_call x1, Pallas kernels, middle_grad(): pl.pallas_call(middle_kernel, name='middle_grad', out_shape=[jax.ShapeDty...  16.8 us
    pallas_call x1, Pallas kernels, spread(): pl.pallas_call(spread_kernel, name='spread', out_shape=[piece(F32), piece...  12.8 us
    pallas_call x1, Pallas kernels, last_grad(): pl.pallas_call(last_kernel, name='last_grad', out_shape=jax.ShapeDtypeStr...  10.7 us
    all_to_all x1, starting transfers between devices, local(): mine = lax.all_to_all(whole, 'wa', 0, 0, tiled=True).reshape(9, C, C)  5.67 us
  transfers between devices with their start and end apart: 18, of which 9 were waited for; matrix products, arithmetic and copies ran while one was open for 4% of the time, Pallas kernels for 19%

profile of v3, /device:TPU:41, one launch (start us, length us, event | category | flops | bytes accessed | tf_op | source)
XLA Modules:
  0.0 187.7 jit_solution(16872224634806913024)
XLA Ops:
  1.8 4.3 %collective-permute-start = (bf16[16,32,256]{2,1,0:T(8,128)(2,1)S(1)}, bf16[16,32,256]{2,1,0:T(8,128)(2,1)S(1)}, u32[]{:S(2)}, u32[]{:S(2)}) collective-permute-start(bf16[16,32,256]{2,1,0:T(8,128)(2,1)S(1)} %get-tuple-element.47), channel_id=1, source_target_pairs={{1,0},{2,1},{3,2},{4,3},{5,4},{6,5},{7,6},{8,7},{9,8},{10,9},{11,1... | collective-permute-start | bytes 786440 | tf_op jit(solution)/shard_map/ppermute | solution.py:23
  6.1 2.9 %collective-permute-start.2 = (bf16[32,32,256]{2,1,0:T(8,128)(2,1)}, bf16[32,32,256]{2,1,0:T(8,128)(2,1)S(1)}, u32[]{:S(2)}, u32[]{:S(2)}) collective-permute-start(bf16[32,32,256]{2,1,0:T(8,128)(2,1)} %tl_ref.1), channel_id=1, source_target_pairs={{16,0},{32,16},{48,32},{64,48},{80,64},{96,80},{112,96},{17,1},{33... | collective-permute-start | bytes 1572872 | tf_op jit(solution)/shard_map/ppermute | solution.py:23
  10.2 4.8 %all-to-all-start = ((s32[16,1,1]{2,1,0:T(1,128)}), s32[16,1,1]{2,1,0:T(1,128)S(1)}, u32[]{:S(2)}, u32[]{:S(2)}) async-start(s32[16,1,1]{2,1,0:T(1,128)} %broadcast_in_dim.7), calls=%async_computation | async-start | bytes 16384 | tf_op jit(solution)/shard_map/all_to_all | solution.py:415
  14.9 4.3 %collective-permute-start.1 = (bf16[16,32,256]{2,1,0:T(8,128)(2,1)S(1)}, bf16[16,32,256]{2,1,0:T(8,128)(2,1)S(1)}, u32[]{:S(2)}, u32[]{:S(2)}) collective-permute-start(bf16[16,32,256]{2,1,0:T(8,128)(2,1)S(1)} %get-tuple-element.46), channel_id=1, source_target_pairs={{1,0},{2,1},{3,2},{4,3},{5,4},{6,5},{7,6},{8,7},{9,8},{10,9},{11,1... | collective-permute-start | bytes 786440 | tf_op jit(solution)/shard_map/ppermute | solution.py:23
  21.9 2.7 %route.1 = (bf16[16,14,16,256]{3,2,1,0:T(8,128)(2,1)}, s32[17]{0:T(128)}) custom-call(s32[16]{0:T(128)} %reduce.1.count_ref, s32[1,16]{1,0:T(1,128)} %perm_ref.1, bf16[8,14,14,256]{3,2,1,0:T(8,128)(2,1)} %copy.13.x_ref), custom_call_target="tpu_custom_call" | custom-call | bytes 4194304 | tf_op jit(solution)/shard_map/route/pallas_call | solution.py:83
  24.7 4.7 %all-to-all-start.1 = ((bf16[16,224,256]{2,1,0:T(8,128)(2,1)}), bf16[16,224,256]{2,1,0:T(8,128)(2,1)S(1)}, u32[]{:S(2)}, u32[]{:S(2)}) async-start(bf16[16,224,256]{2,1,0:T(8,128)(2,1)} %bitcast.18), calls=%async_computation.1 | async-start | bytes 3670016 | tf_op jit(solution)/shard_map/all_to_all | solution.py:423
  30.2 3.3 %collective-permute-start.3 = (bf16[16,32,256]{2,1,0:T(8,128)(2,1)S(1)}, bf16[16,32,256]{2,1,0:T(8,128)(2,1)S(1)}, u32[]{:S(2)}, u32[]{:S(2)}) collective-permute-start(bf16[16,32,256]{2,1,0:T(8,128)(2,1)S(1)} %collective-permute-done.tr0_ref), channel_id=1, source_target_pairs={{16,0},{32,16},{48,32},{64,48},{80,64},{96,80},{112,96},{17,1},{33... | collective-permute-start | bytes 786440 | tf_op jit(solution)/shard_map/ppermute | solution.py:23
  36.2 5.9 %collective-permute-done.4.br1_ref = bf16[16,32,256]{2,1,0:T(8,128)(2,1)} collective-permute-done((bf16[16,32,256]{2,1,0:T(8,128)(2,1)S(1)}, bf16[16,32,256]{2,1,0:T(8,128)(2,1)}, u32[]{:S(2)}, u32[]{:S(2)}) %collective-permute-start.4) | collective-permute-done | bytes 262176 | tf_op jit(solution)/shard_map/ppermute | solution.py:23
  43.0 21.1 %forward.1 = (bf16[256,4096]{1,0:T(8,128)(2,1)}, bf16[256,4096]{1,0:T(8,128)(2,1)}, bf16[16,224,256]{2,1,0:T(8,128)(2,1)}, bf16[16,224,256]{2,1,0:T(8,128)(2,1)}, bf16[18,256,256]{2,1,0:T(8,128)(2,1)}) custom-call(s32[32]{0:T(128)} %reshape.33.corner_ref, bf16[32,32,256]{2,1,0:T(8,128)(2,1)} %tl_ref.1, bf16[16,32,256]{2,1,0:T(8,128)(2,1)} %copy-done.9, ...), custom_call_target="tpu_custom_call" | custom-call | flops 11299999744 | bytes 14680064 | tf_op jit(solution)/shard_map/forward/pallas_call | solution.py:159
  65.4 10.7 %last_grad.1 = bf16[9,256,256]{2,1,0:T(8,128)(2,1)} custom-call(s32[17]{0:T(128)} %get-tuple-element.21.meta_ref, bf16[16,224,256]{2,1,0:T(8,128)(2,1)} %copy-done.2, bf16[16,224,256]{2,1,0:T(8,128)(2,1)} %get-tuple-element.25.g1_ref, bf16[256,4096]{1,0:T(8,128)(2,1)} %get-tuple-element.26.a_ref), custom_call_target="tpu_custom_call" | custom-call | flops 4800000000 | bytes 8388608 | tf_op jit(solution)/shard_map/last_grad/pallas_call | solution.py:236
  76.2 16.8 %middle_grad.1 = (bf16[16,224,256]{2,1,0:T(8,128)(2,1)}, bf16[9,256,256]{2,1,0:T(8,128)(2,1)}) custom-call(s32[17]{0:T(128)} %get-tuple-element.21.meta_ref, bf16[16,224,256]{2,1,0:T(8,128)(2,1)} %copy-done.2, bf16[16,224,256]{2,1,0:T(8,128)(2,1)} %get-tuple-element.25.g1_ref, bf16[16,224,256]{2,1,0:T(8,128)(2,1)} %get-tuple-element.27.g0_ref, ...), custom_call_target="tpu_custom_call" | custom-call | flops 8999999488 | bytes 12582912 | tf_op jit(solution)/shard_map/middle_grad/pallas_call | solution.py:289
  94.6 2.8 %collective-permute-done.5 = bf16[9,256,256]{2,1,0:T(8,128)(2,1)S(1)} collective-permute-done((bf16[9,256,256]{2,1,0:T(8,128)(2,1)S(1)}, bf16[9,256,256]{2,1,0:T(8,128)(2,1)S(1)}, u32[]{:S(2)}, u32[]{:S(2)}) %collective-permute-start.5) | collective-permute-done | bytes 1179680 | tf_op jit(solution)/shard_map/ppermute | solution.py:403
  98.0 22.6 %all_to_all.20 = bf16[16,144,256]{2,1,0:T(8,128)(2,1)S(1)} all-to-all(bf16[16,144,256]{2,1,0:T(8,128)(2,1)S(1)} %bitcast.17), channel_id=1, replica_groups=mesh['ha'=8,'wa'=16] {'wa'}, dimensions={0} | all-to-all | bytes 2359296 | tf_op jit(solution)/shard_map/all_to_all | solution.py:441
  128.2 5.7 %all-to-all-start.3 = ((bf16[16,144,256]{2,1,0:T(8,128)(2,1)}), bf16[16,144,256]{2,1,0:T(8,128)(2,1)S(1)}, u32[]{:S(2)}, u32[]{:S(2)}) async-start(bf16[16,144,256]{2,1,0:T(8,128)(2,1)} %broadcast_in_dim.16), calls=%async_computation.3 | async-start | bytes 2359296 | tf_op jit(solution)/shard_map/all_to_all | solution.py:454
  133.9 12.8 %spread.1 = (f32[32,32,256]{2,1,0:T(8,128)}, bf16[32,32,256]{2,1,0:T(8,128)(2,1)}, bf16[32,32,256]{2,1,0:T(8,128)(2,1)}, bf16[32,32,256]{2,1,0:T(8,128)(2,1)}) custom-call(s32[32]{0:T(128)} %reshape.33.corner_ref, bf16[16,224,256]{2,1,0:T(8,128)(2,1)} %get-tuple-element.31.p_ref, f32[16,32]{1,0:T(8,128)} %select_maximum_fusion.off_ref, ...), custom_call_target="tpu_custom_call" | custom-call | flops 7000000000 | bytes 6291456 | tf_op jit(solution)/shard_map/spread/pallas_call | solution.py:376
  146.7 5.4 %collective-permute-start.9 = (bf16[32,32,256]{2,1,0:T(8,128)(2,1)}, bf16[32,32,256]{2,1,0:T(8,128)(2,1)S(1)}, u32[]{:S(2)}, u32[]{:S(2)}) collective-permute-start(bf16[32,32,256]{2,1,0:T(8,128)(2,1)} %get-tuple-element.33), channel_id=1, source_target_pairs={{0,16},{16,32},{32,48},{48,64},{64,80},{80,96},{96,112},{1,17},{17... | collective-permute-start | bytes 1572872 | tf_op jit(solution)/shard_map/ppermute | solution.py:23
  155.2 3.3 %collective-permute-start.10 = (bf16[16,32,256]{2,1,0:T(8,128)(2,1)S(1)}, bf16[16,32,256]{2,1,0:T(8,128)(2,1)S(1)}, u32[]{:S(2)}, u32[]{:S(2)}) collective-permute-start(bf16[16,32,256]{2,1,0:T(8,128)(2,1)S(1)} %get-tuple-element.45), channel_id=1, source_target_pairs={{0,16},{16,32},{32,48},{48,64},{64,80},{80,96},{96,112},{1,17},{17... | collective-permute-start | bytes 786440 | tf_op jit(solution)/shard_map/ppermute | solution.py:23
  158.5 2.7 %collective-permute-done.12 = bf16[16,32,256]{2,1,0:T(8,128)(2,1)S(1)} collective-permute-done((bf16[16,32,256]{2,1,0:T(8,128)(2,1)S(1)}, bf16[16,32,256]{2,1,0:T(8,128)(2,1)S(1)}, u32[]{:S(2)}, u32[]{:S(2)}) %collective-permute-start.12) | collective-permute-done | bytes 262176 | tf_op jit(solution)/shard_map/ppermute | solution.py:23
  161.2 2.8 %collective-permute-done.10 = bf16[16,32,256]{2,1,0:T(8,128)(2,1)S(1)} collective-permute-done((bf16[16,32,256]{2,1,0:T(8,128)(2,1)S(1)}, bf16[16,32,256]{2,1,0:T(8,128)(2,1)S(1)}, u32[]{:S(2)}, u32[]{:S(2)}) %collective-permute-start.10) | collective-permute-done | bytes 262176 | tf_op jit(solution)/shard_map/ppermute | solution.py:23
  164.2 3.1 %collective-permute-start.13 = (bf16[16,32,256]{2,1,0:T(8,128)(2,1)S(1)}, bf16[16,32,256]{2,1,0:T(8,128)(2,1)S(1)}, u32[]{:S(2)}, u32[]{:S(2)}) collective-permute-start(bf16[16,32,256]{2,1,0:T(8,128)(2,1)S(1)} %get-tuple-element.42), channel_id=1, source_target_pairs={{0,1},{1,2},{2,3},{3,4},{4,5},{5,6},{6,7},{7,8},{8,9},{9,10},{10,1... | collective-permute-start | bytes 786440 | tf_op jit(solution)/shard_map/ppermute | solution.py:23
  167.3 3.1 %collective-permute-start.11 = (bf16[16,32,256]{2,1,0:T(8,128)(2,1)S(1)}, bf16[16,32,256]{2,1,0:T(8,128)(2,1)S(1)}, u32[]{:S(2)}, u32[]{:S(2)}) collective-permute-start(bf16[16,32,256]{2,1,0:T(8,128)(2,1)S(1)} %get-tuple-element.43), channel_id=1, source_target_pairs={{0,1},{1,2},{2,3},{3,4},{4,5},{5,6},{6,7},{7,8},{8,9},{9,10},{10,1... | collective-permute-start | bytes 786440 | tf_op jit(solution)/shard_map/ppermute | solution.py:23
  170.7 3.3 %collective-permute-done.13 = bf16[16,32,256]{2,1,0:T(8,128)(2,1)S(1)} collective-permute-done((bf16[16,32,256]{2,1,0:T(8,128)(2,1)S(1)}, bf16[16,32,256]{2,1,0:T(8,128)(2,1)S(1)}, u32[]{:S(2)}, u32[]{:S(2)}) %collective-permute-start.13) | collective-permute-done | bytes 262176 | tf_op jit(solution)/shard_map/ppermute | solution.py:23
  174.0 5.7 %collective-permute-done.11 = bf16[16,32,256]{2,1,0:T(8,128)(2,1)S(1)} collective-permute-done((bf16[16,32,256]{2,1,0:T(8,128)(2,1)S(1)}, bf16[16,32,256]{2,1,0:T(8,128)(2,1)S(1)}, u32[]{:S(2)}, u32[]{:S(2)}) %collective-permute-start.11) | collective-permute-done | bytes 262176 | tf_op jit(solution)/shard_map/ppermute | solution.py:23
  179.7 2.9 %collective-permute-start.14 = (bf16[9,256,256]{2,1,0:T(8,128)(2,1)S(1)}, bf16[9,256,256]{2,1,0:T(8,128)(2,1)S(1)}, u32[]{:S(2)}, u32[]{:S(2)}) collective-permute-start(bf16[9,256,256]{2,1,0:T(8,128)(2,1)S(1)} %bitcast.15), channel_id=1, source_target_pairs={{0,16},{16,0},{32,48},{48,32},{64,80},{80,64},{96,112},{112,96},{1... | collective-permute-start | bytes 3538952 | tf_op jit(solution)/shard_map/ppermute | solution.py:403
  (69 shorter events, 28.4 us)
Async XLA Ops:
  0.6 19.3 %copy-start.4 = (bf16[8,14,14,256]{3,0,2,1:T(8,128)(2,1)S(1)}, bf16[8,14,14,256]{3,0,2,1:T(8,128)(2,1)}, u32[]{:S(2)}) copy-start(bf16[8,14,14,256]{3,0,2,1:T(8,128)(2,1)} %param.13) | copy-start | bytes 2408452
  1.8 22.8 %collective-permute-start = (bf16[16,32,256]{2,1,0:T(8,128)(2,1)S(1)}, bf16[16,32,256]{2,1,0:T(8,128)(2,1)S(1)}, u32[]{:S(2)}, u32[]{:S(2)}) collective-permute-start(bf16[16,32,256]{2,1,0:T(8,128)(2,1)S(1)} %get-tuple-element.47), channel_id=1, source_target_pairs={{1,0},{2,1},{3,2},{4,3},{5,4},{6,5},{7,6},{8,7},{9,8},{10,9},{11,1... | collective-permute-start | bytes 786440 | tf_op jit(solution)/shard_map/ppermute | solution.py:23
  6.1 36.1 %collective-permute-start.2 = (bf16[32,32,256]{2,1,0:T(8,128)(2,1)}, bf16[32,32,256]{2,1,0:T(8,128)(2,1)S(1)}, u32[]{:S(2)}, u32[]{:S(2)}) collective-permute-start(bf16[32,32,256]{2,1,0:T(8,128)(2,1)} %tl_ref.1), channel_id=1, source_target_pairs={{16,0},{32,16},{48,32},{64,48},{80,64},{96,80},{112,96},{17,1},{33... | collective-permute-start | bytes 1572872 | tf_op jit(solution)/shard_map/ppermute | solution.py:23
  10.2 10.8 %all-to-all-start = ((s32[16,1,1]{2,1,0:T(1,128)}), s32[16,1,1]{2,1,0:T(1,128)S(1)}, u32[]{:S(2)}, u32[]{:S(2)}) async-start(s32[16,1,1]{2,1,0:T(1,128)} %broadcast_in_dim.7), calls=%async_computation | async-start | bytes 16384 | tf_op jit(solution)/shard_map/all_to_all | solution.py:415
  14.9 18.6 %collective-permute-start.1 = (bf16[16,32,256]{2,1,0:T(8,128)(2,1)S(1)}, bf16[16,32,256]{2,1,0:T(8,128)(2,1)S(1)}, u32[]{:S(2)}, u32[]{:S(2)}) collective-permute-start(bf16[16,32,256]{2,1,0:T(8,128)(2,1)S(1)} %get-tuple-element.46), channel_id=1, source_target_pairs={{1,0},{2,1},{3,2},{4,3},{5,4},{6,5},{7,6},{8,7},{9,8},{10,9},{11,1... | collective-permute-start | bytes 786440 | tf_op jit(solution)/shard_map/ppermute | solution.py:23
  24.7 10.8 %copy-start.7 = (pred[16]{0:T(512)(128)(4,1)S(1)}, pred[16]{0:T(512)(128)(4,1)}, u32[]{:S(2)}) copy-start(pred[16]{0:T(512)(128)(4,1)} %constant.38.clone.1) | copy-start | bytes 52
  24.7 39.5 %all-to-all-start.1 = ((bf16[16,224,256]{2,1,0:T(8,128)(2,1)}), bf16[16,224,256]{2,1,0:T(8,128)(2,1)S(1)}, u32[]{:S(2)}, u32[]{:S(2)}) async-start(bf16[16,224,256]{2,1,0:T(8,128)(2,1)} %bitcast.18), calls=%async_computation.1 | async-start | bytes 3670016 | tf_op jit(solution)/shard_map/all_to_all | solution.py:423
  30.2 12.0 %collective-permute-start.3 = (bf16[16,32,256]{2,1,0:T(8,128)(2,1)S(1)}, bf16[16,32,256]{2,1,0:T(8,128)(2,1)S(1)}, u32[]{:S(2)}, u32[]{:S(2)}) collective-permute-start(bf16[16,32,256]{2,1,0:T(8,128)(2,1)S(1)} %collective-permute-done.tr0_ref), channel_id=1, source_target_pairs={{16,0},{32,16},{48,32},{64,48},{80,64},{96,80},{112,96},{17,1},{33... | collective-permute-start | bytes 786440 | tf_op jit(solution)/shard_map/ppermute | solution.py:23
  33.5 8.7 %copy-start.10 = (bf16[16,32,256]{2,1,0:T(8,128)(2,1)}, bf16[16,32,256]{2,1,0:T(8,128)(2,1)S(1)}, u32[]{:S(2)}) copy-start(bf16[16,32,256]{2,1,0:T(8,128)(2,1)S(1)} %collective-permute-done.1.tr1_ref) | copy-start | bytes 786436
  33.5 8.6 %collective-permute-start.4 = (bf16[16,32,256]{2,1,0:T(8,128)(2,1)S(1)}, bf16[16,32,256]{2,1,0:T(8,128)(2,1)}, u32[]{:S(2)}, u32[]{:S(2)}) collective-permute-start(bf16[16,32,256]{2,1,0:T(8,128)(2,1)S(1)} %collective-permute-done.1.tr1_ref), channel_id=1, source_target_pairs={{16,0},{32,16},{48,32},{64,48},{80,64},{96,80},{112,96},{17,1},{33... | collective-permute-start | bytes 786440 | tf_op jit(solution)/shard_map/ppermute | solution.py:23
  76.2 16.8 %copy-start = (bf16[9,256,256]{2,1,0:T(8,128)(2,1)S(1)}, bf16[9,256,256]{2,1,0:T(8,128)(2,1)}, u32[]{:S(2)}) copy-start(bf16[9,256,256]{2,1,0:T(8,128)(2,1)} %last_grad.1) | copy-start | bytes 3538948
  94.5 2.9 %collective-permute-start.5 = (bf16[9,256,256]{2,1,0:T(8,128)(2,1)S(1)}, bf16[9,256,256]{2,1,0:T(8,128)(2,1)S(1)}, u32[]{:S(2)}, u32[]{:S(2)}) collective-permute-start(bf16[9,256,256]{2,1,0:T(8,128)(2,1)S(1)} %broadcast_select_fusion.2), channel_id=1, source_target_pairs={{0,16},{16,0},{32,48},{48,32},{64,80},{80,64},{96,112},{112,96},{1... | collective-permute-start | bytes 3538952 | tf_op jit(solution)/shard_map/ppermute | solution.py:403
  120.8 3.5 %collective-permute-start.8 = (bf16[144,256]{1,0:T(8,128)(2,1)S(1)}, bf16[144,256]{1,0:T(8,128)(2,1)S(1)}, u32[]{:S(2)}, u32[]{:S(2)}) collective-permute-start(bf16[144,256]{1,0:T(8,128)(2,1)S(1)} %reduce_sum.12), channel_id=1, source_target_pairs={{0,96},{16,112},{32,0},{48,16},{64,32},{80,48},{96,64},{112,80},{1... | collective-permute-start | bytes 221192 | tf_op jit(solution)/shard_map/ppermute | solution.py:451
  121.0 5.1 %collective-permute-start.7 = (bf16[144,256]{1,0:T(8,128)(2,1)S(1)}, bf16[144,256]{1,0:T(8,128)(2,1)S(1)}, u32[]{:S(2)}, u32[]{:S(2)}) collective-permute-start(bf16[144,256]{1,0:T(8,128)(2,1)S(1)} %reduce_sum.12), channel_id=1, source_target_pairs={{0,64},{16,80},{32,96},{48,112},{64,0},{80,16},{96,32},{112,48},{1... | collective-permute-start | bytes 221192 | tf_op jit(solution)/shard_map/ppermute | solution.py:451
  123.6 3.5 %collective-permute-start.6 = (bf16[144,256]{1,0:T(8,128)(2,1)S(1)}, bf16[144,256]{1,0:T(8,128)(2,1)S(1)}, u32[]{:S(2)}, u32[]{:S(2)}) collective-permute-start(bf16[144,256]{1,0:T(8,128)(2,1)S(1)} %reduce_sum.12), channel_id=1, source_target_pairs={{0,32},{16,48},{32,64},{48,80},{64,96},{80,112},{96,0},{112,16},{1... | collective-permute-start | bytes 221192 | tf_op jit(solution)/shard_map/ppermute | solution.py:451
  128.2 51.4 %all-to-all-start.3 = ((bf16[16,144,256]{2,1,0:T(8,128)(2,1)}), bf16[16,144,256]{2,1,0:T(8,128)(2,1)S(1)}, u32[]{:S(2)}, u32[]{:S(2)}) async-start(bf16[16,144,256]{2,1,0:T(8,128)(2,1)} %broadcast_in_dim.16), calls=%async_computation.3 | async-start | bytes 2359296 | tf_op jit(solution)/shard_map/all_to_all | solution.py:454
  146.7 17.4 %copy-start.5 = (bf16[32,32,256]{2,1,0:T(8,128)(2,1)S(1)}, bf16[32,32,256]{2,1,0:T(8,128)(2,1)}, u32[]{:S(2)}) copy-start(bf16[32,32,256]{2,1,0:T(8,128)(2,1)} %get-tuple-element.34) | copy-start | bytes 1572868
  146.7 23.8 %collective-permute-start.9 = (bf16[32,32,256]{2,1,0:T(8,128)(2,1)}, bf16[32,32,256]{2,1,0:T(8,128)(2,1)S(1)}, u32[]{:S(2)}, u32[]{:S(2)}) collective-permute-start(bf16[32,32,256]{2,1,0:T(8,128)(2,1)} %get-tuple-element.33), channel_id=1, source_target_pairs={{0,16},{16,32},{32,48},{48,64},{64,80},{80,96},{96,112},{1,17},{17... | collective-permute-start | bytes 1572872 | tf_op jit(solution)/shard_map/ppermute | solution.py:23
  152.1 18.4 %copy-start.3 = (f32[32,32,256]{2,1,0:T(8,128)S(1)}, f32[32,32,256]{2,1,0:T(8,128)}, u32[]{:S(2)}) copy-start(f32[32,32,256]{2,1,0:T(8,128)} %get-tuple-element.32) | copy-start | bytes 3145732
  153.3 8.0 %collective-permute-start.12 = (bf16[16,32,256]{2,1,0:T(8,128)(2,1)S(1)}, bf16[16,32,256]{2,1,0:T(8,128)(2,1)S(1)}, u32[]{:S(2)}, u32[]{:S(2)}) collective-permute-start(bf16[16,32,256]{2,1,0:T(8,128)(2,1)S(1)} %get-tuple-element.44), channel_id=1, source_target_pairs={{0,16},{16,32},{32,48},{48,64},{64,80},{80,96},{96,112},{1,17},{17... | collective-permute-start | bytes 786440 | tf_op jit(solution)/shard_map/ppermute | solution.py:23
  155.2 8.8 %collective-permute-start.10 = (bf16[16,32,256]{2,1,0:T(8,128)(2,1)S(1)}, bf16[16,32,256]{2,1,0:T(8,128)(2,1)S(1)}, u32[]{:S(2)}, u32[]{:S(2)}) collective-permute-start(bf16[16,32,256]{2,1,0:T(8,128)(2,1)S(1)} %get-tuple-element.45), channel_id=1, source_target_pairs={{0,16},{16,32},{32,48},{48,64},{64,80},{80,96},{96,112},{1,17},{17... | collective-permute-start | bytes 786440 | tf_op jit(solution)/shard_map/ppermute | solution.py:23
  164.2 9.8 %collective-permute-start.13 = (bf16[16,32,256]{2,1,0:T(8,128)(2,1)S(1)}, bf16[16,32,256]{2,1,0:T(8,128)(2,1)S(1)}, u32[]{:S(2)}, u32[]{:S(2)}) collective-permute-start(bf16[16,32,256]{2,1,0:T(8,128)(2,1)S(1)} %get-tuple-element.42), channel_id=1, source_target_pairs={{0,1},{1,2},{2,3},{3,4},{4,5},{5,6},{6,7},{7,8},{8,9},{9,10},{10,1... | collective-permute-start | bytes 786440 | tf_op jit(solution)/shard_map/ppermute | solution.py:23
  167.3 12.3 %collective-permute-start.11 = (bf16[16,32,256]{2,1,0:T(8,128)(2,1)S(1)}, bf16[16,32,256]{2,1,0:T(8,128)(2,1)S(1)}, u32[]{:S(2)}, u32[]{:S(2)}) collective-permute-start(bf16[16,32,256]{2,1,0:T(8,128)(2,1)S(1)} %get-tuple-element.43), channel_id=1, source_target_pairs={{0,1},{1,2},{2,3},{3,4},{4,5},{5,6},{6,7},{7,8},{8,9},{9,10},{10,1... | collective-permute-start | bytes 786440 | tf_op jit(solution)/shard_map/ppermute | solution.py:23
  179.7 5.4 %collective-permute-start.14 = (bf16[9,256,256]{2,1,0:T(8,128)(2,1)S(1)}, bf16[9,256,256]{2,1,0:T(8,128)(2,1)S(1)}, u32[]{:S(2)}, u32[]{:S(2)}) collective-permute-start(bf16[9,256,256]{2,1,0:T(8,128)(2,1)S(1)} %bitcast.15), channel_id=1, source_target_pairs={{0,16},{16,0},{32,48},{48,32},{64,80},{80,64},{96,112},{112,96},{1... | collective-permute-start | bytes 3538952 | tf_op jit(solution)/shard_map/ppermute | solution.py:403
  (7 other events, 22.5 us)

commit v4 on v3

--- a/solution.py
+++ b/solution.py
@@ -118,7 +118,7 @@
         places[1] = 4.0 * (at - SPAN * row)
 
     keep = inside(PIX)
-    lane = lax.broadcasted_iota(jnp.int32, (32, 128), 1)
+    lane = lax.broadcasted_iota(jnp.int32, (32, 16), 1)
     for g in range(FG):
         slot = step * FG + g
         top = corner_ref[slot]
@@ -176,7 +176,7 @@
                 whole(BOX, BOX, C),
                 whole(half, BOX, C),
                 whole(half, BOX, C),
-                whole(32, 128),
+                whole(32, 16),
                 whole(18, C, C),
             ],
             out_specs=[columns, columns, regions, regions, whole(18, C, C)],
@@ -197,61 +197,16 @@
 BG = 4
 
 
-def top_grad(meta_ref, slot, in_ref, g1_ref, g):
-    source = meta_ref[slot]
+def top_grad(meta_ref, slot, in_ref, slope):
     live = slot < meta_ref[16]
-    grad = in_ref[source].astype(F32) * g1_ref[g].astype(F32)
+    grad = in_ref[meta_ref[jnp.minimum(slot, 15)]].astype(F32) * slope.astype(F32)
     return jnp.where(live, grad, 0.0)
 
 
-def kernel_grad(step, steps, held, a_ref, acc, o_ref):
-    @pl.when(step == 0)
-    def _():
-        acc[...] = jnp.zeros_like(acc)
-
-    for dy in range(3):
-        for dx in range(3):
-            grads = held[2 - dx, :, 32 - 16 * dy : 32 - 16 * dy + C, :].reshape(BG * C, C)
-            acc[dy * 3 + dx] += dot(a_ref[...], grads)
-
-    @pl.when(step == steps - 1)
-    def _():
-        o_ref[...] = acc[...].astype(BF)
-
-
-def last_kernel(meta_ref, in_ref, g1_ref, a_ref, o_ref, held, acc):
-    step = pl.program_id(0)
-
-    @pl.when(step == 0)
-    def _():
-        clear_edges(held, BG)
-
-    for g in range(BG):
-        hold(held, g, top_grad(meta_ref, step * BG + g, in_ref, g1_ref, g))
-    kernel_grad(step, pl.num_programs(0), held, a_ref, acc, o_ref)
-
-
-def last_grad(meta, incoming, slope1, acts1):
-    slots = slope1.shape[0]
-    return pl.pallas_call(
-        last_kernel,
-        name="last_grad",
-        out_shape=jax.ShapeDtypeStruct((9, C, C), BF),
-        grid_spec=pltpu.PrefetchScalarGridSpec(
-            num_scalar_prefetch=1,
-            grid=(slots // BG,),
-            in_specs=[
-                pl.BlockSpec((16, PIX, C), lambda i, *_: (0, 0, 0)),
-                pl.BlockSpec((BG, PIX, C), lambda i, *_: (i, 0, 0)),
-                pl.BlockSpec((C, BG * C), lambda i, *_: (0, i)),
-            ],
-            out_specs=pl.BlockSpec((9, C, C), lambda i, *_: (0, 0, 0)),
-            scratch_shapes=[pltpu.VMEM((3, BG, ROWS, C), BF), pltpu.VMEM((9, C, C), F32)],
-        ),
-        cost_estimate=pl.CostEstimate(
-            flops=4_800_000_000, bytes_accessed=8 << 20, transcendentals=0
-        ),
-    )(meta, incoming, slope1, acts1)
+def add_tap(held, a_ref, acc, tap):
+    dy, dx = divmod(tap, 3)
+    grads = held[2 - dx, :, 32 - 16 * dy : 32 - 16 * dy + C, :].reshape(BG * C, C)
+    acc[tap] += dot(a_ref[...], grads)
 
 
 def input_grad(held, g, k_ref):
@@ -265,58 +220,89 @@
     return total.astype(BF)
 
 
-def middle_kernel(
-    meta_ref, in_ref, g1_ref, g0_ref, k_ref, a_ref, p_ref, o_ref, upper, held, acc
+def back_kernel(
+    meta_ref, in_ref, first_ref, next_ref, g0_ref, k_ref, a1_ref, a0_ref,
+    p_ref, o1_ref, o0_ref, upper, held, acc1, acc0,
 ):
     step = pl.program_id(0)
+    now = step & 1
 
     @pl.when(step == 0)
     def _():
-        clear_edges(upper, BG)
+        clear_edges(upper.at[0], BG)
+        clear_edges(upper.at[1], BG)
         clear_edges(held, BG)
-
-    for g in range(BG):
-        hold(upper, g, top_grad(meta_ref, step * BG + g, in_ref, g1_ref, g))
-    for g in range(BG):
-        grad = input_grad(upper, g, k_ref).astype(F32) * g0_ref[g].astype(F32)
+        acc1[...] = jnp.zeros_like(acc1)
+        acc0[...] = jnp.zeros_like(acc0)
+        for g in range(BG):
+            hold(upper.at[0], g, top_grad(meta_ref, g, in_ref, first_ref[g]))
+
+    here = upper.at[now]
+    later = upper.at[1 - now]
+
+    def inner_grad(g, grad):
+        grad = grad.astype(F32) * g0_ref[g].astype(F32)
         p_ref[g] = grad.astype(BF)
         hold(held, g, grad)
-    kernel_grad(step, pl.num_programs(0), held, a_ref, acc, o_ref)
-
-
-def middle_grad(meta, incoming, slope1, slope0, kernels, acts0):
+
+    grads = [input_grad(here, 0, k_ref)]
+    for g in range(1, BG):
+        grads.append(input_grad(here, g, k_ref))
+        inner_grad(g - 1, grads[g - 1])
+    for tap in range(9):
+        add_tap(here, a1_ref, acc1, tap)
+        if tap == 0:
+            inner_grad(BG - 1, grads[BG - 1])
+    for tap in range(9):
+        add_tap(held, a0_ref, acc0, tap)
+        if tap % 2 == 0 and tap // 2 < BG:
+            g = tap // 2
+            hold(later, g, top_grad(meta_ref, (step + 1) * BG + g, in_ref, next_ref[g]))
+
+    @pl.when(step == pl.num_programs(0) - 1)
+    def _():
+        o1_ref[...] = acc1[...].astype(BF)
+        o0_ref[...] = acc0[...].astype(BF)
+
+
+def back(meta, incoming, slope1, slope0, kernels, acts1, acts0):
     slots = slope1.shape[0]
+    steps = slots // BG
+    whole = lambda *shape: pl.BlockSpec(shape, lambda i, *_: (0,) * len(shape))
+    regions = pl.BlockSpec((BG, PIX, C), lambda i, *_: (i, 0, 0))
+    columns = pl.BlockSpec((C, BG * C), lambda i, *_: (0, i))
     return pl.pallas_call(
-        middle_kernel,
-        name="middle_grad",
+        back_kernel,
+        name="back",
         out_shape=[
             jax.ShapeDtypeStruct((slots, PIX, C), BF),
+            jax.ShapeDtypeStruct((9, C, C), BF),
             jax.ShapeDtypeStruct((9, C, C), BF),
         ],
         grid_spec=pltpu.PrefetchScalarGridSpec(
             num_scalar_prefetch=1,
-            grid=(slots // BG,),
+            grid=(steps,),
             in_specs=[
-                pl.BlockSpec((16, PIX, C), lambda i, *_: (0, 0, 0)),
-                pl.BlockSpec((BG, PIX, C), lambda i, *_: (i, 0, 0)),
-                pl.BlockSpec((BG, PIX, C), lambda i, *_: (i, 0, 0)),
+                whole(16, PIX, C),
+                whole(BG, PIX, C),
+                pl.BlockSpec((BG, PIX, C), lambda i, *_: (jnp.minimum(i + 1, steps - 1), 0, 0)),
+                regions,
                 pl.BlockSpec((9, C, C), lambda i, *_: (1, 0, 0)),
-                pl.BlockSpec((C, BG * C), lambda i, *_: (0, i)),
-            ],
-            out_specs=[
-                pl.BlockSpec((BG, PIX, C), lambda i, *_: (i, 0, 0)),
-                pl.BlockSpec((9, C, C), lambda i, *_: (0, 0, 0)),
-            ],
+                columns,
+                columns,
+            ],
+            out_specs=[regions, whole(9, C, C), whole(9, C, C)],
             scratch_shapes=[
-                pltpu.VMEM((3, BG, ROWS, C), BF),
+                pltpu.VMEM((2, 3, BG, ROWS, C), BF),
                 pltpu.VMEM((3, BG, ROWS, C), BF),
                 pltpu.VMEM((9, C, C), F32),
+                pltpu.VMEM((9, C, C), F32),
             ],
         ),
         cost_estimate=pl.CostEstimate(
-            flops=9_000_000_000, bytes_accessed=12 << 20, transcendentals=0
-        ),
-    )(meta, incoming, slope1, slope0, kernels, acts0)
+            flops=14_000_000_000, bytes_accessed=16 << 20, transcendentals=0
+        ),
+    )(meta, incoming, slope1, slope1, slope0, kernels, acts1, acts0)
 
 
 SG = 4
@@ -403,6 +389,14 @@
     return lax.ppermute(x, "ha", [(i, i ^ 1) for i in range(lax.axis_size("ha"))])
 
 
+def over_chips(pieces):
+    down, across = lax.axis_size("ha"), lax.axis_size("wa")
+    groups = [[h * across + w for h in range(c, down, 2) for w in range(across)] for c in range(2)]
+    return lax.all_to_all(
+        pieces, ("ha", "wa"), 0, 0, tiled=True, axis_index_groups=groups
+    )
+
+
 def pick_layer(index, first, second):
     return jnp.where(index == 0, first, second)
 
@@ -418,7 +412,6 @@
     from_right = [shifted(piece, "wa", -1) for piece in cut(features)]
     below = shifted(features, "ha", -1)
     outgoing, meta = route(row_counts, owner_perm, cotangent)
-    outgoing, from_right[0] = lax.optimization_barrier((outgoing, from_right[0]))
     corner = [shifted(piece, "ha", -1) for piece in from_right]
     incoming = lax.all_to_all(
         outgoing.reshape(peers, PIX, C), "wa", split_axis=0, concat_axis=0, tiled=True
@@ -429,32 +422,25 @@
     ).astype(F32)
     pad = lambda x: jnp.pad(x, ((0, 0), (0, 2)), constant_values=-1000.0)
     places = jnp.concatenate([pad(places[:, :SIDE]), pad(places[:, SIDE:])], axis=1)
-    place_cols = jnp.pad(places.T, ((0, 0), (0, 112)))
+    place_cols = places.T
     corners = corners.T.reshape(-1)
     acts0, acts1, slope0, slope1, turned = forward(
         corners, pieces, place_cols, kernels.reshape(18, C, C)
     )
-    grad1 = last_grad(meta, incoming, slope1, acts1)
-    inner, grad0 = middle_grad(meta, incoming, slope1, slope0, turned, acts0)
+    inner, grad1, grad0 = back(meta, incoming, slope1, slope0, turned, acts1, acts0)
     mine = swap_cores(pick_layer(core, grad1, grad0)).astype(F32)
     mine = (mine + pick_layer(core, grad0, grad1).astype(F32)).astype(BF)
-    parts = lax.all_to_all(mine.reshape(peers, -1, C), "wa", 0, 0, tiled=True)
+    chips = lax.axis_size("ha") // 2 * peers
+    parts = over_chips(mine.reshape(chips, -1, C))
     tile, right, lower, corner = spread(corners, inner, places, turned)
-    from_above = [shifted(piece, "ha", 1) for piece in (*cut(corner), lower)]
-    part = jnp.sum(parts.astype(F32), axis=0).astype(BF)
-    count = lax.axis_size("ha")
-    sides = []
-    for own, moved in zip(cut(right), from_above):
-        sides.append(shifted((own.astype(F32) + moved.astype(F32)).astype(BF), "wa", 1))
-    total = part.astype(F32)
-    for hop in range(2, count, 2):
-        moved = lax.ppermute(part, "ha", [(i, (i + hop) % count) for i in range(count)])
-        total = total + moved.astype(F32)
-    whole = jnp.broadcast_to(total.astype(BF)[None], (peers, *total.shape))
-    mine = lax.all_to_all(whole, "wa", 0, 0, tiled=True).reshape(9, C, C)
-    tile = tile + from_above[2].astype(F32)
-    mine, tile, *sides = lax.optimization_barrier((mine, tile, *sides))
-    tile = tile + jnp.concatenate(sides).astype(F32)
+    corner, lower = [shifted(piece, "ha", 1) for piece in (corner, lower)]
+    side = shifted((right.astype(F32) + corner.astype(F32)).astype(BF), "wa", 1)
+    tile = tile + lower.astype(F32)
+    total = jnp.sum(parts.astype(F32), axis=0).astype(BF)
+    whole = jnp.broadcast_to(total[None], (chips, *total.shape))
+    mine = over_chips(whole).reshape(9, C, C)
+    mine, tile, side = lax.optimization_barrier((mine, tile, side))
+    tile = tile + side.astype(F32)
     other = swap_cores(mine)
     grads = jnp.stack([pick_layer(core, mine, other), pick_layer(core, other, mine)]).astype(F32)
     return (tile, grads.reshape(2, 3, 3, C, C))

time: 189 us -> 169 us (0.89)
  the two profiles are of different devices: /device:TPU:41 before, /device:TPU:1 now
where the time goes in v4:
time: 169 us; the launch traced here: 166 us
  Pallas kernels  59.5 us (35%)
  starting transfers between devices  56.3 us (33%)
  waiting for transfers between devices  28.8 us (17%)
  other arithmetic  10.8 us (6%)
  local copies, waits for them, and re-layouts  8.83 us (5%)
    pallas_call x1, Pallas kernels, back(): pl.pallas_call(back_kernel, name='back', out_shape=[jax.ShapeDtypeStruct(...  22.8 us
    ppermute x8, waiting for transfers between devices, shifted(): lax.ppermute(value, axis, [(source, source + steps) for source in range(f...  21.5 us
    pallas_call x1, Pallas kernels, forward(): pl.pallas_call(forward_kernel, name='forward', out_shape=[jax.ShapeDtypeS...  21.1 us
    ppermute x8, starting transfers between devices, shifted(): lax.ppermute(value, axis, [(source, source + steps) for source in range(f...  21 us
    all_to_all x2, starting transfers between devices, over_chips(): lax.all_to_all(pieces, ('ha', 'wa'), 0, 0, tiled=True, axis_index_groups=...  16.7 us
    pallas_call x1, Pallas kernels, spread(): pl.pallas_call(spread_kernel, name='spread', out_shape=[piece(F32), piece...  12.8 us
    all_to_all x1, starting transfers between devices, local(): lax.all_to_all(outgoing.reshape(peers, PIX, C), 'wa', split_axis=0, conca...  9.47 us
    all_to_all x1, starting transfers between devices, local(): lax.all_to_all(jnp.broadcast_to(counts[None], (peers, 1, 1)), 'wa', 0, 0,...  7.57 us
  transfers between devices with their start and end apart: 14, of which 7 were waited for; matrix products, arithmetic and copies ran while one was open for 7% of the time, Pallas kernels for 22%

profile of v4, /device:TPU:1, one launch (start us, length us, event | category | flops | bytes accessed | tf_op | source)
XLA Modules:
  0.0 165.8 jit_solution(17763997223215378953)
XLA Ops:
  2.0 7.6 %all-to-all-start = ((s32[16,1,1]{2,1,0:T(1,128)}), s32[16,1,1]{2,1,0:T(1,128)S(1)}, u32[]{:S(2)}, u32[]{:S(2)}) async-start(s32[16,1,1]{2,1,0:T(1,128)} %broadcast_in_dim.7), calls=%async_computation | async-start | bytes 16384 | tf_op jit(solution)/shard_map/all_to_all | solution.py:409
  9.5 2.9 %collective-permute-start.2 = (bf16[32,32,256]{2,1,0:T(8,128)(2,1)}, bf16[32,32,256]{2,1,0:T(8,128)(2,1)S(1)}, u32[]{:S(2)}, u32[]{:S(2)}) collective-permute-start(bf16[32,32,256]{2,1,0:T(8,128)(2,1)} %tl_ref.1), channel_id=1, source_target_pairs={{16,0},{32,16},{48,32},{64,48},{80,64},{96,80},{112,96},{17,1},{33... | collective-permute-start | bytes 1572872 | tf_op jit(solution)/shard_map/ppermute | solution.py:23
  18.8 2.7 %route.1 = (bf16[16,14,16,256]{3,2,1,0:T(8,128)(2,1)}, s32[17]{0:T(128)}) custom-call(s32[16]{0:T(128)} %reduce.1.count_ref, s32[1,16]{1,0:T(1,128)} %perm_ref.1, bf16[8,14,14,256]{3,2,1,0:T(8,128)(2,1)} %copy.15.x_ref), custom_call_target="tpu_custom_call" | custom-call | bytes 4194304 | tf_op jit(solution)/shard_map/route/pallas_call | solution.py:83
  21.5 9.5 %all-to-all-start.1 = ((bf16[16,224,256]{2,1,0:T(8,128)(2,1)}), bf16[16,224,256]{2,1,0:T(8,128)(2,1)S(1)}, u32[]{:S(2)}, u32[]{:S(2)}) async-start(bf16[16,224,256]{2,1,0:T(8,128)(2,1)} %bitcast.13), calls=%async_computation.1 | async-start | bytes 3670016 | tf_op jit(solution)/shard_map/all_to_all | solution.py:416
  31.9 2.1 %collective-permute-start.4 = (bf16[16,32,256]{2,1,0:T(8,128)(2,1)S(1)}, bf16[16,32,256]{2,1,0:T(8,128)(2,1)S(1)}, u32[]{:S(2)}, u32[]{:S(2)}) collective-permute-start(bf16[16,32,256]{2,1,0:T(8,128)(2,1)S(1)} %collective-permute-done.1.tr1_ref), channel_id=1, source_target_pairs={{16,0},{32,16},{48,32},{64,48},{80,64},{96,80},{112,96},{17,1},{33... | collective-permute-start | bytes 786440 | tf_op jit(solution)/shard_map/ppermute | solution.py:23
  34.0 1.9 %collective-permute-start.3 = (bf16[16,32,256]{2,1,0:T(8,128)(2,1)S(1)}, bf16[16,32,256]{2,1,0:T(8,128)(2,1)}, u32[]{:S(2)}, u32[]{:S(2)}) collective-permute-start(bf16[16,32,256]{2,1,0:T(8,128)(2,1)S(1)} %collective-permute-done.tr0_ref), channel_id=1, source_target_pairs={{16,0},{32,16},{48,32},{64,48},{80,64},{96,80},{112,96},{17,1},{33... | collective-permute-start | bytes 786440 | tf_op jit(solution)/shard_map/ppermute | solution.py:23
  36.7 3.8 %collective-permute-done.4.br1_ref = bf16[16,32,256]{2,1,0:T(8,128)(2,1)S(1)} collective-permute-done((bf16[16,32,256]{2,1,0:T(8,128)(2,1)S(1)}, bf16[16,32,256]{2,1,0:T(8,128)(2,1)S(1)}, u32[]{:S(2)}, u32[]{:S(2)}) %collective-permute-start.4) | collective-permute-done | bytes 262176 | tf_op jit(solution)/shard_map/ppermute | solution.py:23
  40.5 2.8 %collective-permute-done.3.br0_ref = bf16[16,32,256]{2,1,0:T(8,128)(2,1)} collective-permute-done((bf16[16,32,256]{2,1,0:T(8,128)(2,1)S(1)}, bf16[16,32,256]{2,1,0:T(8,128)(2,1)}, u32[]{:S(2)}, u32[]{:S(2)}) %collective-permute-start.3) | collective-permute-done | bytes 262176 | tf_op jit(solution)/shard_map/ppermute | solution.py:23
  44.1 21.1 %forward.1 = (bf16[256,4096]{1,0:T(8,128)(2,1)}, bf16[256,4096]{1,0:T(8,128)(2,1)}, bf16[16,224,256]{2,1,0:T(8,128)(2,1)}, bf16[16,224,256]{2,1,0:T(8,128)(2,1)}, bf16[18,256,256]{2,1,0:T(8,128)(2,1)}) custom-call(s32[32]{0:T(128)} %reshape.33.corner_ref, bf16[32,32,256]{2,1,0:T(8,128)(2,1)} %tl_ref.1, bf16[16,32,256]{2,1,0:T(8,128)(2,1)} %copy-done.11, ...), custom_call_target="tpu_custom_call" | custom-call | flops 11299999744 | bytes 14680064 | tf_op jit(solution)/shard_map/forward/pallas_call | solution.py:159
  66.5 22.8 %back.1 = (bf16[16,224,256]{2,1,0:T(8,128)(2,1)}, bf16[9,256,256]{2,1,0:T(8,128)(2,1)}, bf16[9,256,256]{2,1,0:T(8,128)(2,1)}) custom-call(s32[17]{0:T(128)} %get-tuple-element.19.meta_ref, bf16[16,224,256]{2,1,0:T(8,128)(2,1)} %copy-done.2, bf16[16,224,256]{2,1,0:T(8,128)(2,1)} %get-tuple-element.21.first_ref.next_ref, ...), custom_call_target="tpu_custom_call" | custom-call | flops 14000000000 | bytes 16777216 | tf_op jit(solution)/shard_map/back/pallas_call | solution.py:274
  89.3 1.6 broadcast_select_fusion.2
  91.0 2.8 %collective-permute-done.5 = bf16[9,256,256]{2,1,0:T(8,128)(2,1)S(1)} collective-permute-done((bf16[9,256,256]{2,1,0:T(8,128)(2,1)S(1)}, bf16[9,256,256]{2,1,0:T(8,128)(2,1)S(1)}, u32[]{:S(2)}, u32[]{:S(2)}) %collective-permute-start.5) | collective-permute-done | bytes 1179680 | tf_op jit(solution)/shard_map/ppermute | solution.py:389
  95.6 10.8 %all-to-all-start.2 = ((bf16[64,36,256]{2,1,0:T(8,128)(2,1)}), bf16[64,36,256]{2,1,0:T(8,128)(2,1)S(1)}, u32[]{:S(2)}, u32[]{:S(2)}) async-start(bf16[64,36,256]{2,1,0:T(8,128)(2,1)} %reshape.35), calls=%async_computation.2 | async-start | bytes 2621440 | tf_op jit(solution)/shard_map/all_to_all | solution.py:395
  107.1 12.8 %spread.1 = (f32[32,32,256]{2,1,0:T(8,128)}, bf16[32,32,256]{2,1,0:T(8,128)(2,1)}, bf16[32,32,256]{2,1,0:T(8,128)(2,1)}, bf16[32,32,256]{2,1,0:T(8,128)(2,1)}) custom-call(s32[32]{0:T(128)} %reshape.33.corner_ref, bf16[16,224,256]{2,1,0:T(8,128)(2,1)} %get-tuple-element.28.p_ref, f32[16,32]{1,0:T(8,128)} %select_maximum_fusion.off_ref, ...), custom_call_target="tpu_custom_call" | custom-call | flops 7000000000 | bytes 6291456 | tf_op jit(solution)/shard_map/spread/pallas_call | solution.py:362
  119.9 3.5 %collective-permute-start.7 = (bf16[32,32,256]{2,1,0:T(8,128)(2,1)}, bf16[32,32,256]{2,1,0:T(8,128)(2,1)S(1)}, u32[]{:S(2)}, u32[]{:S(2)}) collective-permute-start(bf16[32,32,256]{2,1,0:T(8,128)(2,1)} %get-tuple-element.32), channel_id=1, source_target_pairs={{0,16},{16,32},{32,48},{48,64},{64,80},{80,96},{96,112},{1,17},{17... | collective-permute-start | bytes 1572872 | tf_op jit(solution)/shard_map/ppermute | solution.py:23
  123.3 4.1 %all-to-all-done.2 = bf16[64,36,256]{2,1,0:T(8,128)(2,1)S(1)} async-done(((bf16[64,36,256]{2,1,0:T(8,128)(2,1)}), bf16[64,36,256]{2,1,0:T(8,128)(2,1)S(1)}, u32[]{:S(2)}, u32[]{:S(2)}) %all-to-all-start.2) | async-done | bytes 1179680 | tf_op jit(solution)/shard_map/all_to_all | solution.py:395
  128.8 5.8 %all-to-all-start.3 = ((bf16[64,36,256]{2,1,0:T(8,128)(2,1)}), bf16[64,36,256]{2,1,0:T(8,128)(2,1)S(1)}, u32[]{:S(2)}, u32[]{:S(2)}) async-start(bf16[64,36,256]{2,1,0:T(8,128)(2,1)} %broadcast_in_dim.16), calls=%async_computation.3 | async-start | bytes 2621440 | tf_op jit(solution)/shard_map/all_to_all | solution.py:395
  134.7 4.1 %collective-permute-start.6 = (bf16[32,32,256]{2,1,0:T(8,128)(2,1)S(1)}, bf16[32,32,256]{2,1,0:T(8,128)(2,1)S(1)}, u32[]{:S(2)}, u32[]{:S(2)}) collective-permute-start(bf16[32,32,256]{2,1,0:T(8,128)(2,1)S(1)} %copy-done.9), channel_id=1, source_target_pairs={{0,16},{16,32},{32,48},{48,64},{64,80},{80,96},{96,112},{1,17},{17... | collective-permute-start | bytes 1572872 | tf_op jit(solution)/shard_map/ppermute | solution.py:23
  139.8 3.9 %collective-permute-start.8 = (bf16[32,32,256]{2,1,0:T(8,128)(2,1)}, bf16[32,32,256]{2,1,0:T(8,128)(2,1)}, u32[]{:S(2)}, u32[]{:S(2)}) collective-permute-start(bf16[32,32,256]{2,1,0:T(8,128)(2,1)} %add_convert_fusion.1), channel_id=1, source_target_pairs={{0,1},{1,2},{2,3},{3,4},{4,5},{5,6},{6,7},{7,8},{8,9},{9,10},{10,1... | collective-permute-start | bytes 1572872 | tf_op jit(solution)/shard_map/ppermute | solution.py:23
  143.7 12.3 %collective-permute-done.6 = bf16[32,32,256]{2,1,0:T(8,128)(2,1)S(1)} collective-permute-done((bf16[32,32,256]{2,1,0:T(8,128)(2,1)S(1)}, bf16[32,32,256]{2,1,0:T(8,128)(2,1)S(1)}, u32[]{:S(2)}, u32[]{:S(2)}) %collective-permute-start.6) | collective-permute-done | bytes 524320 | tf_op jit(solution)/shard_map/ppermute | solution.py:23
  156.5 2.7 %collective-permute-done.8 = bf16[32,32,256]{2,1,0:T(8,128)(2,1)} collective-permute-done((bf16[32,32,256]{2,1,0:T(8,128)(2,1)}, bf16[32,32,256]{2,1,0:T(8,128)(2,1)}, u32[]{:S(2)}, u32[]{:S(2)}) %collective-permute-start.8) | collective-permute-done | bytes 524320 | tf_op jit(solution)/shard_map/ppermute | solution.py:23
  159.2 1.5 collective-permute-start.9
  160.7 2.2 %convert_add_fusion = f32[32,32,256]{2,1,0:T(8,128)} fusion(f32[32,32,256]{2,1,0:T(8,128)S(1)} %convert_add_fusion.1, bf16[32,32,256]{2,1,0:T(8,128)(2,1)} %collective-permute-done.8), kind=kLoop, calls=%fused_computation.5 | loop fusion | flops 524288 | bytes 2621440 | tf_op jit(solution)/shard_map/add | solution.py:443
  163.3 2.5 %maximum_convert_fusion = f32[2,3,3,256,256]{4,3,2,1,0:T(8,128)} fusion(bf16[1,3,3,256,256]{4,3,2,1,0:T(8,128)(2,1)S(1)} %bitcast.12, bf16[1,3,3,256,256]{4,3,2,1,0:T(8,128)(2,1)S(1)} %bitcast.11), kind=kLoop, calls=%fused_computation | loop fusion | flops 2359296 | bytes 7077888 | tf_op jit(solution)/shard_map/convert_element_type | solution.py:445
  (60 shorter events, 16.4 us)
Async XLA Ops:
  0.6 16.2 %copy-start.4 = (bf16[8,14,14,256]{3,0,2,1:T(8,128)(2,1)S(1)}, bf16[8,14,14,256]{3,0,2,1:T(8,128)(2,1)}, u32[]{:S(2)}) copy-start(bf16[8,14,14,256]{3,0,2,1:T(8,128)(2,1)} %param.13) | copy-start | bytes 2408452
  2.0 15.9 %all-to-all-start = ((s32[16,1,1]{2,1,0:T(1,128)}), s32[16,1,1]{2,1,0:T(1,128)S(1)}, u32[]{:S(2)}, u32[]{:S(2)}) async-start(s32[16,1,1]{2,1,0:T(1,128)} %broadcast_in_dim.7), calls=%async_computation | async-start | bytes 16384 | tf_op jit(solution)/shard_map/all_to_all | solution.py:409
  9.5 33.8 %collective-permute-start.2 = (bf16[32,32,256]{2,1,0:T(8,128)(2,1)}, bf16[32,32,256]{2,1,0:T(8,128)(2,1)S(1)}, u32[]{:S(2)}, u32[]{:S(2)}) collective-permute-start(bf16[32,32,256]{2,1,0:T(8,128)(2,1)} %tl_ref.1), channel_id=1, source_target_pairs={{16,0},{32,16},{48,32},{64,48},{80,64},{96,80},{112,96},{17,1},{33... | collective-permute-start | bytes 1572872 | tf_op jit(solution)/shard_map/ppermute | solution.py:23
  13.5 18.4 %collective-permute-start.1 = (bf16[16,32,256]{2,1,0:T(8,128)(2,1)S(1)}, bf16[16,32,256]{2,1,0:T(8,128)(2,1)S(1)}, u32[]{:S(2)}, u32[]{:S(2)}) collective-permute-start(bf16[16,32,256]{2,1,0:T(8,128)(2,1)S(1)} %get-tuple-element.38), channel_id=1, source_target_pairs={{1,0},{2,1},{3,2},{4,3},{5,4},{6,5},{7,6},{8,7},{9,8},{10,9},{11,1... | collective-permute-start | bytes 786440 | tf_op jit(solution)/shard_map/ppermute | solution.py:23
  14.8 19.2 %collective-permute-start = (bf16[16,32,256]{2,1,0:T(8,128)(2,1)S(1)}, bf16[16,32,256]{2,1,0:T(8,128)(2,1)S(1)}, u32[]{:S(2)}, u32[]{:S(2)}) collective-permute-start(bf16[16,32,256]{2,1,0:T(8,128)(2,1)S(1)} %get-tuple-element.39), channel_id=1, source_target_pairs={{1,0},{2,1},{3,2},{4,3},{5,4},{6,5},{7,6},{8,7},{9,8},{10,9},{11,1... | collective-permute-start | bytes 786440 | tf_op jit(solution)/shard_map/ppermute | solution.py:23
  21.5 9.5 %copy-start.6 = (s32[16,28]{1,0:T(8,128)S(1)}, s32[16,28]{1,0:T(8,128)}, u32[]{:S(2)}) copy-start(s32[16,28]{1,0:T(8,128)} %param.11) | copy-start | bytes 5380
  21.5 9.6 %copy-start.13 = (s32[16,2]{0,1:T(2,128)S(1)}, s32[16,2]{0,1:T(2,128)}, u32[]{:S(2)}) copy-start(s32[16,2]{0,1:T(2,128)} %param.10) | copy-start | bytes 388
  21.5 14.5 %copy-start.7 = (pred[16]{0:T(512)(128)(4,1)S(1)}, pred[16]{0:T(512)(128)(4,1)}, u32[]{:S(2)}) copy-start(pred[16]{0:T(512)(128)(4,1)} %constant.37.clone.1) | copy-start | bytes 52
  21.5 43.7 %all-to-all-start.1 = ((bf16[16,224,256]{2,1,0:T(8,128)(2,1)}), bf16[16,224,256]{2,1,0:T(8,128)(2,1)S(1)}, u32[]{:S(2)}, u32[]{:S(2)}) async-start(bf16[16,224,256]{2,1,0:T(8,128)(2,1)} %bitcast.13), calls=%async_computation.1 | async-start | bytes 3670016 | tf_op jit(solution)/shard_map/all_to_all | solution.py:416
  31.9 11.4 %copy-start.10 = (bf16[16,32,256]{2,1,0:T(8,128)(2,1)}, bf16[16,32,256]{2,1,0:T(8,128)(2,1)S(1)}, u32[]{:S(2)}) copy-start(bf16[16,32,256]{2,1,0:T(8,128)(2,1)S(1)} %collective-permute-done.1.tr1_ref) | copy-start | bytes 786436
  31.9 8.6 %collective-permute-start.4 = (bf16[16,32,256]{2,1,0:T(8,128)(2,1)S(1)}, bf16[16,32,256]{2,1,0:T(8,128)(2,1)S(1)}, u32[]{:S(2)}, u32[]{:S(2)}) collective-permute-start(bf16[16,32,256]{2,1,0:T(8,128)(2,1)S(1)} %collective-permute-done.1.tr1_ref), channel_id=1, source_target_pairs={{16,0},{32,16},{48,32},{64,48},{80,64},{96,80},{112,96},{17,1},{33... | collective-permute-start | bytes 786440 | tf_op jit(solution)/shard_map/ppermute | solution.py:23
  34.0 9.3 %copy-start.11 = (bf16[16,32,256]{2,1,0:T(8,128)(2,1)}, bf16[16,32,256]{2,1,0:T(8,128)(2,1)S(1)}, u32[]{:S(2)}) copy-start(bf16[16,32,256]{2,1,0:T(8,128)(2,1)S(1)} %collective-permute-done.tr0_ref) | copy-start | bytes 786436
  34.0 9.3 %collective-permute-start.3 = (bf16[16,32,256]{2,1,0:T(8,128)(2,1)S(1)}, bf16[16,32,256]{2,1,0:T(8,128)(2,1)}, u32[]{:S(2)}, u32[]{:S(2)}) collective-permute-start(bf16[16,32,256]{2,1,0:T(8,128)(2,1)S(1)} %collective-permute-done.tr0_ref), channel_id=1, source_target_pairs={{16,0},{32,16},{48,32},{64,48},{80,64},{96,80},{112,96},{17,1},{33... | collective-permute-start | bytes 786440 | tf_op jit(solution)/shard_map/ppermute | solution.py:23
  89.3 4.5 %copy-start = (bf16[9,256,256]{2,1,0:T(8,128)(2,1)S(1)}, bf16[9,256,256]{2,1,0:T(8,128)(2,1)}, u32[]{:S(2)}) copy-start(bf16[9,256,256]{2,1,0:T(8,128)(2,1)} %get-tuple-element.26) | copy-start | bytes 3538948
  90.9 2.9 %collective-permute-start.5 = (bf16[9,256,256]{2,1,0:T(8,128)(2,1)S(1)}, bf16[9,256,256]{2,1,0:T(8,128)(2,1)S(1)}, u32[]{:S(2)}, u32[]{:S(2)}) collective-permute-start(bf16[9,256,256]{2,1,0:T(8,128)(2,1)S(1)} %broadcast_select_fusion.2), channel_id=1, source_target_pairs={{0,16},{16,0},{32,48},{48,32},{64,80},{80,64},{96,112},{112,96},{1... | collective-permute-start | bytes 3538952 | tf_op jit(solution)/shard_map/ppermute | solution.py:389
  95.6 31.9 %all-to-all-start.2 = ((bf16[64,36,256]{2,1,0:T(8,128)(2,1)}), bf16[64,36,256]{2,1,0:T(8,128)(2,1)S(1)}, u32[]{:S(2)}, u32[]{:S(2)}) async-start(bf16[64,36,256]{2,1,0:T(8,128)(2,1)} %reshape.35), calls=%async_computation.2 | async-start | bytes 2621440 | tf_op jit(solution)/shard_map/all_to_all | solution.py:395
  119.9 18.9 %collective-permute-start.7 = (bf16[32,32,256]{2,1,0:T(8,128)(2,1)}, bf16[32,32,256]{2,1,0:T(8,128)(2,1)S(1)}, u32[]{:S(2)}, u32[]{:S(2)}) collective-permute-start(bf16[32,32,256]{2,1,0:T(8,128)(2,1)} %get-tuple-element.32), channel_id=1, source_target_pairs={{0,16},{16,32},{32,48},{48,64},{64,80},{80,96},{96,112},{1,17},{17... | collective-permute-start | bytes 1572872 | tf_op jit(solution)/shard_map/ppermute | solution.py:23
  128.8 5.8 %copy-start.9 = (bf16[32,32,256]{2,1,0:T(8,128)(2,1)S(1)}, bf16[32,32,256]{2,1,0:T(8,128)(2,1)}, u32[]{:S(2)}) copy-start(bf16[32,32,256]{2,1,0:T(8,128)(2,1)} %get-tuple-element.30) | copy-start | bytes 1572868
  128.8 10.0 %copy-start.5 = (bf16[32,32,256]{2,1,0:T(8,128)(2,1)S(1)}, bf16[32,32,256]{2,1,0:T(8,128)(2,1)}, u32[]{:S(2)}) copy-start(bf16[32,32,256]{2,1,0:T(8,128)(2,1)} %get-tuple-element.31) | copy-start | bytes 1572868
  128.8 27.4 %all-to-all-start.3 = ((bf16[64,36,256]{2,1,0:T(8,128)(2,1)}), bf16[64,36,256]{2,1,0:T(8,128)(2,1)S(1)}, u32[]{:S(2)}, u32[]{:S(2)}) async-start(bf16[64,36,256]{2,1,0:T(8,128)(2,1)} %broadcast_in_dim.16), calls=%async_computation.3 | async-start | bytes 2621440 | tf_op jit(solution)/shard_map/all_to_all | solution.py:395
  134.6 21.3 %copy-start.3 = (f32[32,32,256]{2,1,0:T(8,128)S(1)}, f32[32,32,256]{2,1,0:T(8,128)}, u32[]{:S(2)}) copy-start(f32[32,32,256]{2,1,0:T(8,128)} %get-tuple-element.29) | copy-start | bytes 3145732
  134.7 21.3 %collective-permute-start.6 = (bf16[32,32,256]{2,1,0:T(8,128)(2,1)S(1)}, bf16[32,32,256]{2,1,0:T(8,128)(2,1)S(1)}, u32[]{:S(2)}, u32[]{:S(2)}) collective-permute-start(bf16[32,32,256]{2,1,0:T(8,128)(2,1)S(1)} %copy-done.9), channel_id=1, source_target_pairs={{0,16},{16,32},{32,48},{48,64},{64,80},{80,96},{96,112},{1,17},{17... | collective-permute-start | bytes 1572872 | tf_op jit(solution)/shard_map/ppermute | solution.py:23
  139.8 19.4 %collective-permute-start.8 = (bf16[32,32,256]{2,1,0:T(8,128)(2,1)}, bf16[32,32,256]{2,1,0:T(8,128)(2,1)}, u32[]{:S(2)}, u32[]{:S(2)}) collective-permute-start(bf16[32,32,256]{2,1,0:T(8,128)(2,1)} %add_convert_fusion.1), channel_id=1, source_target_pairs={{0,1},{1,2},{2,3},{3,4},{4,5},{5,6},{6,7},{7,8},{8,9},{9,10},{10,1... | collective-permute-start | bytes 1572872 | tf_op jit(solution)/shard_map/ppermute | solution.py:23
  159.2 4.0 %collective-permute-start.9 = (bf16[9,256,256]{2,1,0:T(8,128)(2,1)S(1)}, bf16[9,256,256]{2,1,0:T(8,128)(2,1)S(1)}, u32[]{:S(2)}, u32[]{:S(2)}) collective-permute-start(bf16[9,256,256]{2,1,0:T(8,128)(2,1)S(1)} %reshape.36), channel_id=1, source_target_pairs={{0,16},{16,0},{32,48},{48,32},{64,80},{80,64},{96,112},{112,96},{1... | collective-permute-start | bytes 3538952 | tf_op jit(solution)/shard_map/ppermute | solution.py:389
  (4 other events, 9.4 us)

commit v5 on v4

--- a/solution.py
+++ b/solution.py
@@ -97,21 +97,18 @@
 
 
 def forward_kernel(
-    corner_ref, tl_ref, tr0_ref, tr1_ref, bl_ref, br0_ref, br1_ref, off_ref, k_ref,
+    corner_ref, tl_ref, tr_ref, bl_ref, br_ref, off_ref, k_ref,
     a0_ref, a1_ref, g0_ref, g1_ref, t_ref, ext, places, row_w, weight, held,
 ):
     step = pl.program_id(0)
-    half = BOX // 2
 
     @pl.when(step == 0)
     def _():
         clear_edges(held, FG)
         ext[0:BOX, 0:BOX, :] = tl_ref[...]
-        ext[0:half, BOX : 2 * BOX, :] = tr0_ref[...]
-        ext[half:BOX, BOX : 2 * BOX, :] = tr1_ref[...]
+        ext[0:BOX, BOX : 2 * BOX, :] = tr_ref[...]
         ext[BOX : 2 * BOX, 0:BOX, :] = bl_ref[...]
-        ext[BOX : BOX + half, BOX : 2 * BOX, :] = br0_ref[...]
-        ext[BOX + half : 2 * BOX, BOX : 2 * BOX, :] = br1_ref[...]
+        ext[BOX : 2 * BOX, BOX : 2 * BOX, :] = br_ref[...]
         at = lax.broadcasted_iota(jnp.int32, (16, WIN), 1).astype(F32)
         row = jnp.floor((at + 0.5) * (1.0 / SPAN))
         places[0] = 4.0 * row
@@ -152,7 +149,6 @@
 
 def forward(corners, pieces, offsets, kernels):
     slots = 16
-    half = BOX // 2
     whole = lambda *shape: pl.BlockSpec(shape, lambda i, *_: (0,) * len(shape))
     columns = pl.BlockSpec((C, FG * C), lambda i, *_: (0, i))
     regions = pl.BlockSpec((FG, PIX, C), lambda i, *_: (i, 0, 0))
@@ -171,11 +167,9 @@
             grid=(slots // FG,),
             in_specs=[
                 whole(BOX, BOX, C),
-                whole(half, BOX, C),
-                whole(half, BOX, C),
                 whole(BOX, BOX, C),
-                whole(half, BOX, C),
-                whole(half, BOX, C),
+                whole(BOX, BOX, C),
+                whole(BOX, BOX, C),
                 whole(32, 16),
                 whole(18, C, C),
             ],
@@ -222,7 +216,7 @@
 
 def back_kernel(
     meta_ref, in_ref, first_ref, next_ref, g0_ref, k_ref, a1_ref, a0_ref,
-    p_ref, o1_ref, o0_ref, upper, held, acc1, acc0,
+    p_ref, keep_ref, send_ref, upper, held, acc1, acc0,
 ):
     step = pl.program_id(0)
     now = step & 1
@@ -261,8 +255,17 @@
 
     @pl.when(step == pl.num_programs(0) - 1)
     def _():
-        o1_ref[...] = acc1[...].astype(BF)
-        o0_ref[...] = acc0[...].astype(BF)
+        keeps_first = (lax.axis_index("ha") & 1) == 0
+
+        @pl.when(keeps_first)
+        def _():
+            keep_ref[...] = acc0[...].astype(BF)
+            send_ref[...] = acc1[...].astype(BF)
+
+        @pl.when(jnp.logical_not(keeps_first))
+        def _():
+            keep_ref[...] = acc1[...].astype(BF)
+            send_ref[...] = acc0[...].astype(BF)
 
 
 def back(meta, incoming, slope1, slope0, kernels, acts1, acts0):
@@ -389,14 +392,6 @@
     return lax.ppermute(x, "ha", [(i, i ^ 1) for i in range(lax.axis_size("ha"))])
 
 
-def over_chips(pieces):
-    down, across = lax.axis_size("ha"), lax.axis_size("wa")
-    groups = [[h * across + w for h in range(c, down, 2) for w in range(across)] for c in range(2)]
-    return lax.all_to_all(
-        pieces, ("ha", "wa"), 0, 0, tiled=True, axis_index_groups=groups
-    )
-
-
 def pick_layer(index, first, second):
     return jnp.where(index == 0, first, second)
 
@@ -404,19 +399,17 @@
 def local(features, counts, owner_perm, corners, offsets, kernels, cotangent):
     peers = lax.axis_size("wa")
     core = lax.axis_index("ha") % 2
-    rows = BOX // 2
-    cut = lambda x: (x[:rows], x[rows:])
     row_counts = lax.all_to_all(
         jnp.broadcast_to(counts[None], (peers, 1, 1)), "wa", 0, 0, tiled=True
     ).reshape(peers)
-    from_right = [shifted(piece, "wa", -1) for piece in cut(features)]
+    from_right = shifted(features, "wa", -1)
     below = shifted(features, "ha", -1)
     outgoing, meta = route(row_counts, owner_perm, cotangent)
-    corner = [shifted(piece, "ha", -1) for piece in from_right]
+    corner = shifted(from_right, "ha", -1)
     incoming = lax.all_to_all(
         outgoing.reshape(peers, PIX, C), "wa", split_axis=0, concat_axis=0, tiled=True
     )
-    pieces = (features, *from_right, below, *corner)
+    pieces = (features, from_right, below, corner)
     places = jnp.concatenate(
         [offsets[:, :SIDE], offsets[:, SIDE:] + (corners[:, 1:2] % 16) * 4], axis=1
     ).astype(F32)
@@ -427,18 +420,21 @@
     acts0, acts1, slope0, slope1, turned = forward(
         corners, pieces, place_cols, kernels.reshape(18, C, C)
     )
-    inner, grad1, grad0 = back(meta, incoming, slope1, slope0, turned, acts1, acts0)
-    mine = swap_cores(pick_layer(core, grad1, grad0)).astype(F32)
-    mine = (mine + pick_layer(core, grad0, grad1).astype(F32)).astype(BF)
-    chips = lax.axis_size("ha") // 2 * peers
-    parts = over_chips(mine.reshape(chips, -1, C))
+    inner, keep, send = back(meta, incoming, slope1, slope0, turned, acts1, acts0)
+    mine = (keep.astype(F32) + swap_cores(send).astype(F32)).astype(BF)
+    parts = lax.all_to_all(mine.reshape(peers, -1, C), "wa", 0, 0, tiled=True)
     tile, right, lower, corner = spread(corners, inner, places, turned)
     corner, lower = [shifted(piece, "ha", 1) for piece in (corner, lower)]
+    part = jnp.sum(parts.astype(F32), axis=0).astype(BF)
+    count = lax.axis_size("ha")
+    total = part.astype(F32)
+    for hop in range(2, count, 2):
+        moved = lax.ppermute(part, "ha", [(i, (i + hop) % count) for i in range(count)])
+        total = total + moved.astype(F32)
+    whole = jnp.broadcast_to(total.astype(BF)[None], (peers, *total.shape))
+    mine = lax.all_to_all(whole, "wa", 0, 0, tiled=True).reshape(9, C, C)
     side = shifted((right.astype(F32) + corner.astype(F32)).astype(BF), "wa", 1)
     tile = tile + lower.astype(F32)
-    total = jnp.sum(parts.astype(F32), axis=0).astype(BF)
-    whole = jnp.broadcast_to(total[None], (chips, *total.shape))
-    mine = over_chips(whole).reshape(9, C, C)
     mine, tile, side = lax.optimization_barrier((mine, tile, side))
     tile = tile + side.astype(F32)
     other = swap_cores(mine)

time: 169 us -> 181 us (1.071)
  waiting for transfers between devices: 28.8 us -> 53.3 us
  starting transfers between devices: 56.3 us -> 46.5 us
    all_to_all x2, waiting for transfers between devices: 4.11 us -> 18.2 us  [the longest x1 18.2 us: local(): parts = lax.all_to_all(mine.reshape(peers, -1, C), 'wa', 0, 0, tiled=True)]
    ppermute x8 -> x6, waiting for transfers between devices: 21.5 us -> 28.2 us  [shifted(): lax.ppermute(value, axis, [(source, source + steps) for source in range(f...]
    all_to_all x2, starting transfers between devices: 16.7 us -> 10.8 us  [the longest x1 6.92 us: local(): parts = lax.all_to_all(mine.reshape(peers, -1, C), 'wa', 0, 0, tiled=True)]
    all_to_all x1, starting transfers between devices: 9.47 us -> 4.3 us  [local(): lax.all_to_all(outgoing.reshape(peers, PIX, C), 'wa', split_axis=0, conca...]
    ppermute x0 -> x3, starting transfers between devices: none -> 4.23 us  [local(): lax.ppermute(part, 'ha', [(i, (i + hop) % count) for i in range(count)])]
    all_to_all x1, waiting for transfers between devices: 0.01 us -> 3.42 us  [local(): lax.all_to_all(jnp.broadcast_to(counts[None], (peers, 1, 1)), 'wa', 0, 0,...]
    ppermute x8 -> x6, starting transfers between devices: 21 us -> 18.8 us  [shifted(): lax.ppermute(value, axis, [(source, source + steps) for source in range(f...]
    convert_element_type x1 -> x2, other arithmetic: 0.53 us -> 2.68 us  [the longest x1 2.63 us: local(): mine = (keep.astype(F32) + swap_cores(send).astype(F32)).astype(BF)]
  transfers between devices with their start and end apart: 14 -> 15, of which waited for: 7 -> 7; matrix products, arithmetic and copies ran while one was open for 7% -> 6% of each run, Pallas kernels for 22% -> 21%
where the time goes in v5:
time: 181 us; the launch traced here: 179 us
  Pallas kernels  59.5 us (33%)
  waiting for transfers between devices  53.3 us (29%)
  starting transfers between devices  46.5 us (26%)
  other arithmetic  10.5 us (6%)
  local copies, waits for them, and re-layouts  7.35 us (4%)
    ppermute x6, waiting for transfers between devices, shifted(): lax.ppermute(value, axis, [(source, source + steps) for source in range(f...  28.2 us
    pallas_call x1, Pallas kernels, back(): pl.pallas_call(back_kernel, name='back', out_shape=[jax.ShapeDtypeStruct(...  22.9 us
    pallas_call x1, Pallas kernels, forward(): pl.pallas_call(forward_kernel, name='forward', out_shape=[jax.ShapeDtypeS...  21.2 us
    ppermute x6, starting transfers between devices, shifted(): lax.ppermute(value, axis, [(source, source + steps) for source in range(f...  18.8 us
    all_to_all x1, waiting for transfers between devices, local(): parts = lax.all_to_all(mine.reshape(peers, -1, C), 'wa', 0, 0, tiled=True)  18.2 us
    pallas_call x1, Pallas kernels, spread(): pl.pallas_call(spread_kernel, name='spread', out_shape=[piece(F32), piece...  12.8 us
    all_to_all x1, starting transfers between devices, local(): lax.all_to_all(jnp.broadcast_to(counts[None], (peers, 1, 1)), 'wa', 0, 0,...  8.05 us
    all_to_all x1, starting transfers between devices, local(): parts = lax.all_to_all(mine.reshape(peers, -1, C), 'wa', 0, 0, tiled=True)  6.92 us
  transfers between devices with their start and end apart: 15, of which 7 were waited for; matrix products, arithmetic and copies ran while one was open for 6% of the time, Pallas kernels for 21%

profile of v5, /device:TPU:1, one launch (start us, length us, event | category | flops | bytes accessed | tf_op | source)
XLA Modules:
  0.0 178.7 jit_solution(17669265127210019019)
XLA Ops:
  1.9 3.3 %collective-permute-start.1 = (bf16[32,32,256]{2,1,0:T(8,128)(2,1)}, bf16[32,32,256]{2,1,0:T(8,128)(2,1)S(1)}, u32[]{:S(2)}, u32[]{:S(2)}) collective-permute-start(bf16[32,32,256]{2,1,0:T(8,128)(2,1)} %tl_ref.1), channel_id=1, source_target_pairs={{16,0},{32,16},{48,32},{64,48},{80,64},{96,80},{112,96},{17,1},{33... | collective-permute-start | bytes 1572872 | tf_op jit(solution)/shard_map/ppermute | solution.py:23
  6.5 8.0 %all-to-all-start = ((s32[16,1,1]{2,1,0:T(1,128)}), s32[16,1,1]{2,1,0:T(1,128)S(1)}, u32[]{:S(2)}, u32[]{:S(2)}) async-start(s32[16,1,1]{2,1,0:T(1,128)} %broadcast_in_dim.7), calls=%async_computation | async-start | bytes 16384 | tf_op jit(solution)/shard_map/all_to_all | solution.py:402
  15.2 2.2 %copy.13.x_ref = bf16[8,14,14,256]{3,2,1,0:T(8,128)(2,1)} copy(bf16[8,14,14,256]{3,0,2,1:T(8,128)(2,1)} %param.13) | data formatting | bytes 1605632 | tf_op args[6]
  17.5 3.4 %all-to-all-done = s32[16,1,1]{2,1,0:T(1,128)S(1)} async-done(((s32[16,1,1]{2,1,0:T(1,128)}), s32[16,1,1]{2,1,0:T(1,128)S(1)}, u32[]{:S(2)}, u32[]{:S(2)}) %all-to-all-start) | async-done | bytes 96 | tf_op jit(solution)/shard_map/all_to_all | solution.py:402
  21.8 2.7 %route.1 = (bf16[16,14,16,256]{3,2,1,0:T(8,128)(2,1)}, s32[17]{0:T(128)}) custom-call(s32[16]{0:T(128)} %reduce.1.count_ref, s32[1,16]{1,0:T(1,128)} %perm_ref.1, bf16[8,14,14,256]{3,2,1,0:T(8,128)(2,1)} %copy.13.x_ref), custom_call_target="tpu_custom_call" | custom-call | bytes 4194304 | tf_op jit(solution)/shard_map/route/pallas_call | solution.py:83
  24.5 4.3 %all-to-all-start.1 = ((bf16[16,224,256]{2,1,0:T(8,128)(2,1)}), bf16[16,224,256]{2,1,0:T(8,128)(2,1)S(1)}, u32[]{:S(2)}, u32[]{:S(2)}) async-start(bf16[16,224,256]{2,1,0:T(8,128)(2,1)} %bitcast.17), calls=%async_computation.1 | async-start | bytes 3670016 | tf_op jit(solution)/shard_map/all_to_all | solution.py:409
  28.8 3.8 %collective-permute-start.2 = (bf16[32,32,256]{2,1,0:T(8,128)(2,1)S(1)}, bf16[32,32,256]{2,1,0:T(8,128)(2,1)S(1)}, u32[]{:S(2)}, u32[]{:S(2)}) collective-permute-start(bf16[32,32,256]{2,1,0:T(8,128)(2,1)S(1)} %collective-permute-done.tr_ref), channel_id=1, source_target_pairs={{16,0},{32,16},{48,32},{64,48},{80,64},{96,80},{112,96},{17,1},{33... | collective-permute-start | bytes 1572872 | tf_op jit(solution)/shard_map/ppermute | solution.py:23
  34.3 7.1 %collective-permute-done.2.br_ref = bf16[32,32,256]{2,1,0:T(8,128)(2,1)S(1)} collective-permute-done((bf16[32,32,256]{2,1,0:T(8,128)(2,1)S(1)}, bf16[32,32,256]{2,1,0:T(8,128)(2,1)S(1)}, u32[]{:S(2)}, u32[]{:S(2)}) %collective-permute-start.2) | collective-permute-done | bytes 524320 | tf_op jit(solution)/shard_map/ppermute | solution.py:23
  42.1 21.2 %forward.1 = (bf16[256,4096]{1,0:T(8,128)(2,1)}, bf16[256,4096]{1,0:T(8,128)(2,1)}, bf16[16,224,256]{2,1,0:T(8,128)(2,1)}, bf16[16,224,256]{2,1,0:T(8,128)(2,1)}, bf16[18,256,256]{2,1,0:T(8,128)(2,1)}) custom-call(s32[32]{0:T(128)} %reshape.33.corner_ref, bf16[32,32,256]{2,1,0:T(8,128)(2,1)} %tl_ref.1, bf16[32,32,256]{2,1,0:T(8,128)(2,1)} %copy-done.5, ...), custom_call_target="tpu_custom_call" | custom-call | flops 11299999744 | bytes 14680064 | tf_op jit(solution)/shard_map/forward/pallas_call | solution.py:155
  64.6 22.9 %back.1 = (bf16[16,224,256]{2,1,0:T(8,128)(2,1)}, bf16[9,256,256]{2,1,0:T(8,128)(2,1)}, bf16[9,256,256]{2,1,0:T(8,128)(2,1)}) custom-call(s32[17]{0:T(128)} %get-tuple-element.19.meta_ref, bf16[16,224,256]{2,1,0:T(8,128)(2,1)} %copy-done, bf16[16,224,256]{2,1,0:T(8,128)(2,1)} %get-tuple-element.21.first_ref.next_ref, ...), custom_call_target="tpu_custom_call" | custom-call | flops 14000000000 | bytes 16777216 | tf_op jit(solution)/shard_map/back/pallas_call | solution.py:277
  87.5 3.0 %collective-permute-done.3 = bf16[9,256,256]{2,1,0:T(8,128)(2,1)S(1)} collective-permute-done((bf16[9,256,256]{2,1,0:T(8,128)(2,1)}, bf16[9,256,256]{2,1,0:T(8,128)(2,1)S(1)}, u32[]{:S(2)}, u32[]{:S(2)}) %collective-permute-start.3) | collective-permute-done | bytes 1179680 | tf_op jit(solution)/shard_map/ppermute | solution.py:392
  90.5 2.6 %add_convert_fusion = bf16[9,256,256]{2,1,0:T(8,128)(2,1)} fusion(bf16[9,256,256]{2,1,0:T(8,128)(2,1)S(1)} %collective-permute-done.3, bf16[9,256,256]{2,1,0:T(8,128)(2,1)} %get-tuple-element.26), kind=kLoop, calls=%fused_computation.1 | loop fusion | flops 2359296 | bytes 3538944 | tf_op jit(solution)/shard_map/convert_element_type | solution.py:424
  93.2 6.9 %all-to-all-start.2 = ((bf16[16,144,256]{2,1,0:T(8,128)(2,1)}), bf16[16,144,256]{2,1,0:T(8,128)(2,1)S(1)}, u32[]{:S(2)}, u32[]{:S(2)}) async-start(bf16[16,144,256]{2,1,0:T(8,128)(2,1)} %bitcast.6), calls=%async_computation.2 | async-start | bytes 2359296 | tf_op jit(solution)/shard_map/all_to_all | solution.py:425
  100.8 18.2 %all-to-all-done.2 = bf16[16,144,256]{2,1,0:T(8,128)(2,1)S(1)} async-done(((bf16[16,144,256]{2,1,0:T(8,128)(2,1)}), bf16[16,144,256]{2,1,0:T(8,128)(2,1)S(1)}, u32[]{:S(2)}, u32[]{:S(2)}) %all-to-all-start.2) | async-done | bytes 1179680 | tf_op jit(solution)/shard_map/all_to_all | solution.py:425
  119.6 3.0 %collective-permute-start.5 = (bf16[144,256]{1,0:T(8,128)(2,1)S(1)}, bf16[144,256]{1,0:T(8,128)(2,1)S(1)}, u32[]{:S(2)}, u32[]{:S(2)}) collective-permute-start(bf16[144,256]{1,0:T(8,128)(2,1)S(1)} %reduce_sum.12), channel_id=1, source_target_pairs={{0,64},{16,80},{32,96},{48,112},{64,0},{80,16},{96,32},{112,48},{1... | collective-permute-start | bytes 221192 | tf_op jit(solution)/shard_map/ppermute | solution.py:432
  123.4 12.8 %spread.1 = (f32[32,32,256]{2,1,0:T(8,128)}, bf16[32,32,256]{2,1,0:T(8,128)(2,1)}, bf16[32,32,256]{2,1,0:T(8,128)(2,1)}, bf16[32,32,256]{2,1,0:T(8,128)(2,1)}) custom-call(s32[32]{0:T(128)} %reshape.33.corner_ref, bf16[16,224,256]{2,1,0:T(8,128)(2,1)} %get-tuple-element.28.p_ref, f32[16,32]{1,0:T(8,128)} %select_maximum_fusion.off_ref, ...), custom_call_target="tpu_custom_call" | custom-call | flops 7000000000 | bytes 6291456 | tf_op jit(solution)/shard_map/spread/pallas_call | solution.py:365
  136.2 4.1 %collective-permute-start.8 = (bf16[32,32,256]{2,1,0:T(8,128)(2,1)}, bf16[32,32,256]{2,1,0:T(8,128)(2,1)S(1)}, u32[]{:S(2)}, u32[]{:S(2)}) collective-permute-start(bf16[32,32,256]{2,1,0:T(8,128)(2,1)} %get-tuple-element.32), channel_id=1, source_target_pairs={{0,16},{16,32},{32,48},{48,64},{64,80},{80,96},{96,112},{1,17},{17... | collective-permute-start | bytes 1572872 | tf_op jit(solution)/shard_map/ppermute | solution.py:23
  141.5 3.8 %all-to-all-start.3 = ((bf16[16,144,256]{2,1,0:T(8,128)(2,1)}), bf16[16,144,256]{2,1,0:T(8,128)(2,1)S(1)}, u32[]{:S(2)}, u32[]{:S(2)}) async-start(bf16[16,144,256]{2,1,0:T(8,128)(2,1)} %broadcast_in_dim.16), calls=%async_computation.3 | async-start | bytes 2359296 | tf_op jit(solution)/shard_map/all_to_all | solution.py:435
  145.3 2.1 %collective-permute-start.7 = (bf16[32,32,256]{2,1,0:T(8,128)(2,1)S(1)}, bf16[32,32,256]{2,1,0:T(8,128)(2,1)S(1)}, u32[]{:S(2)}, u32[]{:S(2)}) collective-permute-start(bf16[32,32,256]{2,1,0:T(8,128)(2,1)S(1)} %copy-done.7), channel_id=1, source_target_pairs={{0,16},{16,32},{32,48},{48,64},{64,80},{80,96},{96,112},{1,17},{17... | collective-permute-start | bytes 1572872 | tf_op jit(solution)/shard_map/ppermute | solution.py:23
  147.6 4.2 %collective-permute-start.9 = (bf16[32,32,256]{2,1,0:T(8,128)(2,1)S(1)}, bf16[32,32,256]{2,1,0:T(8,128)(2,1)}, u32[]{:S(2)}, u32[]{:S(2)}) collective-permute-start(bf16[32,32,256]{2,1,0:T(8,128)(2,1)S(1)} %add_convert_fusion.1), channel_id=1, source_target_pairs={{0,1},{1,2},{2,3},{3,4},{4,5},{5,6},{6,7},{7,8},{8,9},{9,10},{10,1... | collective-permute-start | bytes 1572872 | tf_op jit(solution)/shard_map/ppermute | solution.py:23
  151.8 1.7 collective-permute-done.7
  153.7 19.5 %collective-permute-done.9 = bf16[32,32,256]{2,1,0:T(8,128)(2,1)} collective-permute-done((bf16[32,32,256]{2,1,0:T(8,128)(2,1)S(1)}, bf16[32,32,256]{2,1,0:T(8,128)(2,1)}, u32[]{:S(2)}, u32[]{:S(2)}) %collective-permute-start.9) | collective-permute-done | bytes 524320 | tf_op jit(solution)/shard_map/ppermute | solution.py:23
  173.6 2.2 %convert_add_fusion = f32[32,32,256]{2,1,0:T(8,128)} fusion(f32[32,32,256]{2,1,0:T(8,128)S(1)} %convert_add_fusion.1, bf16[32,32,256]{2,1,0:T(8,128)(2,1)} %collective-permute-done.9), kind=kLoop, calls=%fused_computation.4 | loop fusion | flops 524288 | bytes 2621440 | tf_op jit(solution)/shard_map/add | solution.py:439
  176.2 2.5 %maximum_convert_fusion = f32[2,3,3,256,256]{4,3,2,1,0:T(8,128)} fusion(bf16[1,3,3,256,256]{4,3,2,1,0:T(8,128)(2,1)S(1)} %bitcast.14, bf16[1,3,3,256,256]{4,3,2,1,0:T(8,128)(2,1)S(1)} %bitcast.13), kind=kLoop, calls=%fused_computation | loop fusion | flops 2359296 | bytes 7077888 | tf_op jit(solution)/shard_map/convert_element_type | solution.py:441
  (51 shorter events, 11.6 us)
Async XLA Ops:
  0.6 28.2 %collective-permute-start = (bf16[32,32,256]{2,1,0:T(8,128)(2,1)}, bf16[32,32,256]{2,1,0:T(8,128)(2,1)S(1)}, u32[]{:S(2)}, u32[]{:S(2)}) collective-permute-start(bf16[32,32,256]{2,1,0:T(8,128)(2,1)} %tl_ref.1), channel_id=1, source_target_pairs={{1,0},{2,1},{3,2},{4,3},{5,4},{6,5},{7,6},{8,7},{9,8},{10,9},{11,1... | collective-permute-start | bytes 1572872 | tf_op jit(solution)/shard_map/ppermute | solution.py:23
  1.9 32.3 %collective-permute-start.1 = (bf16[32,32,256]{2,1,0:T(8,128)(2,1)}, bf16[32,32,256]{2,1,0:T(8,128)(2,1)S(1)}, u32[]{:S(2)}, u32[]{:S(2)}) collective-permute-start(bf16[32,32,256]{2,1,0:T(8,128)(2,1)} %tl_ref.1), channel_id=1, source_target_pairs={{16,0},{32,16},{48,32},{64,48},{80,64},{96,80},{112,96},{17,1},{33... | collective-permute-start | bytes 1572872 | tf_op jit(solution)/shard_map/ppermute | solution.py:23
  6.5 14.4 %all-to-all-start = ((s32[16,1,1]{2,1,0:T(1,128)}), s32[16,1,1]{2,1,0:T(1,128)S(1)}, u32[]{:S(2)}, u32[]{:S(2)}) async-start(s32[16,1,1]{2,1,0:T(1,128)} %broadcast_in_dim.7), calls=%async_computation | async-start | bytes 16384 | tf_op jit(solution)/shard_map/all_to_all | solution.py:402
  24.5 8.2 %copy-start.3 = (s32[16,28]{1,0:T(8,128)S(1)}, s32[16,28]{1,0:T(8,128)}, u32[]{:S(2)}) copy-start(s32[16,28]{1,0:T(8,128)} %param.11) | copy-start | bytes 5380
  24.5 8.3 %copy-start.9 = (s32[16,2]{0,1:T(2,128)S(1)}, s32[16,2]{0,1:T(2,128)}, u32[]{:S(2)}) copy-start(s32[16,2]{0,1:T(2,128)} %param.10) | copy-start | bytes 388
  24.5 9.0 %copy-start.4 = (pred[16]{0:T(512)(128)(4,1)S(1)}, pred[16]{0:T(512)(128)(4,1)}, u32[]{:S(2)}) copy-start(pred[16]{0:T(512)(128)(4,1)} %constant.32.clone.1) | copy-start | bytes 52
  24.5 38.8 %all-to-all-start.1 = ((bf16[16,224,256]{2,1,0:T(8,128)(2,1)}), bf16[16,224,256]{2,1,0:T(8,128)(2,1)S(1)}, u32[]{:S(2)}, u32[]{:S(2)}) async-start(bf16[16,224,256]{2,1,0:T(8,128)(2,1)} %bitcast.17), calls=%async_computation.1 | async-start | bytes 3670016 | tf_op jit(solution)/shard_map/all_to_all | solution.py:409
  28.8 12.5 %copy-start.5 = (bf16[32,32,256]{2,1,0:T(8,128)(2,1)}, bf16[32,32,256]{2,1,0:T(8,128)(2,1)S(1)}, u32[]{:S(2)}) copy-start(bf16[32,32,256]{2,1,0:T(8,128)(2,1)S(1)} %collective-permute-done.tr_ref) | copy-start | bytes 1572868
  28.8 12.5 %collective-permute-start.2 = (bf16[32,32,256]{2,1,0:T(8,128)(2,1)S(1)}, bf16[32,32,256]{2,1,0:T(8,128)(2,1)S(1)}, u32[]{:S(2)}, u32[]{:S(2)}) collective-permute-start(bf16[32,32,256]{2,1,0:T(8,128)(2,1)S(1)} %collective-permute-done.tr_ref), channel_id=1, source_target_pairs={{16,0},{32,16},{48,32},{64,48},{80,64},{96,80},{112,96},{17,1},{33... | collective-permute-start | bytes 1572872 | tf_op jit(solution)/shard_map/ppermute | solution.py:23
  34.3 7.1 %copy-start.6 = (bf16[32,32,256]{2,1,0:T(8,128)(2,1)}, bf16[32,32,256]{2,1,0:T(8,128)(2,1)S(1)}, u32[]{:S(2)}) copy-start(bf16[32,32,256]{2,1,0:T(8,128)(2,1)S(1)} %collective-permute-done.1.bl_ref) | copy-start | bytes 1572868
  63.3 1.2 copy-start
  87.4 3.1 %collective-permute-start.3 = (bf16[9,256,256]{2,1,0:T(8,128)(2,1)}, bf16[9,256,256]{2,1,0:T(8,128)(2,1)S(1)}, u32[]{:S(2)}, u32[]{:S(2)}) collective-permute-start(bf16[9,256,256]{2,1,0:T(8,128)(2,1)} %get-tuple-element.27), channel_id=1, source_target_pairs={{0,16},{16,0},{32,48},{48,32},{64,80},{80,64},{96,112},{112,96},{1... | collective-permute-start | bytes 3538952 | tf_op jit(solution)/shard_map/ppermute | solution.py:392
  93.2 25.8 %all-to-all-start.2 = ((bf16[16,144,256]{2,1,0:T(8,128)(2,1)}), bf16[16,144,256]{2,1,0:T(8,128)(2,1)S(1)}, u32[]{:S(2)}, u32[]{:S(2)}) async-start(bf16[16,144,256]{2,1,0:T(8,128)(2,1)} %bitcast.6), calls=%async_computation.2 | async-start | bytes 2359296 | tf_op jit(solution)/shard_map/all_to_all | solution.py:425
  119.2 21.1 %collective-permute-start.6 = (bf16[144,256]{1,0:T(8,128)(2,1)S(1)}, bf16[144,256]{1,0:T(8,128)(2,1)S(1)}, u32[]{:S(2)}, u32[]{:S(2)}) collective-permute-start(bf16[144,256]{1,0:T(8,128)(2,1)S(1)} %reduce_sum.12), channel_id=1, source_target_pairs={{0,96},{16,112},{32,0},{48,16},{64,32},{80,48},{96,64},{112,80},{1... | collective-permute-start | bytes 221192 | tf_op jit(solution)/shard_map/ppermute | solution.py:432
  119.6 20.7 %collective-permute-start.5 = (bf16[144,256]{1,0:T(8,128)(2,1)S(1)}, bf16[144,256]{1,0:T(8,128)(2,1)S(1)}, u32[]{:S(2)}, u32[]{:S(2)}) collective-permute-start(bf16[144,256]{1,0:T(8,128)(2,1)S(1)} %reduce_sum.12), channel_id=1, source_target_pairs={{0,64},{16,80},{32,96},{48,112},{64,0},{80,16},{96,32},{112,48},{1... | collective-permute-start | bytes 221192 | tf_op jit(solution)/shard_map/ppermute | solution.py:432
  122.6 17.7 %collective-permute-start.4 = (bf16[144,256]{1,0:T(8,128)(2,1)S(1)}, bf16[144,256]{1,0:T(8,128)(2,1)S(1)}, u32[]{:S(2)}, u32[]{:S(2)}) collective-permute-start(bf16[144,256]{1,0:T(8,128)(2,1)S(1)} %reduce_sum.12), channel_id=1, source_target_pairs={{0,32},{16,48},{32,64},{48,80},{64,96},{80,112},{96,0},{112,16},{1... | collective-permute-start | bytes 221192 | tf_op jit(solution)/shard_map/ppermute | solution.py:432
  136.2 11.2 %collective-permute-start.8 = (bf16[32,32,256]{2,1,0:T(8,128)(2,1)}, bf16[32,32,256]{2,1,0:T(8,128)(2,1)S(1)}, u32[]{:S(2)}, u32[]{:S(2)}) collective-permute-start(bf16[32,32,256]{2,1,0:T(8,128)(2,1)} %get-tuple-element.32), channel_id=1, source_target_pairs={{0,16},{16,32},{32,48},{48,64},{64,80},{80,96},{96,112},{1,17},{17... | collective-permute-start | bytes 1572872 | tf_op jit(solution)/shard_map/ppermute | solution.py:23
  141.5 3.9 %copy-start.7 = (bf16[32,32,256]{2,1,0:T(8,128)(2,1)S(1)}, bf16[32,32,256]{2,1,0:T(8,128)(2,1)}, u32[]{:S(2)}) copy-start(bf16[32,32,256]{2,1,0:T(8,128)(2,1)} %get-tuple-element.30) | copy-start | bytes 1572868
  141.5 5.9 %copy-start.2 = (bf16[32,32,256]{2,1,0:T(8,128)(2,1)S(1)}, bf16[32,32,256]{2,1,0:T(8,128)(2,1)}, u32[]{:S(2)}) copy-start(bf16[32,32,256]{2,1,0:T(8,128)(2,1)} %get-tuple-element.31) | copy-start | bytes 1572868
  141.5 31.8 %all-to-all-start.3 = ((bf16[16,144,256]{2,1,0:T(8,128)(2,1)}), bf16[16,144,256]{2,1,0:T(8,128)(2,1)S(1)}, u32[]{:S(2)}, u32[]{:S(2)}) async-start(bf16[16,144,256]{2,1,0:T(8,128)(2,1)} %broadcast_in_dim.16), calls=%async_computation.3 | async-start | bytes 2359296 | tf_op jit(solution)/shard_map/all_to_all | solution.py:435
  145.3 8.2 %copy-start.1 = (f32[32,32,256]{2,1,0:T(8,128)S(1)}, f32[32,32,256]{2,1,0:T(8,128)}, u32[]{:S(2)}) copy-start(f32[32,32,256]{2,1,0:T(8,128)} %get-tuple-element.29) | copy-start | bytes 3145732
  145.3 8.2 %collective-permute-start.7 = (bf16[32,32,256]{2,1,0:T(8,128)(2,1)S(1)}, bf16[32,32,256]{2,1,0:T(8,128)(2,1)S(1)}, u32[]{:S(2)}, u32[]{:S(2)}) collective-permute-start(bf16[32,32,256]{2,1,0:T(8,128)(2,1)S(1)} %copy-done.7), channel_id=1, source_target_pairs={{0,16},{16,32},{32,48},{48,64},{64,80},{80,96},{96,112},{1,17},{17... | collective-permute-start | bytes 1572872 | tf_op jit(solution)/shard_map/ppermute | solution.py:23
  147.6 25.6 %collective-permute-start.9 = (bf16[32,32,256]{2,1,0:T(8,128)(2,1)S(1)}, bf16[32,32,256]{2,1,0:T(8,128)(2,1)}, u32[]{:S(2)}, u32[]{:S(2)}) collective-permute-start(bf16[32,32,256]{2,1,0:T(8,128)(2,1)S(1)} %add_convert_fusion.1), channel_id=1, source_target_pairs={{0,1},{1,2},{2,3},{3,4},{4,5},{5,6},{6,7},{7,8},{8,9},{9,10},{10,1... | collective-permute-start | bytes 1572872 | tf_op jit(solution)/shard_map/ppermute | solution.py:23
  173.2 2.8 %collective-permute-start.10 = (bf16[9,256,256]{2,1,0:T(8,128)(2,1)S(1)}, bf16[9,256,256]{2,1,0:T(8,128)(2,1)S(1)}, u32[]{:S(2)}, u32[]{:S(2)}) collective-permute-start(bf16[9,256,256]{2,1,0:T(8,128)(2,1)S(1)} %bitcast.15), channel_id=1, source_target_pairs={{0,16},{16,0},{32,48},{48,32},{64,80},{80,64},{96,112},{112,96},{1... | collective-permute-start | bytes 3538952 | tf_op jit(solution)/shard_map/ppermute | solution.py:392
  (1 other events, 0.8 us)

commit v6 on v5

--- a/solution.py
+++ b/solution.py
@@ -167,9 +167,9 @@
             grid=(slots // FG,),
             in_specs=[
                 whole(BOX, BOX, C),
-                whole(BOX, BOX, C),
-                whole(BOX, BOX, C),
-                whole(BOX, BOX, C),
+                pl.BlockSpec(memory_space=pltpu.VMEM),
+                pl.BlockSpec(memory_space=pltpu.VMEM),
+                pl.BlockSpec(memory_space=pltpu.VMEM),
                 whole(32, 16),
                 whole(18, C, C),
             ],
@@ -286,7 +286,7 @@
             num_scalar_prefetch=1,
             grid=(steps,),
             in_specs=[
-                whole(16, PIX, C),
+                pl.BlockSpec(memory_space=pltpu.VMEM),
                 whole(BG, PIX, C),
                 pl.BlockSpec((BG, PIX, C), lambda i, *_: (jnp.minimum(i + 1, steps - 1), 0, 0)),
                 regions,
@@ -409,6 +409,10 @@
     incoming = lax.all_to_all(
         outgoing.reshape(peers, PIX, C), "wa", split_axis=0, concat_axis=0, tiled=True
     )
+    from_right, below, corner, incoming = [
+        pltpu.with_memory_space_constraint(x, pltpu.VMEM)
+        for x in (from_right, below, corner, incoming)
+    ]
     pieces = (features, from_right, below, corner)
     places = jnp.concatenate(
         [offsets[:, :SIDE], offsets[:, SIDE:] + (corners[:, 1:2] % 16) * 4], axis=1

time: 181 us -> 177 us (0.978)
  local copies, waits for them, and re-layouts: 7.35 us -> 5.34 us
    unnamed x21 -> x13, local copies, waits for them, and re-layouts: 4.3 us -> 2.28 us
where the time goes in v6:
time: 177 us; the launch traced here: 175 us
  Pallas kernels  58.3 us (33%)
  waiting for transfers between devices  53.3 us (30%)
  starting transfers between devices  46.5 us (26%)
  other arithmetic  10.5 us (6%)
  local copies, waits for them, and re-layouts  5.34 us (3%)
    ppermute x6, waiting for transfers between devices, shifted(): lax.ppermute(value, axis, [(source, source + steps) for source in range(f...  28.2 us
    pallas_call x1, Pallas kernels, back(): pl.pallas_call(back_kernel, name='back', out_shape=[jax.ShapeDtypeStruct(...  22.2 us
    pallas_call x1, Pallas kernels, forward(): pl.pallas_call(forward_kernel, name='forward', out_shape=[jax.ShapeDtypeS...  20.7 us
    ppermute x6, starting transfers between devices, shifted(): lax.ppermute(value, axis, [(source, source + steps) for source in range(f...  18.8 us
    all_to_all x1, waiting for transfers between devices, local(): parts = lax.all_to_all(mine.reshape(peers, -1, C), 'wa', 0, 0, tiled=True)  18.2 us
    pallas_call x1, Pallas kernels, spread(): pl.pallas_call(spread_kernel, name='spread', out_shape=[piece(F32), piece...  12.8 us
    all_to_all x1, starting transfers between devices, local(): lax.all_to_all(jnp.broadcast_to(counts[None], (peers, 1, 1)), 'wa', 0, 0,...  8.05 us
    all_to_all x1, starting transfers between devices, local(): parts = lax.all_to_all(mine.reshape(peers, -1, C), 'wa', 0, 0, tiled=True)  6.92 us
  transfers between devices with their start and end apart: 15, of which 7 were waited for; matrix products, arithmetic and copies ran while one was open for 6% of the time, Pallas kernels for 21%

profile of v6, /device:TPU:1, one launch (start us, length us, event | category | flops | bytes accessed | tf_op | source)
XLA Modules:
  0.0 175.5 jit_solution(9749799844305331412)
XLA Ops:
  1.9 3.3 %collective-permute-start.1 = (bf16[32,32,256]{2,1,0:T(8,128)(2,1)}, bf16[32,32,256]{2,1,0:T(8,128)(2,1)S(1)}, u32[]{:S(2)}, u32[]{:S(2)}) collective-permute-start(bf16[32,32,256]{2,1,0:T(8,128)(2,1)} %tl_ref.1), channel_id=1, source_target_pairs={{16,0},{32,16},{48,32},{64,48},{80,64},{96,80},{112,96},{17,1},{33... | collective-permute-start | bytes 1572872 | tf_op jit(solution)/shard_map/ppermute | solution.py:23
  6.5 8.0 %all-to-all-start = ((s32[16,1,1]{2,1,0:T(1,128)}), s32[16,1,1]{2,1,0:T(1,128)S(1)}, u32[]{:S(2)}, u32[]{:S(2)}) async-start(s32[16,1,1]{2,1,0:T(1,128)} %broadcast_in_dim.7), calls=%async_computation | async-start | bytes 16384 | tf_op jit(solution)/shard_map/all_to_all | solution.py:402
  15.2 2.2 %copy.13.x_ref = bf16[8,14,14,256]{3,2,1,0:T(8,128)(2,1)} copy(bf16[8,14,14,256]{3,0,2,1:T(8,128)(2,1)} %param.13) | data formatting | bytes 1605632 | tf_op args[6]
  17.5 3.4 %all-to-all-done = s32[16,1,1]{2,1,0:T(1,128)S(1)} async-done(((s32[16,1,1]{2,1,0:T(1,128)}), s32[16,1,1]{2,1,0:T(1,128)S(1)}, u32[]{:S(2)}, u32[]{:S(2)}) %all-to-all-start) | async-done | bytes 96 | tf_op jit(solution)/shard_map/all_to_all | solution.py:402
  21.8 2.7 %route.1 = (bf16[16,14,16,256]{3,2,1,0:T(8,128)(2,1)}, s32[17]{0:T(128)}) custom-call(s32[16]{0:T(128)} %reduce.1.count_ref, s32[1,16]{1,0:T(1,128)} %perm_ref.1, bf16[8,14,14,256]{3,2,1,0:T(8,128)(2,1)} %copy.13.x_ref), custom_call_target="tpu_custom_call" | custom-call | bytes 4194304 | tf_op jit(solution)/shard_map/route/pallas_call | solution.py:83
  24.5 4.3 %all-to-all-start.1 = ((bf16[16,224,256]{2,1,0:T(8,128)(2,1)}), bf16[16,224,256]{2,1,0:T(8,128)(2,1)S(1)}, u32[]{:S(2)}, u32[]{:S(2)}) async-start(bf16[16,224,256]{2,1,0:T(8,128)(2,1)} %bitcast.17), calls=%async_computation.1 | async-start | bytes 3670016 | tf_op jit(solution)/shard_map/all_to_all | solution.py:409
  28.8 3.8 %collective-permute-start.2 = (bf16[32,32,256]{2,1,0:T(8,128)(2,1)S(1)}, bf16[32,32,256]{2,1,0:T(8,128)(2,1)S(1)}, u32[]{:S(2)}, u32[]{:S(2)}) collective-permute-start(bf16[32,32,256]{2,1,0:T(8,128)(2,1)S(1)} %collective-permute-done.tr_ref), channel_id=1, source_target_pairs={{16,0},{32,16},{48,32},{64,48},{80,64},{96,80},{112,96},{17,1},{33... | collective-permute-start | bytes 1572872 | tf_op jit(solution)/shard_map/ppermute | solution.py:23
  34.2 7.0 %collective-permute-done.2.br_ref = bf16[32,32,256]{2,1,0:T(8,128)(2,1)S(1)} collective-permute-done((bf16[32,32,256]{2,1,0:T(8,128)(2,1)S(1)}, bf16[32,32,256]{2,1,0:T(8,128)(2,1)S(1)}, u32[]{:S(2)}, u32[]{:S(2)}) %collective-permute-start.2) | collective-permute-done | bytes 524320 | tf_op jit(solution)/shard_map/ppermute | solution.py:23
  41.3 20.7 %forward.1 = (bf16[256,4096]{1,0:T(8,128)(2,1)}, bf16[256,4096]{1,0:T(8,128)(2,1)}, bf16[16,224,256]{2,1,0:T(8,128)(2,1)}, bf16[16,224,256]{2,1,0:T(8,128)(2,1)}, bf16[18,256,256]{2,1,0:T(8,128)(2,1)}) custom-call(s32[32]{0:T(128)} %reshape.33.corner_ref, bf16[32,32,256]{2,1,0:T(8,128)(2,1)} %tl_ref.1, bf16[32,32,256]{2,1,0:T(8,128)(2,1)S(1)} %collective-permute-done.tr_ref, ...), custom_call_target="tpu_custom_call" | custom-call | flops 11299999744 | bytes 14680064 | tf_op jit(solution)/shard_map/forward/pallas_call | solution.py:155
  62.0 22.2 %back.1 = (bf16[16,224,256]{2,1,0:T(8,128)(2,1)}, bf16[9,256,256]{2,1,0:T(8,128)(2,1)}, bf16[9,256,256]{2,1,0:T(8,128)(2,1)}) custom-call(s32[17]{0:T(128)} %get-tuple-element.19.meta_ref, bf16[16,224,256]{2,1,0:T(8,128)(2,1)S(1)} %all-to-all-done.1.in_ref, bf16[16,224,256]{2,1,0:T(8,128)(2,1)} %get-tuple-element.21.first_ref.next_ref, ...), custom_call_target="tpu_custom_call" | custom-call | flops 14000000000 | bytes 16777216 | tf_op jit(solution)/shard_map/back/pallas_call | solution.py:277
  84.2 3.0 %collective-permute-done.3 = bf16[9,256,256]{2,1,0:T(8,128)(2,1)S(1)} collective-permute-done((bf16[9,256,256]{2,1,0:T(8,128)(2,1)}, bf16[9,256,256]{2,1,0:T(8,128)(2,1)S(1)}, u32[]{:S(2)}, u32[]{:S(2)}) %collective-permute-start.3) | collective-permute-done | bytes 1179680 | tf_op jit(solution)/shard_map/ppermute | solution.py:392
  87.3 2.7 %add_convert_fusion = bf16[9,256,256]{2,1,0:T(8,128)(2,1)} fusion(bf16[9,256,256]{2,1,0:T(8,128)(2,1)S(1)} %collective-permute-done.3, bf16[9,256,256]{2,1,0:T(8,128)(2,1)} %get-tuple-element.26), kind=kLoop, calls=%fused_computation.1 | loop fusion | flops 2359296 | bytes 3538944 | tf_op jit(solution)/shard_map/convert_element_type | solution.py:428
  90.0 6.9 %all-to-all-start.2 = ((bf16[16,144,256]{2,1,0:T(8,128)(2,1)}), bf16[16,144,256]{2,1,0:T(8,128)(2,1)S(1)}, u32[]{:S(2)}, u32[]{:S(2)}) async-start(bf16[16,144,256]{2,1,0:T(8,128)(2,1)} %bitcast.6), calls=%async_computation.2 | async-start | bytes 2359296 | tf_op jit(solution)/shard_map/all_to_all | solution.py:429
  97.6 18.2 %all-to-all-done.2 = bf16[16,144,256]{2,1,0:T(8,128)(2,1)S(1)} async-done(((bf16[16,144,256]{2,1,0:T(8,128)(2,1)}), bf16[16,144,256]{2,1,0:T(8,128)(2,1)S(1)}, u32[]{:S(2)}, u32[]{:S(2)}) %all-to-all-start.2) | async-done | bytes 1179680 | tf_op jit(solution)/shard_map/all_to_all | solution.py:429
  116.4 3.0 %collective-permute-start.5 = (bf16[144,256]{1,0:T(8,128)(2,1)S(1)}, bf16[144,256]{1,0:T(8,128)(2,1)S(1)}, u32[]{:S(2)}, u32[]{:S(2)}) collective-permute-start(bf16[144,256]{1,0:T(8,128)(2,1)S(1)} %reduce_sum.12), channel_id=1, source_target_pairs={{0,64},{16,80},{32,96},{48,112},{64,0},{80,16},{96,32},{112,48},{1... | collective-permute-start | bytes 221192 | tf_op jit(solution)/shard_map/ppermute | solution.py:436
  120.2 12.8 %spread.1 = (f32[32,32,256]{2,1,0:T(8,128)}, bf16[32,32,256]{2,1,0:T(8,128)(2,1)}, bf16[32,32,256]{2,1,0:T(8,128)(2,1)}, bf16[32,32,256]{2,1,0:T(8,128)(2,1)}) custom-call(s32[32]{0:T(128)} %reshape.33.corner_ref, bf16[16,224,256]{2,1,0:T(8,128)(2,1)} %get-tuple-element.28.p_ref, f32[16,32]{1,0:T(8,128)} %select_maximum_fusion.off_ref, ...), custom_call_target="tpu_custom_call" | custom-call | flops 7000000000 | bytes 6291456 | tf_op jit(solution)/shard_map/spread/pallas_call | solution.py:365
  133.0 4.1 %collective-permute-start.8 = (bf16[32,32,256]{2,1,0:T(8,128)(2,1)}, bf16[32,32,256]{2,1,0:T(8,128)(2,1)S(1)}, u32[]{:S(2)}, u32[]{:S(2)}) collective-permute-start(bf16[32,32,256]{2,1,0:T(8,128)(2,1)} %get-tuple-element.32), channel_id=1, source_target_pairs={{0,16},{16,32},{32,48},{48,64},{64,80},{80,96},{96,112},{1,17},{17... | collective-permute-start | bytes 1572872 | tf_op jit(solution)/shard_map/ppermute | solution.py:23
  138.2 3.8 %all-to-all-start.3 = ((bf16[16,144,256]{2,1,0:T(8,128)(2,1)}), bf16[16,144,256]{2,1,0:T(8,128)(2,1)S(1)}, u32[]{:S(2)}, u32[]{:S(2)}) async-start(bf16[16,144,256]{2,1,0:T(8,128)(2,1)} %broadcast_in_dim.16), calls=%async_computation.3 | async-start | bytes 2359296 | tf_op jit(solution)/shard_map/all_to_all | solution.py:439
  142.1 2.1 %collective-permute-start.7 = (bf16[32,32,256]{2,1,0:T(8,128)(2,1)S(1)}, bf16[32,32,256]{2,1,0:T(8,128)(2,1)S(1)}, u32[]{:S(2)}, u32[]{:S(2)}) collective-permute-start(bf16[32,32,256]{2,1,0:T(8,128)(2,1)S(1)} %copy-done.4), channel_id=1, source_target_pairs={{0,16},{16,32},{32,48},{48,64},{64,80},{80,96},{96,112},{1,17},{17... | collective-permute-start | bytes 1572872 | tf_op jit(solution)/shard_map/ppermute | solution.py:23
  144.4 4.2 %collective-permute-start.9 = (bf16[32,32,256]{2,1,0:T(8,128)(2,1)S(1)}, bf16[32,32,256]{2,1,0:T(8,128)(2,1)}, u32[]{:S(2)}, u32[]{:S(2)}) collective-permute-start(bf16[32,32,256]{2,1,0:T(8,128)(2,1)S(1)} %add_convert_fusion.1), channel_id=1, source_target_pairs={{0,1},{1,2},{2,3},{3,4},{4,5},{5,6},{6,7},{7,8},{8,9},{9,10},{10,1... | collective-permute-start | bytes 1572872 | tf_op jit(solution)/shard_map/ppermute | solution.py:23
  148.6 1.7 collective-permute-done.7
  150.5 19.5 %collective-permute-done.9 = bf16[32,32,256]{2,1,0:T(8,128)(2,1)} collective-permute-done((bf16[32,32,256]{2,1,0:T(8,128)(2,1)S(1)}, bf16[32,32,256]{2,1,0:T(8,128)(2,1)}, u32[]{:S(2)}, u32[]{:S(2)}) %collective-permute-start.9) | collective-permute-done | bytes 524320 | tf_op jit(solution)/shard_map/ppermute | solution.py:23
  170.3 2.2 %convert_add_fusion = f32[32,32,256]{2,1,0:T(8,128)} fusion(f32[32,32,256]{2,1,0:T(8,128)S(1)} %convert_add_fusion.1, bf16[32,32,256]{2,1,0:T(8,128)(2,1)} %collective-permute-done.9), kind=kLoop, calls=%fused_computation.4 | loop fusion | flops 524288 | bytes 2621440 | tf_op jit(solution)/shard_map/add | solution.py:443
  173.0 2.5 %maximum_convert_fusion = f32[2,3,3,256,256]{4,3,2,1,0:T(8,128)} fusion(bf16[1,3,3,256,256]{4,3,2,1,0:T(8,128)(2,1)S(1)} %bitcast.14, bf16[1,3,3,256,256]{4,3,2,1,0:T(8,128)(2,1)S(1)} %bitcast.13), kind=kLoop, calls=%fused_computation | loop fusion | flops 2359296 | bytes 7077888 | tf_op jit(solution)/shard_map/convert_element_type | solution.py:445
  (43 shorter events, 9.6 us)
Async XLA Ops:
  0.6 28.2 %collective-permute-start = (bf16[32,32,256]{2,1,0:T(8,128)(2,1)}, bf16[32,32,256]{2,1,0:T(8,128)(2,1)S(1)}, u32[]{:S(2)}, u32[]{:S(2)}) collective-permute-start(bf16[32,32,256]{2,1,0:T(8,128)(2,1)} %tl_ref.1), channel_id=1, source_target_pairs={{1,0},{2,1},{3,2},{4,3},{5,4},{6,5},{7,6},{8,7},{9,8},{10,9},{11,1... | collective-permute-start | bytes 1572872 | tf_op jit(solution)/shard_map/ppermute | solution.py:23
  1.9 32.3 %collective-permute-start.1 = (bf16[32,32,256]{2,1,0:T(8,128)(2,1)}, bf16[32,32,256]{2,1,0:T(8,128)(2,1)S(1)}, u32[]{:S(2)}, u32[]{:S(2)}) collective-permute-start(bf16[32,32,256]{2,1,0:T(8,128)(2,1)} %tl_ref.1), channel_id=1, source_target_pairs={{16,0},{32,16},{48,32},{64,48},{80,64},{96,80},{112,96},{17,1},{33... | collective-permute-start | bytes 1572872 | tf_op jit(solution)/shard_map/ppermute | solution.py:23
  6.5 14.4 %all-to-all-start = ((s32[16,1,1]{2,1,0:T(1,128)}), s32[16,1,1]{2,1,0:T(1,128)S(1)}, u32[]{:S(2)}, u32[]{:S(2)}) async-start(s32[16,1,1]{2,1,0:T(1,128)} %broadcast_in_dim.7), calls=%async_computation | async-start | bytes 16384 | tf_op jit(solution)/shard_map/all_to_all | solution.py:402
  24.5 8.2 %copy-start.2 = (s32[16,28]{1,0:T(8,128)S(1)}, s32[16,28]{1,0:T(8,128)}, u32[]{:S(2)}) copy-start(s32[16,28]{1,0:T(8,128)} %param.11) | copy-start | bytes 5380
  24.5 8.2 %copy-start.5 = (s32[16,2]{0,1:T(2,128)S(1)}, s32[16,2]{0,1:T(2,128)}, u32[]{:S(2)}) copy-start(s32[16,2]{0,1:T(2,128)} %param.10) | copy-start | bytes 388
  24.5 9.0 %copy-start.3 = (pred[16]{0:T(512)(128)(4,1)S(1)}, pred[16]{0:T(512)(128)(4,1)}, u32[]{:S(2)}) copy-start(pred[16]{0:T(512)(128)(4,1)} %constant.32.clone.1) | copy-start | bytes 52
  24.5 37.5 %all-to-all-start.1 = ((bf16[16,224,256]{2,1,0:T(8,128)(2,1)}), bf16[16,224,256]{2,1,0:T(8,128)(2,1)S(1)}, u32[]{:S(2)}, u32[]{:S(2)}) async-start(bf16[16,224,256]{2,1,0:T(8,128)(2,1)} %bitcast.17), calls=%async_computation.1 | async-start | bytes 3670016 | tf_op jit(solution)/shard_map/all_to_all | solution.py:409
  28.8 12.5 %collective-permute-start.2 = (bf16[32,32,256]{2,1,0:T(8,128)(2,1)S(1)}, bf16[32,32,256]{2,1,0:T(8,128)(2,1)S(1)}, u32[]{:S(2)}, u32[]{:S(2)}) collective-permute-start(bf16[32,32,256]{2,1,0:T(8,128)(2,1)S(1)} %collective-permute-done.tr_ref), channel_id=1, source_target_pairs={{16,0},{32,16},{48,32},{64,48},{80,64},{96,80},{112,96},{17,1},{33... | collective-permute-start | bytes 1572872 | tf_op jit(solution)/shard_map/ppermute | solution.py:23
  84.2 3.1 %collective-permute-start.3 = (bf16[9,256,256]{2,1,0:T(8,128)(2,1)}, bf16[9,256,256]{2,1,0:T(8,128)(2,1)S(1)}, u32[]{:S(2)}, u32[]{:S(2)}) collective-permute-start(bf16[9,256,256]{2,1,0:T(8,128)(2,1)} %get-tuple-element.27), channel_id=1, source_target_pairs={{0,16},{16,0},{32,48},{48,32},{64,80},{80,64},{96,112},{112,96},{1... | collective-permute-start | bytes 3538952 | tf_op jit(solution)/shard_map/ppermute | solution.py:392
  90.0 25.8 %all-to-all-start.2 = ((bf16[16,144,256]{2,1,0:T(8,128)(2,1)}), bf16[16,144,256]{2,1,0:T(8,128)(2,1)S(1)}, u32[]{:S(2)}, u32[]{:S(2)}) async-start(bf16[16,144,256]{2,1,0:T(8,128)(2,1)} %bitcast.6), calls=%async_computation.2 | async-start | bytes 2359296 | tf_op jit(solution)/shard_map/all_to_all | solution.py:429
  116.0 21.1 %collective-permute-start.6 = (bf16[144,256]{1,0:T(8,128)(2,1)S(1)}, bf16[144,256]{1,0:T(8,128)(2,1)S(1)}, u32[]{:S(2)}, u32[]{:S(2)}) collective-permute-start(bf16[144,256]{1,0:T(8,128)(2,1)S(1)} %reduce_sum.12), channel_id=1, source_target_pairs={{0,96},{16,112},{32,0},{48,16},{64,32},{80,48},{96,64},{112,80},{1... | collective-permute-start | bytes 221192 | tf_op jit(solution)/shard_map/ppermute | solution.py:436
  116.4 20.7 %collective-permute-start.5 = (bf16[144,256]{1,0:T(8,128)(2,1)S(1)}, bf16[144,256]{1,0:T(8,128)(2,1)S(1)}, u32[]{:S(2)}, u32[]{:S(2)}) collective-permute-start(bf16[144,256]{1,0:T(8,128)(2,1)S(1)} %reduce_sum.12), channel_id=1, source_target_pairs={{0,64},{16,80},{32,96},{48,112},{64,0},{80,16},{96,32},{112,48},{1... | collective-permute-start | bytes 221192 | tf_op jit(solution)/shard_map/ppermute | solution.py:436
  119.4 17.7 %collective-permute-start.4 = (bf16[144,256]{1,0:T(8,128)(2,1)S(1)}, bf16[144,256]{1,0:T(8,128)(2,1)S(1)}, u32[]{:S(2)}, u32[]{:S(2)}) collective-permute-start(bf16[144,256]{1,0:T(8,128)(2,1)S(1)} %reduce_sum.12), channel_id=1, source_target_pairs={{0,32},{16,48},{32,64},{48,80},{64,96},{80,112},{96,0},{112,16},{1... | collective-permute-start | bytes 221192 | tf_op jit(solution)/shard_map/ppermute | solution.py:436
  133.0 11.2 %collective-permute-start.8 = (bf16[32,32,256]{2,1,0:T(8,128)(2,1)}, bf16[32,32,256]{2,1,0:T(8,128)(2,1)S(1)}, u32[]{:S(2)}, u32[]{:S(2)}) collective-permute-start(bf16[32,32,256]{2,1,0:T(8,128)(2,1)} %get-tuple-element.32), channel_id=1, source_target_pairs={{0,16},{16,32},{32,48},{48,64},{64,80},{80,96},{96,112},{1,17},{17... | collective-permute-start | bytes 1572872 | tf_op jit(solution)/shard_map/ppermute | solution.py:23
  138.2 3.9 %copy-start.4 = (bf16[32,32,256]{2,1,0:T(8,128)(2,1)S(1)}, bf16[32,32,256]{2,1,0:T(8,128)(2,1)}, u32[]{:S(2)}) copy-start(bf16[32,32,256]{2,1,0:T(8,128)(2,1)} %get-tuple-element.30) | copy-start | bytes 1572868
  138.2 5.9 %copy-start.1 = (bf16[32,32,256]{2,1,0:T(8,128)(2,1)S(1)}, bf16[32,32,256]{2,1,0:T(8,128)(2,1)}, u32[]{:S(2)}) copy-start(bf16[32,32,256]{2,1,0:T(8,128)(2,1)} %get-tuple-element.31) | copy-start | bytes 1572868
  138.2 31.8 %all-to-all-start.3 = ((bf16[16,144,256]{2,1,0:T(8,128)(2,1)}), bf16[16,144,256]{2,1,0:T(8,128)(2,1)S(1)}, u32[]{:S(2)}, u32[]{:S(2)}) async-start(bf16[16,144,256]{2,1,0:T(8,128)(2,1)} %broadcast_in_dim.16), calls=%async_computation.3 | async-start | bytes 2359296 | tf_op jit(solution)/shard_map/all_to_all | solution.py:439
  142.1 8.2 %copy-start = (f32[32,32,256]{2,1,0:T(8,128)S(1)}, f32[32,32,256]{2,1,0:T(8,128)}, u32[]{:S(2)}) copy-start(f32[32,32,256]{2,1,0:T(8,128)} %get-tuple-element.29) | copy-start | bytes 3145732
  142.1 8.2 %collective-permute-start.7 = (bf16[32,32,256]{2,1,0:T(8,128)(2,1)S(1)}, bf16[32,32,256]{2,1,0:T(8,128)(2,1)S(1)}, u32[]{:S(2)}, u32[]{:S(2)}) collective-permute-start(bf16[32,32,256]{2,1,0:T(8,128)(2,1)S(1)} %copy-done.4), channel_id=1, source_target_pairs={{0,16},{16,32},{32,48},{48,64},{64,80},{80,96},{96,112},{1,17},{17... | collective-permute-start | bytes 1572872 | tf_op jit(solution)/shard_map/ppermute | solution.py:23
  144.4 25.6 %collective-permute-start.9 = (bf16[32,32,256]{2,1,0:T(8,128)(2,1)S(1)}, bf16[32,32,256]{2,1,0:T(8,128)(2,1)}, u32[]{:S(2)}, u32[]{:S(2)}) collective-permute-start(bf16[32,32,256]{2,1,0:T(8,128)(2,1)S(1)} %add_convert_fusion.1), channel_id=1, source_target_pairs={{0,1},{1,2},{2,3},{3,4},{4,5},{5,6},{6,7},{7,8},{8,9},{9,10},{10,1... | collective-permute-start | bytes 1572872 | tf_op jit(solution)/shard_map/ppermute | solution.py:23
  170.0 2.8 %collective-permute-start.10 = (bf16[9,256,256]{2,1,0:T(8,128)(2,1)S(1)}, bf16[9,256,256]{2,1,0:T(8,128)(2,1)S(1)}, u32[]{:S(2)}, u32[]{:S(2)}) collective-permute-start(bf16[9,256,256]{2,1,0:T(8,128)(2,1)S(1)} %bitcast.15), channel_id=1, source_target_pairs={{0,16},{16,0},{32,48},{48,32},{64,80},{80,64},{96,112},{112,96},{1... | collective-permute-start | bytes 3538952 | tf_op jit(solution)/shard_map/ppermute | solution.py:392

commit v7 on v6

--- a/solution.py
+++ b/solution.py
@@ -70,10 +70,10 @@
         region = jnp.clip(arrival // peers, 0, x_ref.shape[0] - 1)
         o_ref[i, :, 0:SIDE, :] = x_ref[region]
         o_ref[i, :, SIDE:PITCH, :] = gap
-        start = start + count_ref[i]
+        start = start + count_ref[i, 0, 0]
     for i in range(peers):
         meta_ref[i] = perm_ref[0, (here_start + i) & (peers - 1)]
-    meta_ref[peers] = count_ref[here]
+    meta_ref[peers] = count_ref[here, 0, 0]
 
 
 def route(counts, perm, cotangent):
@@ -279,8 +279,8 @@
         name="back",
         out_shape=[
             jax.ShapeDtypeStruct((slots, PIX, C), BF),
-            jax.ShapeDtypeStruct((9, C, C), BF),
-            jax.ShapeDtypeStruct((9, C, C), BF),
+            pltpu.VMEM((9, C, C), BF),
+            pltpu.VMEM((9, C, C), BF),
         ],
         grid_spec=pltpu.PrefetchScalarGridSpec(
             num_scalar_prefetch=1,
@@ -294,7 +294,7 @@
                 columns,
                 columns,
             ],
-            out_specs=[regions, whole(9, C, C), whole(9, C, C)],
+            out_specs=[regions] + [pl.BlockSpec(memory_space=pltpu.VMEM)] * 2,
             scratch_shapes=[
                 pltpu.VMEM((2, 3, BG, ROWS, C), BF),
                 pltpu.VMEM((3, BG, ROWS, C), BF),
@@ -302,6 +302,7 @@
                 pltpu.VMEM((9, C, C), F32),
             ],
         ),
+        compiler_params=pltpu.CompilerParams(vmem_limit_bytes=58 << 20),
         cost_estimate=pl.CostEstimate(
             flops=14_000_000_000, bytes_accessed=16 << 20, transcendentals=0
         ),
@@ -401,7 +402,7 @@
     core = lax.axis_index("ha") % 2
     row_counts = lax.all_to_all(
         jnp.broadcast_to(counts[None], (peers, 1, 1)), "wa", 0, 0, tiled=True
-    ).reshape(peers)
+    )
     from_right = shifted(features, "wa", -1)
     below = shifted(features, "ha", -1)
     outgoing, meta = route(row_counts, owner_perm, cotangent)
@@ -428,7 +429,8 @@
     mine = (keep.astype(F32) + swap_cores(send).astype(F32)).astype(BF)
     parts = lax.all_to_all(mine.reshape(peers, -1, C), "wa", 0, 0, tiled=True)
     tile, right, lower, corner = spread(corners, inner, places, turned)
-    corner, lower = [shifted(piece, "ha", 1) for piece in (corner, lower)]
+    corner = shifted(corner, "ha", 1)
+    lower = shifted(lower, "ha", 1)
     part = jnp.sum(parts.astype(F32), axis=0).astype(BF)
     count = lax.axis_size("ha")
     total = part.astype(F32)
@@ -438,9 +440,8 @@
     whole = jnp.broadcast_to(total.astype(BF)[None], (peers, *total.shape))
     mine = lax.all_to_all(whole, "wa", 0, 0, tiled=True).reshape(9, C, C)
     side = shifted((right.astype(F32) + corner.astype(F32)).astype(BF), "wa", 1)
-    tile = tile + lower.astype(F32)
-    mine, tile, side = lax.optimization_barrier((mine, tile, side))
-    tile = tile + side.astype(F32)
+    tile = tile + lower.astype(F32) + side.astype(F32)
+    mine, tile = lax.optimization_barrier((mine, tile))
     other = swap_cores(mine)
     grads = jnp.stack([pick_layer(core, mine, other), pick_layer(core, other, mine)]).astype(F32)
     return (tile, grads.reshape(2, 3, 3, C, C))

time: 177 us -> 166 us (0.938)
  waiting for transfers between devices: 53.3 us -> 43.6 us
  other arithmetic: 10.5 us -> 7.2 us
    all_to_all x1, waiting for transfers between devices: 18.2 us -> 1.65 us  [local(): parts = lax.all_to_all(mine.reshape(peers, -1, C), 'wa', 0, 0, tiled=True)]
    ppermute x3, waiting for transfers between devices: 0.01 us -> 4.46 us  [local(): lax.ppermute(part, 'ha', [(i, (i + hop) % count) for i in range(count)])]
    all_to_all x1, starting transfers between devices: 3.83 us -> 6.82 us  [local(): mine = lax.all_to_all(whole, 'wa', 0, 0, tiled=True).reshape(9, C, C)]
    ppermute x2, waiting for transfers between devices: 3.37 us -> 5.53 us  [swap_cores(): lax.ppermute(x, 'ha', [(i, i ^ 1) for i in range(lax.axis_size('ha'))])]
  transfers between devices with their start and end apart: 15 -> 15, of which waited for: 7 -> 9; matrix products, arithmetic and copies ran while one was open for 6% -> 5% of each run, Pallas kernels for 21% -> 22%
where the time goes in v7:
time: 166 us; the launch traced here: 164 us
  Pallas kernels  57.5 us (35%)
  starting transfers between devices  48 us (29%)
  waiting for transfers between devices  43.6 us (26%)
  other arithmetic  7.2 us (4%)
  local copies, waits for them, and re-layouts  5.99 us (4%)
    ppermute x6, waiting for transfers between devices, shifted(): lax.ppermute(value, axis, [(source, source + steps) for source in range(f...  28.5 us
    pallas_call x1, Pallas kernels, back(): pl.pallas_call(back_kernel, name='back', out_shape=[jax.ShapeDtypeStruct(...  21.3 us
    pallas_call x1, Pallas kernels, forward(): pl.pallas_call(forward_kernel, name='forward', out_shape=[jax.ShapeDtypeS...  20.7 us
    ppermute x6, starting transfers between devices, shifted(): lax.ppermute(value, axis, [(source, source + steps) for source in range(f...  17.5 us
    pallas_call x1, Pallas kernels, spread(): pl.pallas_call(spread_kernel, name='spread', out_shape=[piece(F32), piece...  12.8 us
    all_to_all x1, starting transfers between devices, local(): lax.all_to_all(jnp.broadcast_to(counts[None], (peers, 1, 1)), 'wa', 0, 0,...  8.05 us
    all_to_all x1, starting transfers between devices, local(): parts = lax.all_to_all(mine.reshape(peers, -1, C), 'wa', 0, 0, tiled=True)  6.93 us
    all_to_all x1, starting transfers between devices, local(): mine = lax.all_to_all(whole, 'wa', 0, 0, tiled=True).reshape(9, C, C)  6.82 us
  transfers between devices with their start and end apart: 15, of which 9 were waited for; matrix products, arithmetic and copies ran while one was open for 5% of the time, Pallas kernels for 22%

profile of v7, /device:TPU:1, one launch (start us, length us, event | category | flops | bytes accessed | tf_op | source)
XLA Modules:
  0.0 163.7 jit_solution(9870723755772890070)
XLA Ops:
  1.9 3.3 %collective-permute-start.1 = (bf16[32,32,256]{2,1,0:T(8,128)(2,1)}, bf16[32,32,256]{2,1,0:T(8,128)(2,1)S(1)}, u32[]{:S(2)}, u32[]{:S(2)}) collective-permute-start(bf16[32,32,256]{2,1,0:T(8,128)(2,1)} %tl_ref.1), channel_id=1, source_target_pairs={{16,0},{32,16},{48,32},{64,48},{80,64},{96,80},{112,96},{17,1},{33... | collective-permute-start | bytes 1572872 | tf_op jit(solution)/shard_map/ppermute | solution.py:23
  6.5 8.0 %all-to-all-start = ((s32[16,1,1]{2,1,0:T(1,128)}), s32[16,1,1]{2,1,0:T(1,128)S(1)}, u32[]{:S(2)}, u32[]{:S(2)}) async-start(s32[16,1,1]{2,1,0:T(1,128)} %broadcast_in_dim.7), calls=%async_computation | async-start | bytes 16384 | tf_op jit(solution)/shard_map/all_to_all | solution.py:403
  15.2 2.2 %copy.9.x_ref = bf16[8,14,14,256]{3,2,1,0:T(8,128)(2,1)} copy(bf16[8,14,14,256]{3,0,2,1:T(8,128)(2,1)} %param.13) | data formatting | bytes 1605632 | tf_op args[6]
  17.5 3.4 %all-to-all-done.count_ref = s32[16,1,1]{2,1,0:T(1,128)S(1)} async-done(((s32[16,1,1]{2,1,0:T(1,128)}), s32[16,1,1]{2,1,0:T(1,128)S(1)}, u32[]{:S(2)}, u32[]{:S(2)}) %all-to-all-start) | async-done | bytes 96 | tf_op jit(solution)/shard_map/all_to_all | solution.py:403
  21.5 2.7 %route.1 = (bf16[16,14,16,256]{3,2,1,0:T(8,128)(2,1)}, s32[17]{0:T(128)}) custom-call(s32[16,1,1]{2,1,0:T(1,128)} %copy-done.2, s32[1,16]{1,0:T(1,128)} %perm_ref.1, bf16[8,14,14,256]{3,2,1,0:T(8,128)(2,1)} %copy.9.x_ref), custom_call_target="tpu_custom_call" | custom-call | bytes 4194304 | tf_op jit(solution)/shard_map/route/pallas_call | solution.py:83
  24.2 4.3 %all-to-all-start.1 = ((bf16[16,224,256]{2,1,0:T(8,128)(2,1)}), bf16[16,224,256]{2,1,0:T(8,128)(2,1)S(1)}, u32[]{:S(2)}, u32[]{:S(2)}) async-start(bf16[16,224,256]{2,1,0:T(8,128)(2,1)} %bitcast.17), calls=%async_computation.1 | async-start | bytes 3670016 | tf_op jit(solution)/shard_map/all_to_all | solution.py:410
  28.5 3.8 %collective-permute-start.2 = (bf16[32,32,256]{2,1,0:T(8,128)(2,1)S(1)}, bf16[32,32,256]{2,1,0:T(8,128)(2,1)S(1)}, u32[]{:S(2)}, u32[]{:S(2)}) collective-permute-start(bf16[32,32,256]{2,1,0:T(8,128)(2,1)S(1)} %collective-permute-done.tr_ref), channel_id=1, source_target_pairs={{16,0},{32,16},{48,32},{64,48},{80,64},{96,80},{112,96},{17,1},{33... | collective-permute-start | bytes 1572872 | tf_op jit(solution)/shard_map/ppermute | solution.py:23
  34.0 7.0 %collective-permute-done.2.br_ref = bf16[32,32,256]{2,1,0:T(8,128)(2,1)S(1)} collective-permute-done((bf16[32,32,256]{2,1,0:T(8,128)(2,1)S(1)}, bf16[32,32,256]{2,1,0:T(8,128)(2,1)S(1)}, u32[]{:S(2)}, u32[]{:S(2)}) %collective-permute-start.2) | collective-permute-done | bytes 524320 | tf_op jit(solution)/shard_map/ppermute | solution.py:23
  41.0 20.7 %forward.1 = (bf16[256,4096]{1,0:T(8,128)(2,1)}, bf16[256,4096]{1,0:T(8,128)(2,1)}, bf16[16,224,256]{2,1,0:T(8,128)(2,1)}, bf16[16,224,256]{2,1,0:T(8,128)(2,1)}, bf16[18,256,256]{2,1,0:T(8,128)(2,1)}) custom-call(s32[32]{0:T(128)} %reshape.29.corner_ref, bf16[32,32,256]{2,1,0:T(8,128)(2,1)} %tl_ref.1, bf16[32,32,256]{2,1,0:T(8,128)(2,1)S(1)} %collective-permute-done.tr_ref, ...), custom_call_target="tpu_custom_call" | custom-call | flops 11299999744 | bytes 14680064 | tf_op jit(solution)/shard_map/forward/pallas_call | solution.py:155
  61.7 21.3 %back.1 = (bf16[16,224,256]{2,1,0:T(8,128)(2,1)}, bf16[9,256,256]{2,1,0:T(8,128)(2,1)S(1)}, bf16[9,256,256]{2,1,0:T(8,128)(2,1)S(1)}) custom-call(s32[17]{0:T(128)} %get-tuple-element.18.meta_ref, bf16[16,224,256]{2,1,0:T(8,128)(2,1)S(1)} %all-to-all-done.1.in_ref, bf16[16,224,256]{2,1,0:T(8,128)(2,1)} %get-tuple-element.20.first_ref.next_ref, ...), custom_call_target="tpu_custom_call" | custom-call | flops 14000000000 | bytes 16777216 | tf_op jit(solution)/shard_map/back/pallas_call | solution.py:277
  83.1 2.8 %collective-permute-done.3 = bf16[9,256,256]{2,1,0:T(8,128)(2,1)S(1)} collective-permute-done((bf16[9,256,256]{2,1,0:T(8,128)(2,1)S(1)}, bf16[9,256,256]{2,1,0:T(8,128)(2,1)S(1)}, u32[]{:S(2)}, u32[]{:S(2)}) %collective-permute-start.3) | collective-permute-done | bytes 1179680 | tf_op jit(solution)/shard_map/ppermute | solution.py:393
  87.3 6.9 %all-to-all-start.2 = ((bf16[16,144,256]{2,1,0:T(8,128)(2,1)}), bf16[16,144,256]{2,1,0:T(8,128)(2,1)S(1)}, u32[]{:S(2)}, u32[]{:S(2)}) async-start(bf16[16,144,256]{2,1,0:T(8,128)(2,1)} %bitcast.6), calls=%async_computation.2 | async-start | bytes 2359296 | tf_op jit(solution)/shard_map/all_to_all | solution.py:430
  94.9 12.8 %spread.1 = (f32[32,32,256]{2,1,0:T(8,128)}, bf16[32,32,256]{2,1,0:T(8,128)(2,1)}, bf16[32,32,256]{2,1,0:T(8,128)(2,1)}, bf16[32,32,256]{2,1,0:T(8,128)(2,1)}) custom-call(s32[32]{0:T(128)} %reshape.29.corner_ref, bf16[16,224,256]{2,1,0:T(8,128)(2,1)} %get-tuple-element.27.p_ref, f32[16,32]{1,0:T(8,128)} %select_maximum_fusion.off_ref, ...), custom_call_target="tpu_custom_call" | custom-call | flops 7000000000 | bytes 6291456 | tf_op jit(solution)/shard_map/spread/pallas_call | solution.py:366
  107.7 3.8 %collective-permute-start.8 = (bf16[32,32,256]{2,1,0:T(8,128)(2,1)}, bf16[32,32,256]{2,1,0:T(8,128)(2,1)S(1)}, u32[]{:S(2)}, u32[]{:S(2)}) collective-permute-start(bf16[32,32,256]{2,1,0:T(8,128)(2,1)} %get-tuple-element.31), channel_id=1, source_target_pairs={{0,16},{16,32},{32,48},{48,64},{64,80},{80,96},{96,112},{1,17},{17... | collective-permute-start | bytes 1572872 | tf_op jit(solution)/shard_map/ppermute | solution.py:23
  111.5 1.6 %all-to-all-done.2 = bf16[16,144,256]{2,1,0:T(8,128)(2,1)S(1)} async-done(((bf16[16,144,256]{2,1,0:T(8,128)(2,1)}), bf16[16,144,256]{2,1,0:T(8,128)(2,1)S(1)}, u32[]{:S(2)}, u32[]{:S(2)}) %all-to-all-start.2) | async-done | bytes 1179680 | tf_op jit(solution)/shard_map/all_to_all | solution.py:430
  113.7 3.0 %collective-permute-start.5 = (bf16[144,256]{1,0:T(8,128)(2,1)S(1)}, bf16[144,256]{1,0:T(8,128)(2,1)S(1)}, u32[]{:S(2)}, u32[]{:S(2)}) collective-permute-start(bf16[144,256]{1,0:T(8,128)(2,1)S(1)} %reduce_sum.12), channel_id=1, source_target_pairs={{0,64},{16,80},{32,96},{48,112},{64,0},{80,16},{96,32},{112,48},{1... | collective-permute-start | bytes 221192 | tf_op jit(solution)/shard_map/ppermute | solution.py:438
  117.5 2.9 %collective-permute-done.5 = bf16[144,256]{1,0:T(8,128)(2,1)S(1)} collective-permute-done((bf16[144,256]{1,0:T(8,128)(2,1)S(1)}, bf16[144,256]{1,0:T(8,128)(2,1)S(1)}, u32[]{:S(2)}, u32[]{:S(2)}) %collective-permute-start.5) | collective-permute-done | bytes 73760 | tf_op jit(solution)/shard_map/ppermute | solution.py:438
  123.1 6.8 %all-to-all-start.3 = ((bf16[16,144,256]{2,1,0:T(8,128)(2,1)}), bf16[16,144,256]{2,1,0:T(8,128)(2,1)S(1)}, u32[]{:S(2)}, u32[]{:S(2)}) async-start(bf16[16,144,256]{2,1,0:T(8,128)(2,1)} %broadcast_in_dim.16), calls=%async_computation.3 | async-start | bytes 2359296 | tf_op jit(solution)/shard_map/all_to_all | solution.py:441
  129.9 2.1 %collective-permute-start.7 = (bf16[32,32,256]{2,1,0:T(8,128)(2,1)S(1)}, bf16[32,32,256]{2,1,0:T(8,128)(2,1)S(1)}, u32[]{:S(2)}, u32[]{:S(2)}) collective-permute-start(bf16[32,32,256]{2,1,0:T(8,128)(2,1)S(1)} %copy-done.5), channel_id=1, source_target_pairs={{0,16},{16,32},{32,48},{48,64},{64,80},{80,96},{96,112},{1,17},{17... | collective-permute-start | bytes 1572872 | tf_op jit(solution)/shard_map/ppermute | solution.py:23
  132.2 3.3 %collective-permute-start.9 = (bf16[32,32,256]{2,1,0:T(8,128)(2,1)S(1)}, bf16[32,32,256]{2,1,0:T(8,128)(2,1)S(1)}, u32[]{:S(2)}, u32[]{:S(2)}) collective-permute-start(bf16[32,32,256]{2,1,0:T(8,128)(2,1)S(1)} %add_convert_fusion.1), channel_id=1, source_target_pairs={{0,1},{1,2},{2,3},{3,4},{4,5},{5,6},{6,7},{7,8},{8,9},{9,10},{10,1... | collective-permute-start | bytes 1572872 | tf_op jit(solution)/shard_map/ppermute | solution.py:23
  135.5 2.6 %collective-permute-done.7 = bf16[32,32,256]{2,1,0:T(8,128)(2,1)S(1)} collective-permute-done((bf16[32,32,256]{2,1,0:T(8,128)(2,1)S(1)}, bf16[32,32,256]{2,1,0:T(8,128)(2,1)S(1)}, u32[]{:S(2)}, u32[]{:S(2)}) %collective-permute-start.7) | collective-permute-done | bytes 524320 | tf_op jit(solution)/shard_map/ppermute | solution.py:23
  138.1 18.9 %collective-permute-done.9 = bf16[32,32,256]{2,1,0:T(8,128)(2,1)S(1)} collective-permute-done((bf16[32,32,256]{2,1,0:T(8,128)(2,1)S(1)}, bf16[32,32,256]{2,1,0:T(8,128)(2,1)S(1)}, u32[]{:S(2)}, u32[]{:S(2)}) %collective-permute-start.9) | collective-permute-done | bytes 524320 | tf_op jit(solution)/shard_map/ppermute | solution.py:23
  158.4 2.7 %collective-permute-done.10 = bf16[9,256,256]{2,1,0:T(8,128)(2,1)S(1)} collective-permute-done((bf16[9,256,256]{2,1,0:T(8,128)(2,1)S(1)}, bf16[9,256,256]{2,1,0:T(8,128)(2,1)S(1)}, u32[]{:S(2)}, u32[]{:S(2)}) %collective-permute-start.10) | collective-permute-done | bytes 1179680 | tf_op jit(solution)/shard_map/ppermute | solution.py:393
  161.2 2.5 %maximum_convert_fusion = f32[2,3,3,256,256]{4,3,2,1,0:T(8,128)} fusion(bf16[1,3,3,256,256]{4,3,2,1,0:T(8,128)(2,1)S(1)} %bitcast.14, bf16[1,3,3,256,256]{4,3,2,1,0:T(8,128)(2,1)S(1)} %bitcast.13), kind=kLoop, calls=%fused_computation | loop fusion | flops 2359296 | bytes 7077888 | tf_op jit(solution)/shard_map/convert_element_type | solution.py:446
  (43 shorter events, 12.7 us)
Async XLA Ops:
  0.6 27.9 %collective-permute-start = (bf16[32,32,256]{2,1,0:T(8,128)(2,1)}, bf16[32,32,256]{2,1,0:T(8,128)(2,1)S(1)}, u32[]{:S(2)}, u32[]{:S(2)}) collective-permute-start(bf16[32,32,256]{2,1,0:T(8,128)(2,1)} %tl_ref.1), channel_id=1, source_target_pairs={{1,0},{2,1},{3,2},{4,3},{5,4},{6,5},{7,6},{8,7},{9,8},{10,9},{11,1... | collective-permute-start | bytes 1572872 | tf_op jit(solution)/shard_map/ppermute | solution.py:23
  1.9 32.1 %collective-permute-start.1 = (bf16[32,32,256]{2,1,0:T(8,128)(2,1)}, bf16[32,32,256]{2,1,0:T(8,128)(2,1)S(1)}, u32[]{:S(2)}, u32[]{:S(2)}) collective-permute-start(bf16[32,32,256]{2,1,0:T(8,128)(2,1)} %tl_ref.1), channel_id=1, source_target_pairs={{16,0},{32,16},{48,32},{64,48},{80,64},{96,80},{112,96},{17,1},{33... | collective-permute-start | bytes 1572872 | tf_op jit(solution)/shard_map/ppermute | solution.py:23
  6.5 14.4 %all-to-all-start = ((s32[16,1,1]{2,1,0:T(1,128)}), s32[16,1,1]{2,1,0:T(1,128)S(1)}, u32[]{:S(2)}, u32[]{:S(2)}) async-start(s32[16,1,1]{2,1,0:T(1,128)} %broadcast_in_dim.7), calls=%async_computation | async-start | bytes 16384 | tf_op jit(solution)/shard_map/all_to_all | solution.py:403
  20.9 0.6 copy-start.2
  24.2 8.2 %copy-start.3 = (s32[16,28]{1,0:T(8,128)S(1)}, s32[16,28]{1,0:T(8,128)}, u32[]{:S(2)}) copy-start(s32[16,28]{1,0:T(8,128)} %param.11) | copy-start | bytes 5380
  24.2 8.2 %copy-start.6 = (s32[16,2]{0,1:T(2,128)S(1)}, s32[16,2]{0,1:T(2,128)}, u32[]{:S(2)}) copy-start(s32[16,2]{0,1:T(2,128)} %param.10) | copy-start | bytes 388
  24.2 9.0 %copy-start.4 = (pred[16]{0:T(512)(128)(4,1)S(1)}, pred[16]{0:T(512)(128)(4,1)}, u32[]{:S(2)}) copy-start(pred[16]{0:T(512)(128)(4,1)} %constant.32.clone.1) | copy-start | bytes 52
  24.2 37.5 %all-to-all-start.1 = ((bf16[16,224,256]{2,1,0:T(8,128)(2,1)}), bf16[16,224,256]{2,1,0:T(8,128)(2,1)S(1)}, u32[]{:S(2)}, u32[]{:S(2)}) async-start(bf16[16,224,256]{2,1,0:T(8,128)(2,1)} %bitcast.17), calls=%async_computation.1 | async-start | bytes 3670016 | tf_op jit(solution)/shard_map/all_to_all | solution.py:410
  28.5 12.5 %collective-permute-start.2 = (bf16[32,32,256]{2,1,0:T(8,128)(2,1)S(1)}, bf16[32,32,256]{2,1,0:T(8,128)(2,1)S(1)}, u32[]{:S(2)}, u32[]{:S(2)}) collective-permute-start(bf16[32,32,256]{2,1,0:T(8,128)(2,1)S(1)} %collective-permute-done.tr_ref), channel_id=1, source_target_pairs={{16,0},{32,16},{48,32},{64,48},{80,64},{96,80},{112,96},{17,1},{33... | collective-permute-start | bytes 1572872 | tf_op jit(solution)/shard_map/ppermute | solution.py:23
  83.1 2.8 %collective-permute-start.3 = (bf16[9,256,256]{2,1,0:T(8,128)(2,1)S(1)}, bf16[9,256,256]{2,1,0:T(8,128)(2,1)S(1)}, u32[]{:S(2)}, u32[]{:S(2)}) collective-permute-start(bf16[9,256,256]{2,1,0:T(8,128)(2,1)S(1)} %get-tuple-element.26), channel_id=1, source_target_pairs={{0,16},{16,0},{32,48},{48,32},{64,80},{80,64},{96,112},{112,96},{1... | collective-permute-start | bytes 3538952 | tf_op jit(solution)/shard_map/ppermute | solution.py:393
  87.3 25.8 %all-to-all-start.2 = ((bf16[16,144,256]{2,1,0:T(8,128)(2,1)}), bf16[16,144,256]{2,1,0:T(8,128)(2,1)S(1)}, u32[]{:S(2)}, u32[]{:S(2)}) async-start(bf16[16,144,256]{2,1,0:T(8,128)(2,1)} %bitcast.6), calls=%async_computation.2 | async-start | bytes 2359296 | tf_op jit(solution)/shard_map/all_to_all | solution.py:430
  107.7 24.3 %collective-permute-start.8 = (bf16[32,32,256]{2,1,0:T(8,128)(2,1)}, bf16[32,32,256]{2,1,0:T(8,128)(2,1)S(1)}, u32[]{:S(2)}, u32[]{:S(2)}) collective-permute-start(bf16[32,32,256]{2,1,0:T(8,128)(2,1)} %get-tuple-element.31), channel_id=1, source_target_pairs={{0,16},{16,32},{32,48},{48,64},{64,80},{80,96},{96,112},{1,17},{17... | collective-permute-start | bytes 1572872 | tf_op jit(solution)/shard_map/ppermute | solution.py:23
  113.3 4.2 %collective-permute-start.6 = (bf16[144,256]{1,0:T(8,128)(2,1)S(1)}, bf16[144,256]{1,0:T(8,128)(2,1)S(1)}, u32[]{:S(2)}, u32[]{:S(2)}) collective-permute-start(bf16[144,256]{1,0:T(8,128)(2,1)S(1)} %reduce_sum.12), channel_id=1, source_target_pairs={{0,96},{16,112},{32,0},{48,16},{64,32},{80,48},{96,64},{112,80},{1... | collective-permute-start | bytes 221192 | tf_op jit(solution)/shard_map/ppermute | solution.py:438
  113.7 6.7 %collective-permute-start.5 = (bf16[144,256]{1,0:T(8,128)(2,1)S(1)}, bf16[144,256]{1,0:T(8,128)(2,1)S(1)}, u32[]{:S(2)}, u32[]{:S(2)}) collective-permute-start(bf16[144,256]{1,0:T(8,128)(2,1)S(1)} %reduce_sum.12), channel_id=1, source_target_pairs={{0,64},{16,80},{32,96},{48,112},{64,0},{80,16},{96,32},{112,48},{1... | collective-permute-start | bytes 221192 | tf_op jit(solution)/shard_map/ppermute | solution.py:438
  116.7 5.2 %collective-permute-start.4 = (bf16[144,256]{1,0:T(8,128)(2,1)S(1)}, bf16[144,256]{1,0:T(8,128)(2,1)S(1)}, u32[]{:S(2)}, u32[]{:S(2)}) collective-permute-start(bf16[144,256]{1,0:T(8,128)(2,1)S(1)} %reduce_sum.12), channel_id=1, source_target_pairs={{0,32},{16,48},{32,64},{48,80},{64,96},{80,112},{96,0},{112,16},{1... | collective-permute-start | bytes 221192 | tf_op jit(solution)/shard_map/ppermute | solution.py:438
  123.1 6.9 %copy-start.5 = (bf16[32,32,256]{2,1,0:T(8,128)(2,1)S(1)}, bf16[32,32,256]{2,1,0:T(8,128)(2,1)}, u32[]{:S(2)}) copy-start(bf16[32,32,256]{2,1,0:T(8,128)(2,1)} %get-tuple-element.29) | copy-start | bytes 1572868
  123.1 8.9 %copy-start.1 = (bf16[32,32,256]{2,1,0:T(8,128)(2,1)S(1)}, bf16[32,32,256]{2,1,0:T(8,128)(2,1)}, u32[]{:S(2)}) copy-start(bf16[32,32,256]{2,1,0:T(8,128)(2,1)} %get-tuple-element.30) | copy-start | bytes 1572868
  123.1 35.2 %all-to-all-start.3 = ((bf16[16,144,256]{2,1,0:T(8,128)(2,1)}), bf16[16,144,256]{2,1,0:T(8,128)(2,1)S(1)}, u32[]{:S(2)}, u32[]{:S(2)}) async-start(bf16[16,144,256]{2,1,0:T(8,128)(2,1)} %broadcast_in_dim.16), calls=%async_computation.3 | async-start | bytes 2359296 | tf_op jit(solution)/shard_map/all_to_all | solution.py:441
  129.9 27.1 %copy-start = (f32[32,32,256]{2,1,0:T(8,128)S(1)}, f32[32,32,256]{2,1,0:T(8,128)}, u32[]{:S(2)}) copy-start(f32[32,32,256]{2,1,0:T(8,128)} %get-tuple-element.28) | copy-start | bytes 3145732
  129.9 8.2 %collective-permute-start.7 = (bf16[32,32,256]{2,1,0:T(8,128)(2,1)S(1)}, bf16[32,32,256]{2,1,0:T(8,128)(2,1)S(1)}, u32[]{:S(2)}, u32[]{:S(2)}) collective-permute-start(bf16[32,32,256]{2,1,0:T(8,128)(2,1)S(1)} %copy-done.5), channel_id=1, source_target_pairs={{0,16},{16,32},{32,48},{48,64},{64,80},{80,96},{96,112},{1,17},{17... | collective-permute-start | bytes 1572872 | tf_op jit(solution)/shard_map/ppermute | solution.py:23
  132.2 24.8 %collective-permute-start.9 = (bf16[32,32,256]{2,1,0:T(8,128)(2,1)S(1)}, bf16[32,32,256]{2,1,0:T(8,128)(2,1)S(1)}, u32[]{:S(2)}, u32[]{:S(2)}) collective-permute-start(bf16[32,32,256]{2,1,0:T(8,128)(2,1)S(1)} %add_convert_fusion.1), channel_id=1, source_target_pairs={{0,1},{1,2},{2,3},{3,4},{4,5},{5,6},{6,7},{7,8},{8,9},{9,10},{10,1... | collective-permute-start | bytes 1572872 | tf_op jit(solution)/shard_map/ppermute | solution.py:23
  158.2 2.8 %collective-permute-start.10 = (bf16[9,256,256]{2,1,0:T(8,128)(2,1)S(1)}, bf16[9,256,256]{2,1,0:T(8,128)(2,1)S(1)}, u32[]{:S(2)}, u32[]{:S(2)}) collective-permute-start(bf16[9,256,256]{2,1,0:T(8,128)(2,1)S(1)} %bitcast.15), channel_id=1, source_target_pairs={{0,16},{16,0},{32,48},{48,32},{64,80},{80,64},{96,112},{112,96},{1... | collective-permute-start | bytes 3538952 | tf_op jit(solution)/shard_map/ppermute | solution.py:393

commit v8 on v7

--- a/solution.py
+++ b/solution.py
@@ -391,10 +391,6 @@
 
 def swap_cores(x):
     return lax.ppermute(x, "ha", [(i, i ^ 1) for i in range(lax.axis_size("ha"))])
-
-
-def pick_layer(index, first, second):
-    return jnp.where(index == 0, first, second)
 
 
 def local(features, counts, owner_perm, corners, offsets, kernels, cotangent):
@@ -442,8 +438,10 @@
     side = shifted((right.astype(F32) + corner.astype(F32)).astype(BF), "wa", 1)
     tile = tile + lower.astype(F32) + side.astype(F32)
     mine, tile = lax.optimization_barrier((mine, tile))
+    grads = jnp.zeros((2, *mine.shape), F32)
+    grads = lax.dynamic_update_slice(grads, mine.astype(F32)[None], (core, 0, 0, 0))
     other = swap_cores(mine)
-    grads = jnp.stack([pick_layer(core, mine, other), pick_layer(core, other, mine)]).astype(F32)
+    grads = lax.dynamic_update_slice(grads, other.astype(F32)[None], (1 - core, 0, 0, 0))
     return (tile, grads.reshape(2, 3, 3, C, C))
 
 

time: 166 us -> 164 us (0.988)
  the two profiles are of different devices: /device:TPU:1 before, /device:TPU:47 now
where the time goes in v8:
time: 164 us
  Pallas kernels  57.5 us (35%)
  starting transfers between devices  46.5 us (28%)
  waiting for transfers between devices  44.5 us (27%)
  local copies, waits for them, and re-layouts  8.62 us (5%)
  other arithmetic  4.96 us (3%)
    ppermute x6, waiting for transfers between devices, shifted(): lax.ppermute(value, axis, [(source, source + steps) for source in range(f...  31 us
    pallas_call x1, Pallas kernels, back(): pl.pallas_call(back_kernel, name='back', out_shape=[jax.ShapeDtypeStruct(...  21.3 us
    pallas_call x1, Pallas kernels, forward(): pl.pallas_call(forward_kernel, name='forward', out_shape=[jax.ShapeDtypeS...  20.7 us
    ppermute x6, starting transfers between devices, shifted(): lax.ppermute(value, axis, [(source, source + steps) for source in range(f...  18.3 us
    pallas_call x1, Pallas kernels, spread(): pl.pallas_call(spread_kernel, name='spread', out_shape=[piece(F32), piece...  12.8 us
    ppermute x3, waiting for transfers between devices, local(): lax.ppermute(part, 'ha', [(i, (i + hop) % count) for i in range(count)])  7.09 us
    all_to_all x1, starting transfers between devices, local(): mine = lax.all_to_all(whole, 'wa', 0, 0, tiled=True).reshape(9, C, C)  6.81 us
    all_to_all x1, starting transfers between devices, local(): parts = lax.all_to_all(mine.reshape(peers, -1, C), 'wa', 0, 0, tiled=True)  6.61 us
  transfers between devices with their start and end apart: 15, of which 7 were waited for; matrix products, arithmetic and copies ran while one was open for 6% of the time, Pallas kernels for 22%

profile of v8, /device:TPU:47, one launch (start us, length us, event | category | flops | bytes accessed | tf_op | source)
XLA Modules:
  0.0 163.5 jit_solution(12054522284155852099)
XLA Ops:
  0.6 2.5 %collective-permute-start = (bf16[32,32,256]{2,1,0:T(8,128)(2,1)}, bf16[32,32,256]{2,1,0:T(8,128)(2,1)S(1)}, u32[]{:S(2)}, u32[]{:S(2)}) collective-permute-start(bf16[32,32,256]{2,1,0:T(8,128)(2,1)} %tl_ref.1), channel_id=1, source_target_pairs={{1,0},{2,1},{3,2},{4,3},{5,4},{6,5},{7,6},{8,7},{9,8},{10,9},{11,1... | collective-permute-start | bytes 1572872 | tf_op jit(solution)/shard_map/ppermute | solution.py:23
  3.1 2.9 %collective-permute-start.1 = (bf16[32,32,256]{2,1,0:T(8,128)(2,1)}, bf16[32,32,256]{2,1,0:T(8,128)(2,1)S(1)}, u32[]{:S(2)}, u32[]{:S(2)}) collective-permute-start(bf16[32,32,256]{2,1,0:T(8,128)(2,1)} %tl_ref.1), channel_id=1, source_target_pairs={{16,0},{32,16},{48,32},{64,48},{80,64},{96,80},{112,96},{17,1},{33... | collective-permute-start | bytes 1572872 | tf_op jit(solution)/shard_map/ppermute | solution.py:23
  7.2 6.5 %all-to-all-start = ((s32[16,1,1]{2,1,0:T(1,128)}), s32[16,1,1]{2,1,0:T(1,128)S(1)}, u32[]{:S(2)}, u32[]{:S(2)}) async-start(s32[16,1,1]{2,1,0:T(1,128)} %broadcast_in_dim.30), calls=%async_computation | async-start | bytes 16384 | tf_op jit(solution)/shard_map/all_to_all | solution.py:399
  14.4 2.2 %copy.9.x_ref = bf16[8,14,14,256]{3,2,1,0:T(8,128)(2,1)} copy(bf16[8,14,14,256]{3,0,2,1:T(8,128)(2,1)} %param.13) | data formatting | bytes 1605632 | tf_op args[6]
  16.6 1.8 %all-to-all-done.count_ref = s32[16,1,1]{2,1,0:T(1,128)S(1)} async-done(((s32[16,1,1]{2,1,0:T(1,128)}), s32[16,1,1]{2,1,0:T(1,128)S(1)}, u32[]{:S(2)}, u32[]{:S(2)}) %all-to-all-start) | async-done | bytes 96 | tf_op jit(solution)/shard_map/all_to_all | solution.py:399
  19.1 2.7 %route.1 = (bf16[16,14,16,256]{3,2,1,0:T(8,128)(2,1)}, s32[17]{0:T(128)}) custom-call(s32[16,1,1]{2,1,0:T(1,128)} %copy-done.3, s32[1,16]{1,0:T(1,128)} %perm_ref.1, bf16[8,14,14,256]{3,2,1,0:T(8,128)(2,1)} %copy.9.x_ref), custom_call_target="tpu_custom_call" | custom-call | bytes 4194304 | tf_op jit(solution)/shard_map/route/pallas_call | solution.py:83
  21.8 5.9 %all-to-all-start.1 = ((bf16[16,224,256]{2,1,0:T(8,128)(2,1)}), bf16[16,224,256]{2,1,0:T(8,128)(2,1)S(1)}, u32[]{:S(2)}, u32[]{:S(2)}) async-start(bf16[16,224,256]{2,1,0:T(8,128)(2,1)} %bitcast.21), calls=%async_computation.1 | async-start | bytes 3670016 | tf_op jit(solution)/shard_map/all_to_all | solution.py:406
  27.7 4.1 %collective-permute-start.2 = (bf16[32,32,256]{2,1,0:T(8,128)(2,1)S(1)}, bf16[32,32,256]{2,1,0:T(8,128)(2,1)S(1)}, u32[]{:S(2)}, u32[]{:S(2)}) collective-permute-start(bf16[32,32,256]{2,1,0:T(8,128)(2,1)S(1)} %collective-permute-done.tr_ref), channel_id=1, source_target_pairs={{16,0},{32,16},{48,32},{64,48},{80,64},{96,80},{112,96},{17,1},{33... | collective-permute-start | bytes 1572872 | tf_op jit(solution)/shard_map/ppermute | solution.py:23
  33.4 7.0 %collective-permute-done.2.br_ref = bf16[32,32,256]{2,1,0:T(8,128)(2,1)S(1)} collective-permute-done((bf16[32,32,256]{2,1,0:T(8,128)(2,1)S(1)}, bf16[32,32,256]{2,1,0:T(8,128)(2,1)S(1)}, u32[]{:S(2)}, u32[]{:S(2)}) %collective-permute-start.2) | collective-permute-done | bytes 524320 | tf_op jit(solution)/shard_map/ppermute | solution.py:23
  40.4 20.7 %forward.1 = (bf16[256,4096]{1,0:T(8,128)(2,1)}, bf16[256,4096]{1,0:T(8,128)(2,1)}, bf16[16,224,256]{2,1,0:T(8,128)(2,1)}, bf16[16,224,256]{2,1,0:T(8,128)(2,1)}, bf16[18,256,256]{2,1,0:T(8,128)(2,1)}) custom-call(s32[32]{0:T(128)} %reshape.27.corner_ref, bf16[32,32,256]{2,1,0:T(8,128)(2,1)} %tl_ref.1, bf16[32,32,256]{2,1,0:T(8,128)(2,1)S(1)} %collective-permute-done.tr_ref, ...), custom_call_target="tpu_custom_call" | custom-call | flops 11299999744 | bytes 14680064 | tf_op jit(solution)/shard_map/forward/pallas_call | solution.py:155
  61.1 21.3 %back.1 = (bf16[16,224,256]{2,1,0:T(8,128)(2,1)}, bf16[9,256,256]{2,1,0:T(8,128)(2,1)S(1)}, bf16[9,256,256]{2,1,0:T(8,128)(2,1)S(1)}) custom-call(s32[17]{0:T(128)} %get-tuple-element.18.meta_ref, bf16[16,224,256]{2,1,0:T(8,128)(2,1)S(1)} %all-to-all-done.1.in_ref, bf16[16,224,256]{2,1,0:T(8,128)(2,1)} %get-tuple-element.20.first_ref.next_ref, ...), custom_call_target="tpu_custom_call" | custom-call | flops 14000000000 | bytes 16777216 | tf_op jit(solution)/shard_map/back/pallas_call | solution.py:277
  82.5 2.8 %collective-permute-done.3 = bf16[9,256,256]{2,1,0:T(8,128)(2,1)S(1)} collective-permute-done((bf16[9,256,256]{2,1,0:T(8,128)(2,1)S(1)}, bf16[9,256,256]{2,1,0:T(8,128)(2,1)S(1)}, u32[]{:S(2)}, u32[]{:S(2)}) %collective-permute-start.3) | collective-permute-done | bytes 1179680 | tf_op jit(solution)/shard_map/ppermute | solution.py:393
  86.7 6.6 %all-to-all-start.2 = ((bf16[16,144,256]{2,1,0:T(8,128)(2,1)}), bf16[16,144,256]{2,1,0:T(8,128)(2,1)S(1)}, u32[]{:S(2)}, u32[]{:S(2)}) async-start(bf16[16,144,256]{2,1,0:T(8,128)(2,1)} %bitcast.6), calls=%async_computation.2 | async-start | bytes 2359296 | tf_op jit(solution)/shard_map/all_to_all | solution.py:426
  94.0 12.8 %spread.1 = (f32[32,32,256]{2,1,0:T(8,128)}, bf16[32,32,256]{2,1,0:T(8,128)(2,1)}, bf16[32,32,256]{2,1,0:T(8,128)(2,1)}, bf16[32,32,256]{2,1,0:T(8,128)(2,1)}) custom-call(s32[32]{0:T(128)} %reshape.27.corner_ref, bf16[16,224,256]{2,1,0:T(8,128)(2,1)} %get-tuple-element.27.p_ref, f32[16,32]{1,0:T(8,128)} %select_maximum_fusion.off_ref, ...), custom_call_target="tpu_custom_call" | custom-call | flops 7000000000 | bytes 6291456 | tf_op jit(solution)/shard_map/spread/pallas_call | solution.py:366
  106.7 3.9 %collective-permute-start.8 = (bf16[32,32,256]{2,1,0:T(8,128)(2,1)}, bf16[32,32,256]{2,1,0:T(8,128)(2,1)S(1)}, u32[]{:S(2)}, u32[]{:S(2)}) collective-permute-start(bf16[32,32,256]{2,1,0:T(8,128)(2,1)} %get-tuple-element.31), channel_id=1, source_target_pairs={{0,16},{16,32},{32,48},{48,64},{64,80},{80,96},{96,112},{1,17},{17... | collective-permute-start | bytes 1572872 | tf_op jit(solution)/shard_map/ppermute | solution.py:23
  110.9 1.9 %collective-permute-start.5 = (bf16[144,256]{1,0:T(8,128)(2,1)S(1)}, bf16[144,256]{1,0:T(8,128)(2,1)S(1)}, u32[]{:S(2)}, u32[]{:S(2)}) collective-permute-start(bf16[144,256]{1,0:T(8,128)(2,1)S(1)} %reduce_sum.12), channel_id=1, source_target_pairs={{0,64},{16,80},{32,96},{48,112},{64,0},{80,16},{96,32},{112,48},{1... | collective-permute-start | bytes 221192 | tf_op jit(solution)/shard_map/ppermute | solution.py:434
  112.7 7.1 %collective-permute-done.4 = bf16[144,256]{1,0:T(8,128)(2,1)S(1)} collective-permute-done((bf16[144,256]{1,0:T(8,128)(2,1)S(1)}, bf16[144,256]{1,0:T(8,128)(2,1)S(1)}, u32[]{:S(2)}, u32[]{:S(2)}) %collective-permute-start.4) | collective-permute-done | bytes 73760 | tf_op jit(solution)/shard_map/ppermute | solution.py:434
  121.0 6.8 %all-to-all-start.3 = ((bf16[16,144,256]{2,1,0:T(8,128)(2,1)}), bf16[16,144,256]{2,1,0:T(8,128)(2,1)S(1)}, u32[]{:S(2)}, u32[]{:S(2)}) async-start(bf16[16,144,256]{2,1,0:T(8,128)(2,1)} %broadcast_in_dim.31), calls=%async_computation.3 | async-start | bytes 2359296 | tf_op jit(solution)/shard_map/all_to_all | solution.py:437
  127.8 2.0 %collective-permute-start.7 = (bf16[32,32,256]{2,1,0:T(8,128)(2,1)}, bf16[32,32,256]{2,1,0:T(8,128)(2,1)S(1)}, u32[]{:S(2)}, u32[]{:S(2)}) collective-permute-start(bf16[32,32,256]{2,1,0:T(8,128)(2,1)} %get-tuple-element.29), channel_id=1, source_target_pairs={{0,16},{16,32},{32,48},{48,64},{64,80},{80,96},{96,112},{1,17},{17... | collective-permute-start | bytes 1572872 | tf_op jit(solution)/shard_map/ppermute | solution.py:23
  129.9 3.1 %collective-permute-start.9 = (bf16[32,32,256]{2,1,0:T(8,128)(2,1)S(1)}, bf16[32,32,256]{2,1,0:T(8,128)(2,1)S(1)}, u32[]{:S(2)}, u32[]{:S(2)}) collective-permute-start(bf16[32,32,256]{2,1,0:T(8,128)(2,1)S(1)} %add_convert_fusion.1), channel_id=1, source_target_pairs={{0,1},{1,2},{2,3},{3,4},{4,5},{5,6},{6,7},{7,8},{8,9},{9,10},{10,1... | collective-permute-start | bytes 1572872 | tf_op jit(solution)/shard_map/ppermute | solution.py:23
  133.0 3.1 %collective-permute-done.7 = bf16[32,32,256]{2,1,0:T(8,128)(2,1)S(1)} collective-permute-done((bf16[32,32,256]{2,1,0:T(8,128)(2,1)}, bf16[32,32,256]{2,1,0:T(8,128)(2,1)S(1)}, u32[]{:S(2)}, u32[]{:S(2)}) %collective-permute-start.7) | collective-permute-done | bytes 524320 | tf_op jit(solution)/shard_map/ppermute | solution.py:23
  136.2 20.9 %collective-permute-done.9 = bf16[32,32,256]{2,1,0:T(8,128)(2,1)S(1)} collective-permute-done((bf16[32,32,256]{2,1,0:T(8,128)(2,1)S(1)}, bf16[32,32,256]{2,1,0:T(8,128)(2,1)S(1)}, u32[]{:S(2)}, u32[]{:S(2)}) %collective-permute-start.9) | collective-permute-done | bytes 524320 | tf_op jit(solution)/shard_map/ppermute | solution.py:23
  159.3 1.8 %collective-permute-done.10 = bf16[9,256,256]{2,1,0:T(8,128)(2,1)S(1)} collective-permute-done((bf16[9,256,256]{2,1,0:T(8,128)(2,1)S(1)}, bf16[9,256,256]{2,1,0:T(8,128)(2,1)S(1)}, u32[]{:S(2)}, u32[]{:S(2)}) %collective-permute-start.10) | collective-permute-done | bytes 1179680 | tf_op jit(solution)/shard_map/ppermute | solution.py:393
  161.3 2.2 %copy-done = f32[2,9,256,256]{3,2,1,0:T(8,128)} copy-done((f32[2,9,256,256]{3,2,1,0:T(8,128)}, f32[2,9,256,256]{3,2,1,0:T(8,128)S(1)}, u32[]{:S(2)}) %copy-start) | copy-done | bytes 4718616
  (44 shorter events, 9.7 us)
Async XLA Ops:
  0.6 27.0 %collective-permute-start = (bf16[32,32,256]{2,1,0:T(8,128)(2,1)}, bf16[32,32,256]{2,1,0:T(8,128)(2,1)S(1)}, u32[]{:S(2)}, u32[]{:S(2)}) collective-permute-start(bf16[32,32,256]{2,1,0:T(8,128)(2,1)} %tl_ref.1), channel_id=1, source_target_pairs={{1,0},{2,1},{3,2},{4,3},{5,4},{6,5},{7,6},{8,7},{9,8},{10,9},{11,1... | collective-permute-start | bytes 1572872 | tf_op jit(solution)/shard_map/ppermute | solution.py:23
  3.1 30.3 %collective-permute-start.1 = (bf16[32,32,256]{2,1,0:T(8,128)(2,1)}, bf16[32,32,256]{2,1,0:T(8,128)(2,1)S(1)}, u32[]{:S(2)}, u32[]{:S(2)}) collective-permute-start(bf16[32,32,256]{2,1,0:T(8,128)(2,1)} %tl_ref.1), channel_id=1, source_target_pairs={{16,0},{32,16},{48,32},{64,48},{80,64},{96,80},{112,96},{17,1},{33... | collective-permute-start | bytes 1572872 | tf_op jit(solution)/shard_map/ppermute | solution.py:23
  7.2 11.2 %all-to-all-start = ((s32[16,1,1]{2,1,0:T(1,128)}), s32[16,1,1]{2,1,0:T(1,128)S(1)}, u32[]{:S(2)}, u32[]{:S(2)}) async-start(s32[16,1,1]{2,1,0:T(1,128)} %broadcast_in_dim.30), calls=%async_computation | async-start | bytes 16384 | tf_op jit(solution)/shard_map/all_to_all | solution.py:399
  18.5 0.6 copy-start.3
  21.7 10.0 %copy-start.4 = (s32[16,28]{1,0:T(8,128)S(1)}, s32[16,28]{1,0:T(8,128)}, u32[]{:S(2)}) copy-start(s32[16,28]{1,0:T(8,128)} %param.11) | copy-start | bytes 5380
  21.7 10.3 %copy-start.5 = (pred[16]{0:T(512)(128)(4,1)S(1)}, pred[16]{0:T(512)(128)(4,1)}, u32[]{:S(2)}) copy-start(pred[16]{0:T(512)(128)(4,1)} %constant.35.clone.1) | copy-start | bytes 52
  21.8 11.0 %copy-start.6 = (s32[16,2]{0,1:T(2,128)S(1)}, s32[16,2]{0,1:T(2,128)}, u32[]{:S(2)}) copy-start(s32[16,2]{0,1:T(2,128)} %param.10) | copy-start | bytes 388
  21.8 39.4 %all-to-all-start.1 = ((bf16[16,224,256]{2,1,0:T(8,128)(2,1)}), bf16[16,224,256]{2,1,0:T(8,128)(2,1)S(1)}, u32[]{:S(2)}, u32[]{:S(2)}) async-start(bf16[16,224,256]{2,1,0:T(8,128)(2,1)} %bitcast.21), calls=%async_computation.1 | async-start | bytes 3670016 | tf_op jit(solution)/shard_map/all_to_all | solution.py:406
  27.7 12.8 %collective-permute-start.2 = (bf16[32,32,256]{2,1,0:T(8,128)(2,1)S(1)}, bf16[32,32,256]{2,1,0:T(8,128)(2,1)S(1)}, u32[]{:S(2)}, u32[]{:S(2)}) collective-permute-start(bf16[32,32,256]{2,1,0:T(8,128)(2,1)S(1)} %collective-permute-done.tr_ref), channel_id=1, source_target_pairs={{16,0},{32,16},{48,32},{64,48},{80,64},{96,80},{112,96},{17,1},{33... | collective-permute-start | bytes 1572872 | tf_op jit(solution)/shard_map/ppermute | solution.py:23
  82.5 2.8 %collective-permute-start.3 = (bf16[9,256,256]{2,1,0:T(8,128)(2,1)S(1)}, bf16[9,256,256]{2,1,0:T(8,128)(2,1)S(1)}, u32[]{:S(2)}, u32[]{:S(2)}) collective-permute-start(bf16[9,256,256]{2,1,0:T(8,128)(2,1)S(1)} %get-tuple-element.26), channel_id=1, source_target_pairs={{0,16},{16,0},{32,48},{48,32},{64,80},{80,64},{96,112},{112,96},{1... | collective-permute-start | bytes 3538952 | tf_op jit(solution)/shard_map/ppermute | solution.py:393
  86.7 23.9 %all-to-all-start.2 = ((bf16[16,144,256]{2,1,0:T(8,128)(2,1)}), bf16[16,144,256]{2,1,0:T(8,128)(2,1)S(1)}, u32[]{:S(2)}, u32[]{:S(2)}) async-start(bf16[16,144,256]{2,1,0:T(8,128)(2,1)} %bitcast.6), calls=%async_computation.2 | async-start | bytes 2359296 | tf_op jit(solution)/shard_map/all_to_all | solution.py:426
  106.7 23.0 %collective-permute-start.8 = (bf16[32,32,256]{2,1,0:T(8,128)(2,1)}, bf16[32,32,256]{2,1,0:T(8,128)(2,1)S(1)}, u32[]{:S(2)}, u32[]{:S(2)}) collective-permute-start(bf16[32,32,256]{2,1,0:T(8,128)(2,1)} %get-tuple-element.31), channel_id=1, source_target_pairs={{0,16},{16,32},{32,48},{48,64},{64,80},{80,96},{96,112},{1,17},{17... | collective-permute-start | bytes 1572872 | tf_op jit(solution)/shard_map/ppermute | solution.py:23
  110.8 9.0 %collective-permute-start.4 = (bf16[144,256]{1,0:T(8,128)(2,1)S(1)}, bf16[144,256]{1,0:T(8,128)(2,1)S(1)}, u32[]{:S(2)}, u32[]{:S(2)}) collective-permute-start(bf16[144,256]{1,0:T(8,128)(2,1)S(1)} %reduce_sum.12), channel_id=1, source_target_pairs={{0,32},{16,48},{32,64},{48,80},{64,96},{80,112},{96,0},{112,16},{1... | collective-permute-start | bytes 221192 | tf_op jit(solution)/shard_map/ppermute | solution.py:434
  110.9 9.0 %collective-permute-start.5 = (bf16[144,256]{1,0:T(8,128)(2,1)S(1)}, bf16[144,256]{1,0:T(8,128)(2,1)S(1)}, u32[]{:S(2)}, u32[]{:S(2)}) collective-permute-start(bf16[144,256]{1,0:T(8,128)(2,1)S(1)} %reduce_sum.12), channel_id=1, source_target_pairs={{0,64},{16,80},{32,96},{48,112},{64,0},{80,16},{96,32},{112,48},{1... | collective-permute-start | bytes 221192 | tf_op jit(solution)/shard_map/ppermute | solution.py:434
  112.7 7.1 %collective-permute-start.6 = (bf16[144,256]{1,0:T(8,128)(2,1)S(1)}, bf16[144,256]{1,0:T(8,128)(2,1)S(1)}, u32[]{:S(2)}, u32[]{:S(2)}) collective-permute-start(bf16[144,256]{1,0:T(8,128)(2,1)S(1)} %reduce_sum.12), channel_id=1, source_target_pairs={{0,96},{16,112},{32,0},{48,16},{64,32},{80,48},{96,64},{112,80},{1... | collective-permute-start | bytes 221192 | tf_op jit(solution)/shard_map/ppermute | solution.py:434
  119.9 9.9 %copy-start.2 = (bf16[32,32,256]{2,1,0:T(8,128)(2,1)S(1)}, bf16[32,32,256]{2,1,0:T(8,128)(2,1)}, u32[]{:S(2)}) copy-start(bf16[32,32,256]{2,1,0:T(8,128)(2,1)} %get-tuple-element.30) | copy-start | bytes 1572868
  121.0 36.1 %copy-start.1 = (f32[32,32,256]{2,1,0:T(8,128)S(1)}, f32[32,32,256]{2,1,0:T(8,128)}, u32[]{:S(2)}) copy-start(f32[32,32,256]{2,1,0:T(8,128)} %get-tuple-element.28) | copy-start | bytes 3145732
  121.0 37.3 %all-to-all-start.3 = ((bf16[16,144,256]{2,1,0:T(8,128)(2,1)}), bf16[16,144,256]{2,1,0:T(8,128)(2,1)S(1)}, u32[]{:S(2)}, u32[]{:S(2)}) async-start(bf16[16,144,256]{2,1,0:T(8,128)(2,1)} %broadcast_in_dim.31), calls=%async_computation.3 | async-start | bytes 2359296 | tf_op jit(solution)/shard_map/all_to_all | solution.py:437
  127.8 8.4 %collective-permute-start.7 = (bf16[32,32,256]{2,1,0:T(8,128)(2,1)}, bf16[32,32,256]{2,1,0:T(8,128)(2,1)S(1)}, u32[]{:S(2)}, u32[]{:S(2)}) collective-permute-start(bf16[32,32,256]{2,1,0:T(8,128)(2,1)} %get-tuple-element.29), channel_id=1, source_target_pairs={{0,16},{16,32},{32,48},{48,64},{64,80},{80,96},{96,112},{1,17},{17... | collective-permute-start | bytes 1572872 | tf_op jit(solution)/shard_map/ppermute | solution.py:23
  129.9 27.1 %collective-permute-start.9 = (bf16[32,32,256]{2,1,0:T(8,128)(2,1)S(1)}, bf16[32,32,256]{2,1,0:T(8,128)(2,1)S(1)}, u32[]{:S(2)}, u32[]{:S(2)}) collective-permute-start(bf16[32,32,256]{2,1,0:T(8,128)(2,1)S(1)} %add_convert_fusion.1), channel_id=1, source_target_pairs={{0,1},{1,2},{2,3},{3,4},{4,5},{5,6},{6,7},{7,8},{8,9},{9,10},{10,1... | collective-permute-start | bytes 1572872 | tf_op jit(solution)/shard_map/ppermute | solution.py:23
  158.2 2.9 %collective-permute-start.10 = (bf16[9,256,256]{2,1,0:T(8,128)(2,1)S(1)}, bf16[9,256,256]{2,1,0:T(8,128)(2,1)S(1)}, u32[]{:S(2)}, u32[]{:S(2)}) collective-permute-start(bf16[9,256,256]{2,1,0:T(8,128)(2,1)S(1)} %bitcast.19), channel_id=1, source_target_pairs={{0,16},{16,0},{32,48},{48,32},{64,80},{80,64},{96,112},{112,96},{1... | collective-permute-start | bytes 3538952 | tf_op jit(solution)/shard_map/ppermute | solution.py:393
  161.3 2.2 %copy-start = (f32[2,9,256,256]{3,2,1,0:T(8,128)}, f32[2,9,256,256]{3,2,1,0:T(8,128)S(1)}, u32[]{:S(2)}) copy-start(f32[2,9,256,256]{3,2,1,0:T(8,128)S(1)} %convert_dynamic-update-slice_fusion) | copy-start | bytes 14155780
